TPU v7x, 32 devices: a whole 2x2x4 slice. The times are simulated.
32 devices in a mesh: energy: 8 (over y, x, core), elem: 4 (over z).
Axes of the slice: x: 2, y: 2, z: 4, core: 2. Of those that a mesh axis runs over, the one named last changes fastest.
Arguments:
- g_lesser: bfloat16 [2, 512, 2048], P(None, 'energy', 'elem'), may hold values from -6 to 6
- g_greater: bfloat16 [2, 512, 2048], P(None, 'energy', 'elem'), may hold values from -6 to 6
- send_rows: int32 [4, 8, 4, 32], P('elem'), may hold values from 0 to 63, as said below
- partner_slot: int32 [2048], P('elem'), may hold values from 0 to 127, as said below
Outputs:
- polarization_lesser: bfloat16 [2, 512, 2048], P(None, 'energy', 'elem')
- polarization_greater: bfloat16 [2, 512, 2048], P(None, 'energy', 'elem')
Inputs may be any that keep to these rules, and one draw needn't show every extreme that they name: partner is an involution on the elements that keeps the element piece n. The groups fall into two halves of 2 groups; for a sending group b and element piece n, send_rows[b, n, a, :] lists 32 distinct rows when a lies in b's half (b itself included) and zeros otherwise; every row of that piece of the sender appears exactly once over all receivers of its half. `partner_slot`: every slot named points into a receiving group's half and to a slot that carries a row; the 64 elements of one element piece of a group name 64 distinct slots.
All inputs are finite; a program needn't handle non-finite values.
Results may differ from a plain program's by a relative error of at most 0.001.
Values may be sent and summed in bfloat16 or wider, within the bound.
No kernel may reach another device: no remote copies, remote signals or barrier semaphores. Data moves between devices by JAX's collectives and lax.ppermute only.
A program may use at most 64 MiB of HBM per device.

v0:
```python
from functools import partial
import math

import jax
import jax.numpy as jnp
from jax import lax
from jax.sharding import PartitionSpec as P


def factor_pair(length):
    divisor = math.isqrt(length)
    while length % divisor:
        divisor -= 1
    return divisor


def phase_tables(rows_count, cols_count, modulus, inverse):
    sign_factor = 1.0 if inverse else -1.0
    left_index = jnp.arange(rows_count, dtype=jnp.int32)
    right_index = jnp.arange(cols_count, dtype=jnp.int32)
    phases = (left_index[:, None] * right_index[None, :] % modulus).astype(jnp.float32) * (
        2.0 * math.pi / modulus
    )
    return (jnp.cos(phases), sign_factor * jnp.sin(phases))


def transform(real_part, imag_part, inverse):
    signals, length, width = real_part.shape
    first_size = factor_pair(length)
    second_size = length // first_size
    cos_first, sin_first = phase_tables(first_size, first_size, first_size, inverse)
    cos_twist, sin_twist = phase_tables(first_size, second_size, length, inverse)
    cos_second, sin_second = phase_tables(second_size, second_size, second_size, inverse)
    product = partial(jnp.einsum, precision=lax.Precision.HIGHEST)
    real_grid = real_part.reshape(signals, first_size, second_size, width)
    imag_grid = imag_part.reshape(signals, first_size, second_size, width)
    inner_re = product("ka,sabe->skbe", cos_first, real_grid) - product(
        "ka,sabe->skbe", sin_first, imag_grid
    )
    inner_im = product("ka,sabe->skbe", cos_first, imag_grid) + product(
        "ka,sabe->skbe", sin_first, real_grid
    )
    twist_cos = cos_twist[None, :, :, None]
    twist_sin = sin_twist[None, :, :, None]
    twist_re = inner_re * twist_cos - inner_im * twist_sin
    twist_im = inner_re * twist_sin + inner_im * twist_cos
    outer_re = product("qb,skbe->sqke", cos_second, twist_re) - product(
        "qb,skbe->sqke", sin_second, twist_im
    )
    outer_im = product("qb,skbe->sqke", cos_second, twist_im) + product(
        "qb,skbe->sqke", sin_second, twist_re
    )
    return (outer_re.reshape(signals, length, width), outer_im.reshape(signals, length, width))


def reverse_energy(values):
    return jnp.roll(jnp.flip(values, axis=1), 1, axis=1)


def shards(g_lesser, g_greater, send_rows, partner_slot):
    piece_index = lax.axis_index("energy")
    energy_count = lax.axis_size("energy")
    group_rows = partner_slot.shape[0]
    elem_dev = group_rows // energy_count
    own_lesser, own_greater = (
        lax.all_to_all(g_lesser, "energy", split_axis=2, concat_axis=1, tiled=True),
        lax.all_to_all(g_greater, "energy", split_axis=2, concat_axis=1, tiled=True),
    )
    own_rows = jnp.stack([own_lesser, own_greater])
    partner_columns = lax.dynamic_slice_in_dim(partner_slot, piece_index * elem_dev, elem_dev, 0)
    chosen_rows = lax.dynamic_index_in_dim(send_rows[0], piece_index, 0, keepdims=False).reshape(-1)
    outgoing = jnp.take(own_rows, chosen_rows, axis=3)
    incoming = lax.all_to_all(outgoing, "elem", split_axis=3, concat_axis=3, tiled=True)
    partner_rows = jnp.take(incoming, partner_columns, axis=3)
    signals = jnp.concatenate([own_rows, partner_rows], 0).astype(jnp.float32)
    spec_re, spec_im = transform(signals[:, 0], signals[:, 1], False)
    near_re = spec_re[:2]
    near_im = spec_im[:2]
    far_re = reverse_energy(jnp.stack([spec_re[3], spec_re[2]]))
    far_im = reverse_energy(jnp.stack([spec_im[3], spec_im[2]]))
    prod_re = near_re * far_re - near_im * far_im
    prod_im = near_re * far_im + near_im * far_re
    back_re, back_im = transform(prod_re, prod_im, True)
    length = back_re.shape[1]
    factor = 1.0 / (length * math.sqrt(length))
    result = jnp.stack([factor * back_im, -factor * back_re], 1).astype(jnp.bfloat16)
    lesser_out, greater_out = (
        lax.all_to_all(result[0], "energy", split_axis=1, concat_axis=2, tiled=True),
        lax.all_to_all(result[1], "energy", split_axis=1, concat_axis=2, tiled=True),
    )
    return (lesser_out, greater_out)


def solution(mesh):
    in_specs = (
        P(None, "energy", "elem"),
        P(None, "energy", "elem"),
        P("elem", None, None, None),
        P("elem"),
    )
    out_specs = (P(None, "energy", "elem"), P(None, "energy", "elem"))
    return jax.shard_map(shards, mesh=mesh, in_specs=in_specs, out_specs=out_specs, check_vma=False)
```

profile of v0, /device:TPU:0, one launch (start us, length us, event | category | flops | bytes accessed | tf_op | source)
XLA Modules:
  0.0 93.1 jit_solution(4972418240594326676)
XLA Ops:
  0.6 1.1 %copy.86 = bf16[2,64,512]{1,0,2:T(2,128)(2,1)S(1)} copy(bf16[2,64,512]{2,1,0:T(8,128)(2,1)} %param.4) | data formatting | bytes 262144 | tf_op args[0]
  1.7 0.9 reshape.175
  2.6 5.3 %all-to-all-start = ((bf16[8,2,4096]{2,1,0:T(2,128)(2,1)}), bf16[8,2,4096]{2,1,0:T(2,128)(2,1)S(1)}, u32[]{:S(2)}, u32[]{:S(2)}) async-start(bf16[8,2,4096]{2,1,0:T(2,128)(2,1)} %reshape.175), calls=%async_computation | async-start | bytes 262144 | tf_op jit(solution)/shard_map/all_to_all | solution.py:66
  8.3 0.9 reshape.173
  9.2 4.3 %all-to-all-done = bf16[8,2,4096]{2,1,0:T(2,128)(2,1)S(1)} async-done(((bf16[8,2,4096]{2,1,0:T(2,128)(2,1)}), bf16[8,2,4096]{2,1,0:T(2,128)(2,1)S(1)}, u32[]{:S(2)}, u32[]{:S(2)}) %all-to-all-start) | async-done | bytes 131104 | tf_op jit(solution)/shard_map/all_to_all | solution.py:66
  13.5 3.4 %all-to-all-start.1 = ((bf16[8,2,4096]{2,1,0:T(2,128)(2,1)}), bf16[8,2,4096]{2,1,0:T(2,128)(2,1)S(1)}, u32[]{:S(2)}, u32[]{:S(2)}) async-start(bf16[8,2,4096]{2,1,0:T(2,128)(2,1)} %reshape.173), calls=%async_computation.1 | async-start | bytes 262144 | tf_op jit(solution)/shard_map/all_to_all | solution.py:67
  17.6 4.7 %all-to-all-done.1 = bf16[8,2,4096]{2,1,0:T(2,128)(2,1)S(1)} async-done(((bf16[8,2,4096]{2,1,0:T(2,128)(2,1)}), bf16[8,2,4096]{2,1,0:T(2,128)(2,1)S(1)}, u32[]{:S(2)}, u32[]{:S(2)}) %all-to-all-start.1) | async-done | bytes 131104 | tf_op jit(solution)/shard_map/all_to_all | solution.py:67
  23.4 1.7 %gather_fusion = bf16[128,2,2,512]{3,2,1,0:T(2,128)(2,1)S(1)} fusion(bf16[2,2,512,64]{2,1,3,0:T(2,128)(2,1)S(1)} %pad_maximum_fusion.4, s32[1024]{0:T(1024)S(1)} %pad_clamp_fusion.1), kind=kCustom, calls=%fused_computation | custom fusion | bytes 1049088 | tf_op jit(solution)/shard_map/jit(_take)/gather | solution.py:72
  25.1 1.4 %fusion.22 = bf16[2,2,512,128]{2,1,0,3:T(2,128)(2,1)} fusion(bf16[128,2,2,512]{3,2,1,0:T(2,128)(2,1)S(1)} %gather_fusion, pred[128]{0:T(512)(128)(4,1)S(1)} %compare_and_fusion), kind=kLoop, calls=%fused_computation.49 | loop fusion | flops 262144 | bytes 1048704 | tf_op jit(solution)/shard_map/jit(_take)/select_n | solution.py:72
  26.5 4.9 %all-to-all-start.2 = ((bf16[2,2,512,128]{2,1,0,3:T(2,128)(2,1)}), bf16[2,2,512,128]{2,1,0,3:T(2,128)(2,1)S(1)}, u32[]{:S(2)}, u32[]{:S(2)}) async-start(bf16[2,2,512,128]{2,1,0,3:T(2,128)(2,1)} %fusion.22), calls=%async_computation.2 | async-start | bytes 1048576 | tf_op jit(solution)/shard_map/all_to_all | solution.py:73
  32.6 13.1 %all-to-all-done.2 = bf16[2,2,512,128]{2,1,0,3:T(2,128)(2,1)S(1)} async-done(((bf16[2,2,512,128]{2,1,0,3:T(2,128)(2,1)}), bf16[2,2,512,128]{2,1,0,3:T(2,128)(2,1)S(1)}, u32[]{:S(2)}, u32[]{:S(2)}) %all-to-all-start.2) | async-done | bytes 524320 | tf_op jit(solution)/shard_map/all_to_all | solution.py:73
  46.0 1.1 %gather_fusion.1 = bf16[64,2,2,512]{3,2,1,0:T(2,128)(2,1)S(1)} fusion(bf16[2,2,512,128]{2,1,3,0:T(2,128)(2,1)S(1)} %copy.92, s32[1024]{0:T(1024)S(1)} %pad_clamp_fusion), kind=kCustom, calls=%fused_computation.1 | custom fusion | bytes 524544 | tf_op jit(solution)/shard_map/jit(_take)/gather | solution.py:74
  53.0 1.4 %fusion.12 = f32[4,16,64,32]{2,3,1,0:T(8,128)S(1)} fusion(f32[4,16,32,64]{3,1,2,0:T(8,128)S(1)} %get-tuple-element.4), kind=kOutput, calls=%fused_computation.25 | convolution fusion | flops 50345984 | bytes 1048576 | tf_op jit(solution)/shard_map/qb,skbe->sqke/dot_general | solution.py:50
  54.4 1.4 %fusion.16 = f32[4,16,64,32]{2,3,1,0:T(8,128)S(1)} fusion(f32[4,16,32,64]{3,1,2,0:T(8,128)S(1)} %get-tuple-element.5), kind=kOutput, calls=%fused_computation.29 | convolution fusion | flops 50345984 | bytes 1048576 | tf_op jit(solution)/shard_map/qb,skbe->sqke/dot_general | solution.py:47
  55.8 1.4 %fusion.1 = f32[4,32,16,64]{3,1,2,0:T(8,128)S(1)} fusion(f32[4,16,64,32]{2,3,1,0:T(8,128)S(1)} %fusion.16, f32[4,16,32,64]{3,1,2,0:T(8,128)S(1)} %get-tuple-element.4), kind=kOutput, calls=%fused_computation.5 | convolution fusion | flops 50478080 | bytes 1572864 | tf_op jit(solution)/shard_map/qb,skbe->sqke/dot_general | solution.py:47
  57.2 1.0 %copy-done.1 = f32[4,32,16,64]{3,1,2,0:T(8,128)} copy-done((f32[4,32,16,64]{3,1,2,0:T(8,128)}, f32[4,32,16,64]{3,1,2,0:T(8,128)S(1)}, u32[]{:S(2)}) %copy-start.1) | copy-done | bytes 524312
  58.2 1.4 %fusion = f32[4,32,16,64]{3,1,2,0:T(8,128)S(1)} fusion(f32[4,16,64,32]{2,3,1,0:T(8,128)S(1)} %fusion.12, f32[4,16,32,64]{3,1,2,0:T(8,128)S(1)} %get-tuple-element.5), kind=kOutput, calls=%fused_computation.3 | convolution fusion | flops 50478080 | bytes 1572864 | tf_op jit(solution)/shard_map/qb,skbe->sqke/dot_general | solution.py:50
  59.6 1.0 %copy-done.2 = f32[4,32,16,64]{3,1,2,0:T(8,128)} copy-done((f32[4,32,16,64]{3,1,2,0:T(8,128)}, f32[4,32,16,64]{3,1,2,0:T(8,128)S(1)}, u32[]{:S(2)}) %copy-start.2) | copy-done | bytes 524312
  67.5 0.9 fusion.7
  68.4 1.1 %multiply_subtract_fusion.1 = (f32[2,16,32,64]{3,1,2,0:T(8,128)S(1)}, f32[2,16,32,64]{3,1,2,0:T(8,128)S(1)}) fusion(f32[2,16,32,64]{3,1,2,0:T(8,128)S(1)} %fusion.7, f32[16,32]{0,1:T(8,128)S(1)} %get-tuple-element.19, f32[16,32]{0,1:T(8,128)S(1)} %fusion.90, f32[2,32,64,16]{2,3,1,0:T(8,128)S(1)} %fusion.29, f32[2,16,32,64]{3,2,1,0:T(8,128)S(1)} %get-tuple-element.6), kind=kOutput, calls=%fused_computation.47 | convolution fusion | flops 13045248 | bytes 1314816 | tf_op jit(solution)/shard_map/ka,sabe->skbe/dot_general | solution.py:40
  74.1 3.4 %all-to-all-start.4 = ((bf16[8,2,4096]{2,1,0:T(2,128)(2,1)}), bf16[8,2,4096]{2,1,0:T(2,128)(2,1)S(1)}, u32[]{:S(2)}, u32[]{:S(2)}) async-start(bf16[8,2,4096]{2,1,0:T(2,128)(2,1)} %reshape.179), calls=%async_computation.4 | async-start | bytes 262144 | tf_op jit(solution)/shard_map/all_to_all | solution.py:89
  78.7 4.3 %all-to-all-done.4 = bf16[8,2,4096]{2,1,0:T(2,128)(2,1)S(1)} async-done(((bf16[8,2,4096]{2,1,0:T(2,128)(2,1)}), bf16[8,2,4096]{2,1,0:T(2,128)(2,1)S(1)}, u32[]{:S(2)}, u32[]{:S(2)}) %all-to-all-start.4) | async-done | bytes 131104 | tf_op jit(solution)/shard_map/all_to_all | solution.py:89
  83.0 3.4 %all-to-all-start.3 = ((bf16[8,2,4096]{2,1,0:T(2,128)(2,1)}), bf16[8,2,4096]{2,1,0:T(2,128)(2,1)S(1)}, u32[]{:S(2)}, u32[]{:S(2)}) async-start(bf16[8,2,4096]{2,1,0:T(2,128)(2,1)} %reshape.177), calls=%async_computation.3 | async-start | bytes 262144 | tf_op jit(solution)/shard_map/all_to_all | solution.py:88
  87.6 4.2 %all-to-all-done.3 = bf16[8,2,4096]{2,1,0:T(2,128)(2,1)S(1)} async-done(((bf16[8,2,4096]{2,1,0:T(2,128)(2,1)}), bf16[8,2,4096]{2,1,0:T(2,128)(2,1)S(1)}, u32[]{:S(2)}, u32[]{:S(2)}) %all-to-all-start.3) | async-done | bytes 131104 | tf_op jit(solution)/shard_map/all_to_all | solution.py:88
  (76 shorter events, 24.7 us)
Async XLA Ops:
  0.6 7.3 %copy-start = (s32[1,8,4,32]{3,2,1,0:T(4,128)S(1)}, s32[1,8,4,32]{3,2,1,0:T(4,128)}, u32[]{:S(2)}) copy-start(s32[1,8,4,32]{3,2,1,0:T(4,128)} %param.6) | copy-start | bytes 12292
  2.6 5.5 %copy-start.3 = (bf16[2,64,512]{2,1,0:T(8,128)(2,1)S(1)}, bf16[2,64,512]{2,1,0:T(8,128)(2,1)}, u32[]{:S(2)}) copy-start(bf16[2,64,512]{2,1,0:T(8,128)(2,1)} %param.5) | copy-start | bytes 393220
  2.6 10.8 %all-to-all-start = ((bf16[8,2,4096]{2,1,0:T(2,128)(2,1)}), bf16[8,2,4096]{2,1,0:T(2,128)(2,1)S(1)}, u32[]{:S(2)}, u32[]{:S(2)}) async-start(bf16[8,2,4096]{2,1,0:T(2,128)(2,1)} %reshape.175), calls=%async_computation | async-start | bytes 262144 | tf_op jit(solution)/shard_map/all_to_all | solution.py:66
  13.5 8.8 %all-to-all-start.1 = ((bf16[8,2,4096]{2,1,0:T(2,128)(2,1)}), bf16[8,2,4096]{2,1,0:T(2,128)(2,1)S(1)}, u32[]{:S(2)}, u32[]{:S(2)}) async-start(bf16[8,2,4096]{2,1,0:T(2,128)(2,1)} %reshape.173), calls=%async_computation.1 | async-start | bytes 262144 | tf_op jit(solution)/shard_map/all_to_all | solution.py:67
  26.5 19.2 %all-to-all-start.2 = ((bf16[2,2,512,128]{2,1,0,3:T(2,128)(2,1)}), bf16[2,2,512,128]{2,1,0,3:T(2,128)(2,1)S(1)}, u32[]{:S(2)}, u32[]{:S(2)}) async-start(bf16[2,2,512,128]{2,1,0,3:T(2,128)(2,1)} %fusion.22), calls=%async_computation.2 | async-start | bytes 1048576 | tf_op jit(solution)/shard_map/all_to_all | solution.py:73
  57.2 1.0 %copy-start.1 = (f32[4,32,16,64]{3,1,2,0:T(8,128)}, f32[4,32,16,64]{3,1,2,0:T(8,128)S(1)}, u32[]{:S(2)}) copy-start(f32[4,32,16,64]{3,1,2,0:T(8,128)S(1)} %fusion.1) | copy-start | bytes 1572868
  59.6 1.0 %copy-start.2 = (f32[4,32,16,64]{3,1,2,0:T(8,128)}, f32[4,32,16,64]{3,1,2,0:T(8,128)S(1)}, u32[]{:S(2)}) copy-start(f32[4,32,16,64]{3,1,2,0:T(8,128)S(1)} %fusion) | copy-start | bytes 1572868
  60.6 1.0 %slice-start = ((f32[4,32,16,64]{3,1,2,0:T(8,128)}), f32[2,32,16,64]{3,1,2,0:T(8,128)S(1)}, s32[]{:S(2)}) async-start(f32[4,32,16,64]{3,1,2,0:T(8,128)} %copy-done.1), calls=%async_computation.5 | async-start | bytes 1048576 | tf_op jit(solution)/shard_map/slice | solution.py:77
  62.9 1.0 %slice-start.1 = ((f32[4,32,16,64]{3,1,2,0:T(8,128)}), f32[2,32,16,64]{3,1,2,0:T(8,128)S(1)}, s32[]{:S(2)}) async-start(f32[4,32,16,64]{3,1,2,0:T(8,128)} %copy-done.2), calls=%async_computation.6 | async-start | bytes 1048576 | tf_op jit(solution)/shard_map/slice | solution.py:78
  74.1 8.8 %all-to-all-start.4 = ((bf16[8,2,4096]{2,1,0:T(2,128)(2,1)}), bf16[8,2,4096]{2,1,0:T(2,128)(2,1)S(1)}, u32[]{:S(2)}, u32[]{:S(2)}) async-start(bf16[8,2,4096]{2,1,0:T(2,128)(2,1)} %reshape.179), calls=%async_computation.4 | async-start | bytes 262144 | tf_op jit(solution)/shard_map/all_to_all | solution.py:89
  83.0 8.8 %all-to-all-start.3 = ((bf16[8,2,4096]{2,1,0:T(2,128)(2,1)}), bf16[8,2,4096]{2,1,0:T(2,128)(2,1)S(1)}, u32[]{:S(2)}, u32[]{:S(2)}) async-start(bf16[8,2,4096]{2,1,0:T(2,128)(2,1)} %reshape.177), calls=%async_computation.3 | async-start | bytes 262144 | tf_op jit(solution)/shard_map/all_to_all | solution.py:88
where the time goes:
time: 93.8 us; the launch traced here: 93.1 us
  waiting for transfers between devices  30.5 us (33%)
  local copies, waits for them, and re-layouts  21.7 us (23%)
  starting transfers between devices  20.3 us (22%)
  matrix products  15.2 us (16%)
  other arithmetic  4.33 us (5%)
  between operations  1.15 us (1%)
    all_to_all x1, waiting for transfers between devices, shards(): lax.all_to_all(outgoing, 'elem', split_axis=3, concat_axis=3, tiled=True)  13.1 us
    unnamed x18, local copies, waits for them, and re-layouts  7.64 us
    all_to_all x1, starting transfers between devices, shards(): lax.all_to_all(g_lesser, 'energy', split_axis=2, concat_axis=1, tiled=True)  5.3 us
    all_to_all x1, starting transfers between devices, shards(): lax.all_to_all(outgoing, 'elem', split_axis=3, concat_axis=3, tiled=True)  4.87 us
    all_to_all x1, waiting for transfers between devices, shards(): lax.all_to_all(g_greater, 'energy', split_axis=2, concat_axis=1, tiled=True)  4.68 us
    all_to_all x1, waiting for transfers between devices, shards(): lax.all_to_all(result[1], 'energy', split_axis=1, concat_axis=2, tiled=True)  4.29 us
    all_to_all x1, waiting for transfers between devices, shards(): lax.all_to_all(g_lesser, 'energy', split_axis=2, concat_axis=1, tiled=True)  4.26 us
    all_to_all x1, waiting for transfers between devices, shards(): lax.all_to_all(result[0], 'energy', split_axis=1, concat_axis=2, tiled=True)  4.19 us
  transfers between devices with their start and end apart: 5, of which 5 were waited for; matrix products, arithmetic and copies ran while one was open for 5% of the time, Pallas kernels for 0%

commit v1 on v0

v1 whole, which is shorter than its diff:
```python
import functools
import math

import jax
import jax.numpy as jnp
import numpy as np
from jax import lax
from jax.experimental import pallas as pl
from jax.experimental.pallas import tpu as pltpu
from jax.sharding import PartitionSpec as P

BF16 = jnp.bfloat16
F32 = jnp.float32
VMEM_BYTES = 24 * 1024 * 1024


def fourier_tables(length):
    half = length // 2
    steps = np.arange(half)[:, None] * np.arange(length)[None, :] % length
    angle = steps * (2.0 * math.pi / length)
    sines = np.sin(angle)
    sines[0] = 1.0 - 2.0 * (np.arange(length) % 2)
    table = np.concatenate([np.cos(angle), sines], 0)

    def split(values):
        high = values.astype(np.float32).astype(jnp.bfloat16)
        low = (values - high.astype(np.float64)).astype(np.float32).astype(jnp.bfloat16)
        return np.stack([high, low])

    return split(table), split(table.T)


def pack_kernel(lesser_ref, greater_ref, out_ref):
    pieces, _, _, lanes = out_ref.shape
    width = lanes // 2
    for n in range(pieces):
        cols = slice(n * width, (n + 1) * width)
        out_ref[n] = jnp.concatenate([lesser_ref[:, :, cols], greater_ref[:, :, cols]], axis=-1)


def unpack_kernel(in_ref, lesser_ref, greater_ref):
    pieces, _, _, lanes = in_ref.shape
    width = lanes // 2
    per_tile = max(1, 128 // width)
    for first in range(0, pieces, per_tile):
        group = range(first, min(first + per_tile, pieces))
        cols = slice(first * width, (group[-1] + 1) * width)
        lesser_ref[:, :, cols] = jnp.concatenate([in_ref[n][:, :, :width] for n in group], axis=-1)
        greater_ref[:, :, cols] = jnp.concatenate([in_ref[n][:, :, width:] for n in group], axis=-1)


def one_hot(index_row, depth):
    rows = lax.broadcasted_iota(jnp.int32, (depth, index_row.shape[-1]), 0)
    return jnp.where(rows == index_row, 1.0, 0.0).astype(BF16)


def dot(a, b):
    return lax.dot_general(a, b, (((1,), (0,)), ((), ())), preferred_element_type=F32)


def rows_of(ref, part):
    blocks, _, energies, lanes = ref.shape
    return ref[:, part].reshape(blocks * energies, lanes)


def select_kernel(index_ref, own_ref, out_ref):
    lanes = own_ref.shape[-1]
    for part in range(2):
        picked = dot(rows_of(own_ref, part), one_hot(index_ref[part : part + 1, :], lanes))
        if part == 0:
            total = picked
        else:
            total = total + picked
    out_ref[...] = total.astype(BF16)


def correlate_kernel(index_ref, own_ref, far_ref, forward_ref, inverse_ref, out_ref):
    blocks, _, energies, lanes = own_ref.shape
    length = blocks * energies
    half = length // 2
    far = far_ref[...]
    pick_own = one_hot(index_ref[0:1, :], lanes)
    columns = [rows_of(own_ref, 0), rows_of(own_ref, 1)]
    for part in range(2):
        pick_far = one_hot(index_ref[1 + part : 2 + part, :], far.shape[-1])
        columns.append((dot(columns[part], pick_own) + dot(far, pick_far)).astype(BF16))
    signals = jnp.concatenate(columns, axis=-1)
    spectra = dot(forward_ref[0], signals) + dot(forward_ref[1], signals)
    even, odd = spectra[:half], spectra[half:]

    def split(values):
        return [values[:, i * lanes : (i + 1) * lanes] for i in range(4)]

    def combine(even, odd, odd_even):
        a_re, a_im, c_re, c_im = split(even)
        b_re, b_im, d_re, d_im = split(odd)
        u_re = a_re * c_re - a_im * c_im + (b_re * d_re - b_im * d_im)
        u_im = a_re * c_im + a_im * c_re + (b_re * d_im + b_im * d_re)
        v_re = b_re * c_re - b_im * c_im - (a_re * d_re - a_im * d_im)
        v_im = b_re * c_im + b_im * c_re - (a_re * d_im + a_im * d_re)
        return u_re, u_im, v_re, v_im

    def ends(even, odd):
        a_re, a_im, c_re, c_im = split(even)
        b_re, b_im, d_re, d_im = split(odd)
        return (
            0.5 * (a_re * c_re - a_im * c_im),
            0.5 * (a_re * c_im + a_im * c_re),
            0.5 * (b_re * d_re - b_im * d_im),
            0.5 * (b_re * d_im + b_im * d_re),
        )

    first = lax.broadcasted_iota(jnp.int32, (half, lanes), 0) == 0
    u_re, u_im, v_re, v_im = [
        jnp.where(first, end, mid) for mid, end in zip(combine(even, odd, None), ends(even, odd))
    ]
    top = jnp.concatenate([u_im, -u_re], axis=-1)
    bottom = jnp.concatenate([v_im, -v_re], axis=-1)
    products = jnp.concatenate([top, bottom], axis=0)
    high = products.astype(BF16)
    low = (products - high.astype(F32)).astype(BF16)
    back = dot(inverse_ref[0], high) + (dot(inverse_ref[0], low) + dot(inverse_ref[1], high))
    result = (back * (2.0 / (length * math.sqrt(length)))).astype(BF16)
    for part in range(2):
        out_ref[:, part] = result[:, part * lanes : (part + 1) * lanes].reshape(blocks, energies, lanes)


def call(kernel, out_shape, flops, *args):
    outs = out_shape if isinstance(out_shape, (list, tuple)) else [out_shape]
    moved = sum(math.prod(v.shape) * v.dtype.itemsize for v in [*args, *outs])
    return pl.pallas_call(
        kernel,
        out_shape=out_shape,
        compiler_params=pltpu.CompilerParams(vmem_limit_bytes=VMEM_BYTES),
        cost_estimate=pl.CostEstimate(flops=flops, bytes_accessed=moved, transcendentals=0),
    )(*args)


def shards(g_lesser, g_greater, send_rows, partner_slot):
    piece = lax.axis_index("energy")
    group = lax.axis_index("elem")
    pieces = lax.axis_size("energy")
    groups = lax.axis_size("elem")
    _, energies, group_rows = g_lesser.shape
    width = group_rows // pieces
    cap = send_rows.shape[-1]
    lanes = 2 * width
    length = pieces * energies

    packed = call(
        pack_kernel, jax.ShapeDtypeStruct((pieces, 2, energies, lanes), BF16), 0, g_lesser, g_greater
    )
    own = lax.all_to_all(packed, "energy", split_axis=0, concat_axis=0, tiled=True)

    lists = lax.dynamic_index_in_dim(send_rows[0], piece, 0, keepdims=False)
    slots = lax.dynamic_slice_in_dim(partner_slot, piece * width, width, 0)
    source, place = slots // cap, slots % cap
    if groups == 4 and cap >= 2:
        ids = jnp.arange(groups, dtype=jnp.int32)
        others = jnp.where((ids != group)[:, None], lists, 0)
        cross_rows = jnp.sum(others, axis=0)
        flip = jnp.sum(jnp.where(jnp.sum(others, axis=1) > 0, ids ^ group, 0))
        near_rows = jnp.sum(jnp.where((ids == group)[:, None], lists, 0), axis=0)
        none = jnp.full((2 * cap,), -1, jnp.int32)
        both = jnp.concatenate([cross_rows, cross_rows + width])
        picks = jnp.stack([jnp.concatenate([both, none]), jnp.concatenate([none, both])])
        outgoing = call(
            select_kernel, jax.ShapeDtypeStruct((length, 4 * cap), BF16), 4 * length * lanes * 4 * cap, picks, own
        )

        def swap(values, bit):
            return lax.ppermute(values, "elem", [(i, i ^ bit) for i in range(groups)])

        one = swap(outgoing, 1)
        two = swap(jnp.where(flip == 3, one, outgoing), 2)
        far = jnp.where(flip == 1, one, two)
        steps = jnp.arange(cap, dtype=jnp.int32)
        row = jnp.sum(jnp.where(place[:, None] == steps[None, :], near_rows[None, :], 0), axis=1)
        near = source == group
        own_row = jnp.where(near, row, -1)
        own_greater = jnp.where(near, row + width, -1)
        far_lesser = jnp.where(near, -1, place)
        far_greater = jnp.where(near, -1, place + cap)
        far_step = 2 * cap
    else:
        rows = lists.reshape(-1)
        pick = (jnp.arange(width, dtype=jnp.int32)[:, None] == rows[None, :]).astype(BF16)
        split = own.reshape(pieces, 2, energies, 2, width)
        outgoing = jnp.einsum("pceds,sm->mpced", split, pick, preferred_element_type=F32).astype(BF16)
        incoming = lax.all_to_all(outgoing, "elem", split_axis=0, concat_axis=0, tiled=True)
        far = jnp.transpose(incoming, (1, 3, 2, 4, 0)).reshape(length, 4 * groups * cap)
        own_row = jnp.full((width,), -1, jnp.int32)
        own_greater = own_row
        far_lesser = slots
        far_greater = slots + groups * cap
        far_step = 2 * groups * cap
    far_row = jnp.concatenate([far_greater, far_lesser])
    index = jnp.stack(
        [jnp.concatenate([own_greater, own_row]), far_row, jnp.where(far_row < 0, -1, far_row + far_step)]
    )
    forward, inverse = fourier_tables(length)
    result = call(
        correlate_kernel,
        jax.ShapeDtypeStruct((pieces, 2, energies, lanes), BF16),
        2 * length * length * lanes * 14,
        index,
        own,
        far,
        jnp.asarray(forward),
        jnp.asarray(inverse),
    )
    back = lax.all_to_all(result, "energy", split_axis=0, concat_axis=0, tiled=True)
    out = jax.ShapeDtypeStruct((2, energies, group_rows), BF16)
    lesser_out, greater_out = call(unpack_kernel, [out, out], 0, back)
    return (lesser_out, greater_out)


def solution(mesh):
    in_specs = (
        P(None, "energy", "elem"),
        P(None, "energy", "elem"),
        P("elem", None, None, None),
        P("elem"),
    )
    out_specs = (P(None, "energy", "elem"), P(None, "energy", "elem"))
    return jax.shard_map(shards, mesh=mesh, in_specs=in_specs, out_specs=out_specs, check_vma=False)
```

time: 93.8 us -> 41.3 us (0.44)
  waiting for transfers between devices: 30.5 us -> 10.2 us
  local copies, waits for them, and re-layouts: 21.7 us -> 1.81 us
  matrix products: 15.2 us -> 0 us
  starting transfers between devices: 20.3 us -> 9.47 us
  blocking collectives: 0 us -> 9.84 us
  Pallas kernels: 0 us -> 4.06 us
    all_to_all x5 -> x1, waiting for transfers between devices: 30.5 us -> 3.69 us  [shards(): lax.all_to_all(packed, 'energy', split_axis=0, concat_axis=0, tiled=True)]
    dot_general x16 -> x0, matrix products: 15.2 us -> none  [the longest x2 2.17 us: transform(): product('qb,skbe->sqke', sin_second, twist_im)]
    all_to_all x5 -> x1, starting transfers between devices: 20.3 us -> 5.17 us  [shards(): lax.all_to_all(packed, 'energy', split_axis=0, concat_axis=0, tiled=True)]
    all_to_all x0 -> x1, blocking collectives: none -> 9.84 us  [shards(): lax.all_to_all(result, 'energy', split_axis=0, concat_axis=0, tiled=True)]
    slice x17 -> x0, local copies, waits for them, and re-layouts: 6.54 us -> none  [the longest x3 1.95 us: shards(): spec_re, spec_im = transform(signals[:, 0], signals[:, 1], False)]
    ppermute x0 -> x2, waiting for transfers between devices: none -> 6.52 us  [swap(): return lax.ppermute(values, 'elem', [(i, i ^ bit) for i in range(groups)])]
    unnamed x18 -> x8, local copies, waits for them, and re-layouts: 7.64 us -> 1.81 us
    ppermute x0 -> x2, starting transfers between devices: none -> 4.3 us  [swap(): return lax.ppermute(values, 'elem', [(i, i ^ bit) for i in range(groups)])]
  transfers between devices with their start and end apart: 5 -> 3, of which waited for: 5 -> 3; matrix products, arithmetic and copies ran while one was open for 5% -> 8% of each run, Pallas kernels for 0% -> 0%
where the time goes in v1:
time: 41.3 us; the launch traced here: 40.9 us
  waiting for transfers between devices  10.2 us (25%)
  blocking collectives  9.84 us (24%)
  starting transfers between devices  9.47 us (23%)
  Pallas kernels  4.06 us (10%)
  other arithmetic  3.5 us (8%)
  between operations  2.01 us (5%)
  local copies, waits for them, and re-layouts  1.81 us (4%)
    all_to_all x1, blocking collectives, shards(): lax.all_to_all(result, 'energy', split_axis=0, concat_axis=0, tiled=True)  9.84 us
    ppermute x2, waiting for transfers between devices, swap(): return lax.ppermute(values, 'elem', [(i, i ^ bit) for i in range(groups)])  6.52 us
    all_to_all x1, starting transfers between devices, shards(): lax.all_to_all(packed, 'energy', split_axis=0, concat_axis=0, tiled=True)  5.17 us
    ppermute x2, starting transfers between devices, swap(): return lax.ppermute(values, 'elem', [(i, i ^ bit) for i in range(groups)])  4.3 us
    pallas_call x4, Pallas kernels, call(): pl.pallas_call(kernel, out_shape=out_shape, compiler_params=pltpu.Compile...  4.06 us
    all_to_all x1, waiting for transfers between devices, shards(): lax.all_to_all(packed, 'energy', split_axis=0, concat_axis=0, tiled=True)  3.69 us
    unnamed x8, local copies, waits for them, and re-layouts  1.81 us
    reduce_sum x2, other arithmetic, shards(): flip = jnp.sum(jnp.where(jnp.sum(others, axis=1) > 0, ids ^ group, 0))  1.51 us
  transfers between devices with their start and end apart: 3, of which 3 were waited for; matrix products, arithmetic and copies ran while one was open for 8% of the time, Pallas kernels for 0%

profile of v1, /device:TPU:0, one launch (start us, length us, event | category | flops | bytes accessed | tf_op | source)
XLA Modules:
  0.0 40.9 jit_solution(13283201049450297770)
XLA Ops:
  0.6 0.0 copy-start
  0.6 0.9 %copy-done = bf16[2,64,512]{2,1,0:T(8,128)(2,1)S(1)} copy-done((bf16[2,64,512]{2,1,0:T(8,128)(2,1)S(1)}, bf16[2,64,512]{2,1,0:T(8,128)(2,1)}, u32[]{:S(2)}) %copy-start) | copy-done | bytes 131096
  1.5 0.9 %copy-done.1 = bf16[2,64,512]{2,1,0:T(8,128)(2,1)S(1)} copy-done((bf16[2,64,512]{2,1,0:T(8,128)(2,1)S(1)}, bf16[2,64,512]{2,1,0:T(8,128)(2,1)}, u32[]{:S(2)}) %copy-start.1) | copy-done | bytes 131096
  2.4 0.8 %shard_map.77 = bf16[8,2,64,128]{3,2,1,0:T(8,128)(2,1)} custom-call(bf16[2,64,512]{2,1,0:T(8,128)(2,1)S(1)} %copy-done, bf16[2,64,512]{2,1,0:T(8,128)(2,1)S(1)} %copy-done.1), custom_call_target="tpu_custom_call" | custom-call | bytes 524288 | tf_op jit(solution)/shard_map/pallas_call | solution.py:131
  3.3 5.2 %all-to-all-start = ((bf16[8,2,64,128]{3,2,1,0:T(8,128)(2,1)}), bf16[8,2,64,128]{3,2,1,0:T(8,128)(2,1)S(1)}, u32[]{:S(2)}, u32[]{:S(2)}) async-start(bf16[8,2,64,128]{3,2,1,0:T(8,128)(2,1)} %shard_map.77), calls=%async_computation | async-start | bytes 524288 | tf_op jit(solution)/shard_map/all_to_all | solution.py:153
  8.4 0.9 %fusion.2 = (s32[4]{0:T(128)S(1)}, s32[32]{0:T(128)S(1)}, s32[32]{0:T(128)S(1)}) fusion(s32[1,8,4,32]{3,2,1,0:T(4,128)} %param.8, s32[]{:T(128)S(6)} %select_n.76, pred[4]{0:T(512)(128)(4,1)S(1)} %get-tuple-element.14, pred[4]{0:T(512)(128)(4,1)S(1)} %get-tuple-element.15), kind=kLoop, calls=%fused_computation.13 | loop fusion | flops 572 | bytes 796 | tf_op jit(solution)/shard_map/reduce_sum | solution.py:162
  9.3 0.6 %fusion.3 = s32[]{:T(128)} fusion(s32[4]{0:T(128)S(1)} %get-tuple-element.2, s32[]{:T(128)S(6)} %axis_index.25), kind=kLoop, calls=%fused_computation.18 | loop fusion | flops 15 | bytes 24 | tf_op jit(solution)/shard_map/reduce_sum | solution.py:162
  10.0 0.1 add_bitcast_fusion.2
  10.0 0.8 %and_select_fusion = (s32[64]{0:T(128)S(1)}, s32[64]{0:T(128)S(1)}) fusion(s32[512]{0:T(512)} %param.9, s32[]{:T(128)S(6)} %select_n.73), kind=kLoop, calls=%fused_computation.10 | loop fusion | flops 704 | bytes 772 | tf_op jit(solution)/shard_map/jit(remainder)/select_n | solution.py:157
  10.8 0.1 select_reduce_fusion
  10.9 0.8 %add_select_fusion.1 = (s32[64]{0:T(128)S(1)}, pred[64]{0:T(512)(128)(4,1)S(1)}) fusion(s32[64]{0:T(128)S(1)} %select_reduce_fusion, s32[]{:T(128)S(6)} %axis_index.25, s32[64]{0:T(128)S(1)} %get-tuple-element.8, s32[512]{0:T(512)} %param.9, s32[]{:T(128)S(6)} %select_n.73), kind=kLoop, calls=%fused_computation.26 | loop fusion | flops 960 | bytes 1096 | tf_op jit(solution)/shard_map/jit(_where)/select_n | solution.py:181
  11.7 3.7 %all-to-all-done.own_ref = bf16[8,2,64,128]{3,2,1,0:T(8,128)(2,1)S(1)} async-done(((bf16[8,2,64,128]{3,2,1,0:T(8,128)(2,1)}), bf16[8,2,64,128]{3,2,1,0:T(8,128)(2,1)S(1)}, u32[]{:S(2)}, u32[]{:S(2)}) %all-to-all-start) | async-done | bytes 262176 | tf_op jit(solution)/shard_map/all_to_all | solution.py:153
  15.4 0.2 shard_map.78
  15.6 1.6 %collective-permute-start = (bf16[512,128]{1,0:T(8,128)(2,1)S(1)}, bf16[512,128]{1,0:T(8,128)(2,1)S(1)}, u32[]{:S(2)}, u32[]{:S(2)}) collective-permute-start(bf16[512,128]{1,0:T(8,128)(2,1)S(1)} %shard_map.78), channel_id=1, source_target_pairs={{0,1},{1,0},{2,3},{3,2},{4,5},{5,4},{6,7},{7,6},{8,9},{9,8},{10,11... | collective-permute-start | bytes 393224 | tf_op jit(solution)/shard_map/ppermute | solution.py:172
  17.2 0.1 add_bitcast_fusion
  18.0 0.1 add_bitcast_fusion.1
  18.0 2.6 %collective-permute-done = bf16[512,128]{1,0:T(8,128)(2,1)S(1)} collective-permute-done((bf16[512,128]{1,0:T(8,128)(2,1)S(1)}, bf16[512,128]{1,0:T(8,128)(2,1)S(1)}, u32[]{:S(2)}, u32[]{:S(2)}) %collective-permute-start) | collective-permute-done | bytes 131104 | tf_op jit(solution)/shard_map/ppermute | solution.py:172
  20.6 2.7 %collective-permute-start.1 = (bf16[512,128]{1,0:T(8,128)(2,1)S(1)}, bf16[512,128]{1,0:T(8,128)(2,1)S(1)}, u32[]{:S(2)}, u32[]{:S(2)}) collective-permute-start(bf16[512,128]{1,0:T(8,128)(2,1)S(1)} %broadcast_select_fusion), channel_id=1, source_target_pairs={{0,2},{1,3},{2,0},{3,1},{4,6},{5,7},{6,4},{7,5},{8,10},{9,11},{10,... | collective-permute-start | bytes 393224 | tf_op jit(solution)/shard_map/ppermute | solution.py:172
  23.3 0.1 compare_select_fusion.1
  24.1 3.9 %collective-permute-done.1 = bf16[512,128]{1,0:T(8,128)(2,1)S(1)} collective-permute-done((bf16[512,128]{1,0:T(8,128)(2,1)S(1)}, bf16[512,128]{1,0:T(8,128)(2,1)S(1)}, u32[]{:S(2)}, u32[]{:S(2)}) %collective-permute-start.1) | collective-permute-done | bytes 131104 | tf_op jit(solution)/shard_map/ppermute | solution.py:172
  28.0 0.0 copy-done.2
  28.0 2.2 %shard_map.79 = bf16[8,2,64,128]{3,2,1,0:T(8,128)(2,1)S(1)} custom-call(s32[3,128]{1,0:T(4,128)S(1)} %pad_add_fusion.index_ref, bf16[8,2,64,128]{3,2,1,0:T(8,128)(2,1)S(1)} %all-to-all-done.own_ref, bf16[512,128]{1,0:T(8,128)(2,1)S(1)} %broadcast_select_fusion.1.far_ref, bf16[2,512,512]{2,1,0:T(8,128)(2,1)S(1)} %copy-done.2, bf16[2,512,512]{2,1,0:T(8,128)(2,1)S(1)} %copy-done.3), custom_call_target="tpu_custom_call" | custom-call | flops 939524096 | bytes 2754048 | tf_op jit(solution)/shard_map/pallas_call | solution.py:131
  30.2 9.8 %all_to_all.10.in_ref = bf16[8,2,64,128]{3,2,1,0:T(8,128)(2,1)S(1)} all-to-all(bf16[8,2,64,128]{3,2,1,0:T(8,128)(2,1)S(1)} %shard_map.79), channel_id=1, replica_groups=mesh['energy'=8,'elem'=4] {'energy'}, dimensions={0} | all-to-all | bytes 524288 | tf_op jit(solution)/shard_map/all_to_all | solution.py:212
  40.1 0.8 %shard_map.80 = (bf16[2,64,512]{2,1,0:T(8,128)(2,1)}, bf16[2,64,512]{2,1,0:T(8,128)(2,1)}) custom-call(bf16[8,2,64,128]{3,2,1,0:T(8,128)(2,1)S(1)} %all_to_all.10.in_ref), custom_call_target="tpu_custom_call" | custom-call | bytes 524288 | tf_op jit(solution)/shard_map/pallas_call | solution.py:131
  (12 shorter events, 0.1 us)
Async XLA Ops:
  0.6 0.9 %copy-start = (bf16[2,64,512]{2,1,0:T(8,128)(2,1)S(1)}, bf16[2,64,512]{2,1,0:T(8,128)(2,1)}, u32[]{:S(2)}) copy-start(bf16[2,64,512]{2,1,0:T(8,128)(2,1)} %lesser_ref.1) | copy-start | bytes 393220
  1.5 0.9 %copy-start.1 = (bf16[2,64,512]{2,1,0:T(8,128)(2,1)S(1)}, bf16[2,64,512]{2,1,0:T(8,128)(2,1)}, u32[]{:S(2)}) copy-start(bf16[2,64,512]{2,1,0:T(8,128)(2,1)} %greater_ref.1) | copy-start | bytes 393220
  2.4 25.6 %copy-start.2 = (bf16[2,512,512]{2,1,0:T(8,128)(2,1)S(1)}, bf16[2,512,512]{2,1,0:T(8,128)(2,1)}, u32[]{:S(2)}) copy-start(bf16[2,512,512]{2,1,0:T(8,128)(2,1)} %constant.63.clone.forward_ref) | copy-start | bytes 3145732
  2.4 25.6 %copy-start.3 = (bf16[2,512,512]{2,1,0:T(8,128)(2,1)S(1)}, bf16[2,512,512]{2,1,0:T(8,128)(2,1)}, u32[]{:S(2)}) copy-start(bf16[2,512,512]{2,1,0:T(8,128)(2,1)} %constant.64.clone.inverse_ref) | copy-start | bytes 3145732
  3.3 12.1 %all-to-all-start = ((bf16[8,2,64,128]{3,2,1,0:T(8,128)(2,1)}), bf16[8,2,64,128]{3,2,1,0:T(8,128)(2,1)S(1)}, u32[]{:S(2)}, u32[]{:S(2)}) async-start(bf16[8,2,64,128]{3,2,1,0:T(8,128)(2,1)} %shard_map.77), calls=%async_computation | async-start | bytes 524288 | tf_op jit(solution)/shard_map/all_to_all | solution.py:153
  15.6 5.0 %collective-permute-start = (bf16[512,128]{1,0:T(8,128)(2,1)S(1)}, bf16[512,128]{1,0:T(8,128)(2,1)S(1)}, u32[]{:S(2)}, u32[]{:S(2)}) collective-permute-start(bf16[512,128]{1,0:T(8,128)(2,1)S(1)} %shard_map.78), channel_id=1, source_target_pairs={{0,1},{1,0},{2,3},{3,2},{4,5},{5,4},{6,7},{7,6},{8,9},{9,8},{10,11... | collective-permute-start | bytes 393224 | tf_op jit(solution)/shard_map/ppermute | solution.py:172
  20.6 7.3 %collective-permute-start.1 = (bf16[512,128]{1,0:T(8,128)(2,1)S(1)}, bf16[512,128]{1,0:T(8,128)(2,1)S(1)}, u32[]{:S(2)}, u32[]{:S(2)}) collective-permute-start(bf16[512,128]{1,0:T(8,128)(2,1)S(1)} %broadcast_select_fusion), channel_id=1, source_target_pairs={{0,2},{1,3},{2,0},{3,1},{4,6},{5,7},{6,4},{7,5},{8,10},{9,11},{10,... | collective-permute-start | bytes 393224 | tf_op jit(solution)/shard_map/ppermute | solution.py:172

commit v2 on v1

v2 whole, which is shorter than its diff:
```python
import functools
import math

import jax
import jax.numpy as jnp
import numpy as np
from jax import lax
from jax.experimental import pallas as pl
from jax.experimental.pallas import tpu as pltpu
from jax.sharding import PartitionSpec as P

BF16 = jnp.bfloat16
F32 = jnp.float32
VMEM_BYTES = 24 * 1024 * 1024


def fourier_tables(length):
    half = length // 2
    steps = np.arange(half)[:, None] * np.arange(length)[None, :] % length
    angle = steps * (2.0 * math.pi / length)
    sines = np.sin(angle)
    sines[0] = 1.0 - 2.0 * (np.arange(length) % 2)
    table = np.concatenate([np.cos(angle), sines], 0)

    def split(values):
        high = values.astype(np.float32).astype(jnp.bfloat16)
        low = (values - high.astype(np.float64)).astype(np.float32).astype(jnp.bfloat16)
        return np.stack([high, low])

    return split(table), split(table.T)


def pack_kernel(lesser_ref, greater_ref, out_ref):
    pieces, _, _, lanes = out_ref.shape
    width = lanes // 2
    for n in range(pieces):
        cols = slice(n * width, (n + 1) * width)
        out_ref[n] = jnp.concatenate([lesser_ref[:, :, cols], greater_ref[:, :, cols]], axis=-1)


def unpack_kernel(in_ref, lesser_ref, greater_ref):
    pieces, _, _, lanes = in_ref.shape
    width = lanes // 2
    per_tile = max(1, 128 // width)
    for first in range(0, pieces, per_tile):
        group = range(first, min(first + per_tile, pieces))
        cols = slice(first * width, (group[-1] + 1) * width)
        lesser_ref[:, :, cols] = jnp.concatenate([in_ref[n][:, :, :width] for n in group], axis=-1)
        greater_ref[:, :, cols] = jnp.concatenate([in_ref[n][:, :, width:] for n in group], axis=-1)


def one_hot(index_row, depth):
    rows = lax.broadcasted_iota(jnp.int32, (depth, index_row.shape[-1]), 0)
    return jnp.where(rows == index_row, 1.0, 0.0).astype(BF16)


def dot(a, b):
    return lax.dot_general(a, b, (((1,), (0,)), ((), ())), preferred_element_type=F32)


def rows_of(ref, part):
    blocks, _, energies, lanes = ref.shape
    return ref[:, part].reshape(blocks * energies, lanes)


def forward_sums(table_ref, signals):
    return dot(table_ref[0], signals) + dot(table_ref[1], signals)


def correlate(near, far, inverse_ref):
    half = near.shape[0] // 2
    length = near.shape[0]
    lanes = near.shape[1] // 2

    def parts(sums):
        return [sums[i * half : (i + 1) * half, j * lanes : (j + 1) * lanes] for i in range(2) for j in range(2)]

    a_re, a_im, b_re, b_im = parts(near)
    c_re, c_im, d_re, d_im = parts(far)
    first = lax.broadcasted_iota(jnp.int32, (half, lanes), 0) == 0
    ac_re, ac_im = a_re * c_re - a_im * c_im, a_re * c_im + a_im * c_re
    bd_re, bd_im = b_re * d_re - b_im * d_im, b_re * d_im + b_im * d_re
    u_re = jnp.where(first, 0.5 * ac_re, ac_re + bd_re)
    u_im = jnp.where(first, 0.5 * ac_im, ac_im + bd_im)
    v_re = jnp.where(first, 0.5 * bd_re, b_re * c_re - b_im * c_im - (a_re * d_re - a_im * d_im))
    v_im = jnp.where(first, 0.5 * bd_im, b_re * c_im + b_im * c_re - (a_re * d_im + a_im * d_re))
    top = jnp.concatenate([u_im, -u_re], axis=-1)
    bottom = jnp.concatenate([v_im, -v_re], axis=-1)
    products = jnp.concatenate([top, bottom], axis=0)
    high = products.astype(BF16)
    low = (products - high.astype(F32)).astype(BF16)
    back = dot(inverse_ref[0], high) + (dot(inverse_ref[0], low) + dot(inverse_ref[1], high))
    return (back * (2.0 / (length * math.sqrt(length)))).astype(BF16)


def correlate_kernel(index_ref, own_ref, far_ref, forward_ref, inverse_ref, out_ref):
    blocks, _, energies, lanes = own_ref.shape
    far = far_ref[...]
    own, partner = [], []
    for part in range(2):
        pick_far = one_hot(index_ref[part : part + 1, :], far.shape[-1])
        own.append(rows_of(own_ref, part))
        partner.append(dot(far, pick_far).astype(BF16))
    near = forward_sums(forward_ref, jnp.concatenate(own, axis=-1))
    result = correlate(near, forward_sums(forward_ref, jnp.concatenate(partner, axis=-1)), inverse_ref)
    for part in range(2):
        out_ref[:, part] = result[:, part * lanes : (part + 1) * lanes].reshape(blocks, energies, lanes)


def call(kernel, out_shape, flops, *args, scratch=()):
    outs = out_shape if isinstance(out_shape, (list, tuple)) else [out_shape]
    moved = sum(math.prod(v.shape) * v.dtype.itemsize for v in [*args, *outs])
    return pl.pallas_call(
        kernel,
        out_shape=out_shape,
        scratch_shapes=list(scratch),
        compiler_params=pltpu.CompilerParams(vmem_limit_bytes=VMEM_BYTES),
        cost_estimate=pl.CostEstimate(flops=flops, bytes_accessed=moved, transcendentals=0),
    )(*args)


def place():
    me = lax.axis_index("energy")
    return me // 2, me % 2


def split_kernel(lesser_ref, greater_ref, *out_refs):
    chip, _ = place()
    width = out_refs[0].shape[-1] // 2
    for j, out_ref in enumerate(out_refs):
        cols = pl.ds(pl.multiple_of((chip ^ j) * 2 * width, 2 * width), 2 * width)
        lesser, greater = lesser_ref[:, :, cols], greater_ref[:, :, cols]
        out_ref[0] = jnp.concatenate([lesser[..., :width], greater[..., :width]], axis=-1)
        out_ref[1] = jnp.concatenate([lesser[..., width:], greater[..., width:]], axis=-1)


def lane_row(lanes):
    return lax.broadcasted_iota(jnp.int32, (1, lanes), 1)


def row_list(lists_ref, piece, group, own):
    lists = lists_ref[piece]
    here = lax.broadcasted_iota(jnp.int32, lists.shape, 0) == group
    return jnp.sum(jnp.where(here == own, lists, 0), axis=0, keepdims=True)


def outgoing_kernel(lists_ref, *refs):
    in_refs, (first_ref, second_ref, sibling_ref) = refs[:4], refs[4:]
    chip, core = place()
    group = lax.axis_index("elem")
    energies, lanes = first_ref.shape[1:]
    cap = lanes // 4
    lane = lane_row(lanes)
    for which, out_ref in enumerate((first_ref, second_ref)):
        rows = row_list(lists_ref, 2 * chip + which, group, False)
        rows = rows + jnp.where(lane // cap % 2 == 1, lanes // 2, 0)
        total = None
        for part in range(2):
            values = jnp.concatenate([ref[which, part] for ref in in_refs], axis=0)
            picked = dot(values, one_hot(jnp.where(lane // (2 * cap) == part, rows, -1), lanes))
            total = picked if total is None else total + picked
        out_ref[...] = total.astype(BF16).reshape(4, energies, lanes)
    for j, ref in enumerate(in_refs):
        sibling_ref[j] = ref[1 - core]


def exchange_kernel(lists_ref, slots_ref, *refs):
    in_refs, (sibling_ref, far_ref, far_sibling_ref, forward_ref, inverse_ref) = refs[:4], refs[4:9]
    out_refs, (own, far) = refs[9:13], refs[13:]
    chip, core = place()
    group = lax.axis_index("elem")
    energies, lanes = far_ref.shape[1:]
    width, cap = lanes // 2, lanes // 4
    for j, ref in enumerate(in_refs):
        here = pl.ds(pl.multiple_of((2 * (chip ^ j) + core) * energies, energies), energies)
        there = pl.ds(pl.multiple_of((2 * (chip ^ j) + 1 - core) * energies, energies), energies)
        for part in range(2):
            cols = slice(part * lanes, (part + 1) * lanes)
            own[here, cols] = ref[core, part]
            own[there, cols] = sibling_ref[j, part]
        far[here, :] = far_ref[j]
        far[there, :] = far_sibling_ref[j]
    piece = 2 * chip + core
    lane = lane_row(lanes)
    slots = slots_ref[pl.ds(piece, 1), :]
    source = slots // cap
    spot = slots - source * cap + jnp.where(lane < width, cap, 0)
    rows = row_list(lists_ref, piece, group, True) + jnp.where(lane // cap % 2 == 1, width, 0)
    chosen = one_hot(jnp.where(lane < 2 * cap, rows, -1), lanes)
    pick_own = dot(chosen, one_hot(jnp.where(source == group, spot, -1), lanes)).astype(BF16)
    cross = far[...]
    partner = []
    for part in range(2):
        pick_far = one_hot(jnp.where(source == group, -1, spot + 2 * cap * part), lanes)
        both = dot(own[:, part * lanes : (part + 1) * lanes], pick_own) + dot(cross, pick_far)
        partner.append(both.astype(BF16))
    near = forward_sums(forward_ref, own[...])
    result = correlate(near, forward_sums(forward_ref, jnp.concatenate(partner, axis=-1)), inverse_ref)
    own[...] = result
    for j, ref in enumerate(out_refs):
        for which in range(2):
            here = pl.ds(pl.multiple_of((2 * (chip ^ j) + which) * energies, energies), energies)
            for part in range(2):
                ref[which, part] = own[here, part * lanes : (part + 1) * lanes]


def join_kernel(*refs):
    in_refs, sibling_refs, (lesser_ref, greater_ref) = refs[:4], refs[4:8], refs[8:]
    chip, core = place()
    width = in_refs[0].shape[-1] // 2
    for j in range(4):
        mine, other = in_refs[j][core], sibling_refs[j][core]
        even = jnp.where(core == 0, mine, other)
        odd = jnp.where(core == 0, other, mine)
        cols = pl.ds(pl.multiple_of((chip ^ j) * 2 * width, 2 * width), 2 * width)
        lesser_ref[:, :, cols] = jnp.concatenate([even[..., :width], odd[..., :width]], axis=-1)
        greater_ref[:, :, cols] = jnp.concatenate([even[..., width:], odd[..., width:]], axis=-1)


def swap(values, axis, bit):
    return lax.ppermute(values, axis, [(i, i ^ bit) for i in range(lax.axis_size(axis))])


def over_chips(values):
    return [values[0]] + [swap(values[j], "energy", 2 * j) for j in range(1, 4)]


def four_chips(g_lesser, g_greater, send_rows, partner_slot):
    chip, core = place()
    group = lax.axis_index("elem")
    _, energies, group_rows = g_lesser.shape
    groups, cap = send_rows.shape[2:]
    lanes = 4 * cap
    length = 8 * energies
    pair = jax.ShapeDtypeStruct((2, 2, energies, lanes), BF16)
    quarter = jax.ShapeDtypeStruct((4, energies, lanes), BF16)
    sibling = jax.ShapeDtypeStruct((4, 2, energies, lanes), BF16)

    lists = jnp.tile(send_rows[0], (1, 1, 4))
    slots = jnp.tile(partner_slot.reshape(8, lanes // 2), (1, 2))
    ids = jnp.arange(groups, dtype=jnp.int32)
    filled = jnp.sum(send_rows[0], axis=2) > 0
    flips = jnp.sum(jnp.where(filled, (ids ^ group)[None, :], 0), axis=1)
    flip_first = lax.dynamic_index_in_dim(flips, 2 * chip, 0, keepdims=False)
    flip_second = lax.dynamic_index_in_dim(flips, 2 * chip + 1, 0, keepdims=False)

    arrived = over_chips(call(split_kernel, [pair] * 4, 0, g_lesser, g_greater))
    first, second, for_sibling = call(outgoing_kernel, [quarter, quarter, sibling], 2**26, lists, *arrived)
    first_one, second_one = swap(first, "elem", 1), swap(second, "elem", 2)
    from_sibling = swap(for_sibling, "energy", 1)
    first_two = swap(jnp.where(flip_first == 3, first_one, first), "elem", 2)
    second_two = swap(jnp.where(flip_second == 3, second_one, second), "elem", 1)
    first = jnp.where(flip_first == 1, first_one, first_two)
    second = jnp.where(flip_second == 2, second_one, second_two)
    far_sibling = swap(jnp.where(core == 0, second, first), "energy", 1)
    far = jnp.where(core == 0, first, second)
    forward, inverse = fourier_tables(length)
    results = call(
        exchange_kernel,
        [pair] * 4,
        2 * length * length * lanes * 14,
        lists,
        slots,
        *arrived,
        from_sibling,
        far,
        far_sibling,
        jnp.asarray(forward),
        jnp.asarray(inverse),
        scratch=[pltpu.VMEM((length, 2 * lanes), BF16), pltpu.VMEM((length, lanes), BF16)],
    )
    back = over_chips(results)
    back_sibling = [swap(values, "energy", 1) for values in back]
    out = jax.ShapeDtypeStruct((2, energies, group_rows), BF16)
    return tuple(call(join_kernel, [out, out], 0, *back, *back_sibling))


def any_mesh(g_lesser, g_greater, send_rows, partner_slot):
    piece = lax.axis_index("energy")
    pieces = lax.axis_size("energy")
    _, energies, group_rows = g_lesser.shape
    groups, cap = send_rows.shape[2:]
    width = group_rows // pieces
    lanes = 2 * width
    length = pieces * energies
    packed_shape = jax.ShapeDtypeStruct((pieces, 2, energies, lanes), BF16)
    packed = call(pack_kernel, packed_shape, 0, g_lesser, g_greater)
    own = lax.all_to_all(packed, "energy", split_axis=0, concat_axis=0, tiled=True)
    rows = lax.dynamic_index_in_dim(send_rows[0], piece, 0, keepdims=False).reshape(-1)
    slots = lax.dynamic_slice_in_dim(partner_slot, piece * width, width, 0)
    pick = (jnp.arange(width, dtype=jnp.int32)[:, None] == rows[None, :]).astype(BF16)
    split = own.reshape(pieces, 2, energies, 2, width)
    outgoing = jnp.einsum("pceds,sm->mpced", split, pick, preferred_element_type=F32).astype(BF16)
    incoming = lax.all_to_all(outgoing, "elem", split_axis=0, concat_axis=0, tiled=True)
    table_width = groups * cap
    far = jnp.transpose(incoming, (1, 3, 2, 4, 0)).reshape(length, 4 * table_width)
    index = jnp.concatenate([slots + table_width, slots])
    index = jnp.stack([index, index + 2 * table_width])
    forward, inverse = fourier_tables(length)
    result = call(
        correlate_kernel,
        packed_shape,
        2 * length * length * lanes * 14,
        index,
        own,
        far,
        jnp.asarray(forward),
        jnp.asarray(inverse),
    )
    back = lax.all_to_all(result, "energy", split_axis=0, concat_axis=0, tiled=True)
    out = jax.ShapeDtypeStruct((2, energies, group_rows), BF16)
    return tuple(call(unpack_kernel, [out, out], 0, back))


def shards(g_lesser, g_greater, send_rows, partner_slot):
    _, pieces, groups, cap = send_rows.shape
    fits = pieces == 8 and groups == 4 and cap == 32 and partner_slot.shape[0] == 512
    path = four_chips if fits else any_mesh
    return path(g_lesser, g_greater, send_rows, partner_slot)


def solution(mesh):
    in_specs = (
        P(None, "energy", "elem"),
        P(None, "energy", "elem"),
        P("elem", None, None, None),
        P("elem"),
    )
    out_specs = (P(None, "energy", "elem"), P(None, "energy", "elem"))
    return jax.shard_map(shards, mesh=mesh, in_specs=in_specs, out_specs=out_specs, check_vma=False)
```

time: 41.3 us -> 40.2 us (0.973)
  blocking collectives: 9.84 us -> 0 us
  starting transfers between devices: 9.47 us -> 14.4 us
  local copies, waits for them, and re-layouts: 1.81 us -> 5.2 us
  other arithmetic: 3.5 us -> 1.07 us
  waiting for transfers between devices: 10.2 us -> 12.5 us
  between operations: 2.01 us -> 3.36 us
  Pallas kernels: 4.06 us -> 3.29 us
    ppermute x2 -> x16, starting transfers between devices: 4.3 us -> 14.4 us  [swap(): lax.ppermute(values, axis, [(i, i ^ bit) for i in range(lax.axis_size(axi...]
    all_to_all x1 -> x0, blocking collectives: 9.84 us -> none  [shards(): lax.all_to_all(result, 'energy', split_axis=0, concat_axis=0, tiled=True)]
    ppermute x2 -> x16, waiting for transfers between devices: 6.52 us -> 12.5 us  [swap(): lax.ppermute(values, axis, [(i, i ^ bit) for i in range(lax.axis_size(axi...]
    all_to_all x1 -> x0, starting transfers between devices: 5.17 us -> none  [shards(): lax.all_to_all(packed, 'energy', split_axis=0, concat_axis=0, tiled=True)]
    all_to_all x1 -> x0, waiting for transfers between devices: 3.69 us -> none  [shards(): lax.all_to_all(packed, 'energy', split_axis=0, concat_axis=0, tiled=True)]
    unnamed x8 -> x10, local copies, waits for them, and re-layouts: 1.81 us -> 3.61 us
    select_n x6 -> x3, other arithmetic: 1.64 us -> 0.04 us  [the longest x1 0.02 us: four_chips(): far_sibling = swap(jnp.where(core == 0, second, first), 'energy', 1)]
    another operation x1 -> x5, local copies, waits for them, and re-layouts: 0.01 us -> 1 us  [the longest x2 0.84 us: four_chips(): lists = jnp.tile(send_rows[0], (1, 1, 4))]
  transfers between devices with their start and end apart: 3 -> 16, of which waited for: 3 -> 10; matrix products, arithmetic and copies ran while one was open for 8% -> 7% of each run, Pallas kernels for 0% -> 0%
where the time goes in v2:
time: 40.2 us; the launch traced here: 39.8 us
  starting transfers between devices  14.4 us (36%)
  waiting for transfers between devices  12.5 us (31%)
  local copies, waits for them, and re-layouts  5.2 us (13%)
  between operations  3.36 us (8%)
  Pallas kernels  3.29 us (8%)
  other arithmetic  1.07 us (3%)
    ppermute x16, starting transfers between devices, swap(): lax.ppermute(values, axis, [(i, i ^ bit) for i in range(lax.axis_size(axi...  14.4 us
    ppermute x16, waiting for transfers between devices, swap(): lax.ppermute(values, axis, [(i, i ^ bit) for i in range(lax.axis_size(axi...  12.5 us
    unnamed x10, local copies, waits for them, and re-layouts  3.61 us
    pallas_call x4, Pallas kernels, call(): pl.pallas_call(kernel, out_shape=out_shape, scratch_shapes=list(scratch),...  3.29 us
    reduce_sum x1, other arithmetic, four_chips(): filled = jnp.sum(send_rows[0], axis=2) > 0  0.92 us
    another operation x2, local copies, waits for them, and re-layouts, four_chips(): lists = jnp.tile(send_rows[0], (1, 1, 4))  0.84 us
  transfers between devices with their start and end apart: 16, of which 10 were waited for; matrix products, arithmetic and copies ran while one was open for 7% of the time, Pallas kernels for 0%

profile of v2, /device:TPU:0, one launch (start us, length us, event | category | flops | bytes accessed | tf_op | source)
XLA Modules:
  0.0 39.8 jit_solution(18255287551569057667)
XLA Ops:
  0.6 0.9 %copy-done = bf16[2,64,512]{2,1,0:T(8,128)(2,1)S(1)} copy-done((bf16[2,64,512]{2,1,0:T(8,128)(2,1)S(1)}, bf16[2,64,512]{2,1,0:T(8,128)(2,1)}, u32[]{:S(2)}) %copy-start) | copy-done | bytes 131096
  1.5 0.9 %copy-done.1 = bf16[2,64,512]{2,1,0:T(8,128)(2,1)S(1)} copy-done((bf16[2,64,512]{2,1,0:T(8,128)(2,1)S(1)}, bf16[2,64,512]{2,1,0:T(8,128)(2,1)}, u32[]{:S(2)}) %copy-start.1) | copy-done | bytes 131096
  2.6 3.0 %collective-permute-start = (bf16[2,2,64,128]{3,2,1,0:T(8,128)(2,1)S(1)}, bf16[2,2,64,128]{3,2,1,0:T(8,128)(2,1)S(1)}, u32[]{:S(2)}, u32[]{:S(2)}) collective-permute-start(bf16[2,2,64,128]{3,2,1,0:T(8,128)(2,1)S(1)} %get-tuple-element.14), channel_id=1, source_target_pairs={{0,8},{4,12},{8,0},{12,4},{16,24},{20,28},{24,16},{28,20},{1,9},{5... | collective-permute-start | bytes 196616 | tf_op jit(solution)/shard_map/ppermute | solution.py:221
  5.6 1.5 %collective-permute-start.1 = (bf16[2,2,64,128]{3,2,1,0:T(8,128)(2,1)S(1)}, bf16[2,2,64,128]{3,2,1,0:T(8,128)(2,1)S(1)}, u32[]{:S(2)}, u32[]{:S(2)}) collective-permute-start(bf16[2,2,64,128]{3,2,1,0:T(8,128)(2,1)S(1)} %get-tuple-element.15), channel_id=1, source_target_pairs={{0,16},{4,20},{8,24},{12,28},{16,0},{20,4},{24,8},{28,12},{1,17},{... | collective-permute-start | bytes 196616 | tf_op jit(solution)/shard_map/ppermute | solution.py:221
  7.1 0.9 %reduce_sum.18 = s32[8,4]{1,0:T(8,128)S(1)} reduce(s32[1,8,4,32]{3,2,1,0:T(4,128)} %param.8, s32[]{:T(128)} %constant.47.clone.1), dimensions={0,3}, to_apply=%region_0.1 | reduce | flops 992 | bytes 4228 | tf_op jit(solution)/shard_map/reduce_sum | solution.py:242
  8.1 0.7 %tile.21 = s32[8,4,4,32]{3,2,1,0:T(4,128)S(1)} broadcast(s32[8,4,32]{2,1,0:T(4,128)} %bitcast.5), dimensions={0,1,3} | broadcast | bytes 20480 | tf_op jit(solution)/shard_map/tile | solution.py:239
  8.9 0.9 %collective-permute-done.1.refs_2_ = bf16[2,2,64,128]{3,2,1,0:T(8,128)(2,1)S(1)} collective-permute-done((bf16[2,2,64,128]{3,2,1,0:T(8,128)(2,1)S(1)}, bf16[2,2,64,128]{3,2,1,0:T(8,128)(2,1)S(1)}, u32[]{:S(2)}, u32[]{:S(2)}) %collective-permute-start.1) | collective-permute-done | bytes 65568 | tf_op jit(solution)/shard_map/ppermute | solution.py:221
  9.9 2.4 %collective-permute-done.2.refs_3_ = bf16[2,2,64,128]{3,2,1,0:T(8,128)(2,1)S(1)} collective-permute-done((bf16[2,2,64,128]{3,2,1,0:T(8,128)(2,1)S(1)}, bf16[2,2,64,128]{3,2,1,0:T(8,128)(2,1)S(1)}, u32[]{:S(2)}, u32[]{:S(2)}) %collective-permute-start.2) | collective-permute-done | bytes 65568 | tf_op jit(solution)/shard_map/ppermute | solution.py:221
  12.5 2.7 %collective-permute-start.6 = (bf16[4,64,128]{2,1,0:T(8,128)(2,1)S(1)}, bf16[4,64,128]{2,1,0:T(8,128)(2,1)S(1)}, u32[]{:S(2)}, u32[]{:S(2)}) collective-permute-start(bf16[4,64,128]{2,1,0:T(8,128)(2,1)S(1)} %get-tuple-element.19), channel_id=1, source_target_pairs={{0,2},{1,3},{2,0},{3,1},{4,6},{5,7},{6,4},{7,5},{8,10},{9,11},{10,... | collective-permute-start | bytes 196616 | tf_op jit(solution)/shard_map/ppermute | solution.py:221
  15.3 0.6 %fusion = (s32[1]{0:T(128)}, s32[1]{0:T(128)}) fusion(s32[8]{0:T(128)S(1)} %select_reduce_fusion, s32[]{:T(128)S(6)} %select_n.67, s32[]{:T(128)S(6)} %select_n.62), kind=kLoop, calls=%fused_computation.8 | loop fusion | bytes 24 | tf_op jit(solution)/shard_map/jit(dynamic_index_in_dim)/dynamic_slice | solution.py:245
  17.2 1.6 %collective-permute-start.4 = (bf16[4,64,128]{2,1,0:T(8,128)(2,1)S(1)}, bf16[4,64,128]{2,1,0:T(8,128)(2,1)S(1)}, u32[]{:S(2)}, u32[]{:S(2)}) collective-permute-start(bf16[4,64,128]{2,1,0:T(8,128)(2,1)S(1)} %get-tuple-element.18), channel_id=1, source_target_pairs={{0,1},{1,0},{2,3},{3,2},{4,5},{5,4},{6,7},{7,6},{8,9},{9,8},{10,11... | collective-permute-start | bytes 196616 | tf_op jit(solution)/shard_map/ppermute | solution.py:221
  18.8 0.7 %collective-permute-start.7 = (bf16[4,64,128]{2,1,0:T(8,128)(2,1)S(1)}, bf16[4,64,128]{2,1,0:T(8,128)(2,1)S(1)}, u32[]{:S(2)}, u32[]{:S(2)}) collective-permute-start(bf16[4,64,128]{2,1,0:T(8,128)(2,1)S(1)} %broadcast_select_fusion), channel_id=1, source_target_pairs={{0,1},{1,0},{2,3},{3,2},{4,5},{5,4},{6,7},{7,6},{8,9},{9,8},{10,11... | collective-permute-start | bytes 196616 | tf_op jit(solution)/shard_map/ppermute | solution.py:221
  19.5 2.0 %collective-permute-done.4 = bf16[4,64,128]{2,1,0:T(8,128)(2,1)S(1)} collective-permute-done((bf16[4,64,128]{2,1,0:T(8,128)(2,1)S(1)}, bf16[4,64,128]{2,1,0:T(8,128)(2,1)S(1)}, u32[]{:S(2)}, u32[]{:S(2)}) %collective-permute-start.4) | collective-permute-done | bytes 65568 | tf_op jit(solution)/shard_map/ppermute | solution.py:221
  21.5 1.2 %collective-permute-start.5 = (bf16[4,64,128]{2,1,0:T(8,128)(2,1)S(1)}, bf16[4,64,128]{2,1,0:T(8,128)(2,1)S(1)}, u32[]{:S(2)}, u32[]{:S(2)}) collective-permute-start(bf16[4,64,128]{2,1,0:T(8,128)(2,1)S(1)} %broadcast_select_fusion.2), channel_id=1, source_target_pairs={{0,2},{1,3},{2,0},{3,1},{4,6},{5,7},{6,4},{7,5},{8,10},{9,11},{10,... | collective-permute-start | bytes 196616 | tf_op jit(solution)/shard_map/ppermute | solution.py:221
  24.1 2.7 %collective-permute-done.5 = bf16[4,64,128]{2,1,0:T(8,128)(2,1)S(1)} collective-permute-done((bf16[4,64,128]{2,1,0:T(8,128)(2,1)S(1)}, bf16[4,64,128]{2,1,0:T(8,128)(2,1)S(1)}, u32[]{:S(2)}, u32[]{:S(2)}) %collective-permute-start.5) | collective-permute-done | bytes 65568 | tf_op jit(solution)/shard_map/ppermute | solution.py:221
  28.1 1.2 %copy-done.3 = bf16[2,512,512]{2,1,0:T(8,128)(2,1)S(1)} copy-done((bf16[2,512,512]{2,1,0:T(8,128)(2,1)S(1)}, bf16[2,512,512]{2,1,0:T(8,128)(2,1)}, u32[]{:S(2)}) %copy-start.3) | copy-done | bytes 1048600
  29.3 2.1 %shard_map.79 = (bf16[2,2,64,128]{3,2,1,0:T(8,128)(2,1)S(1)}, bf16[2,2,64,128]{3,2,1,0:T(8,128)(2,1)S(1)}, bf16[2,2,64,128]{3,2,1,0:T(8,128)(2,1)S(1)}, bf16[2,2,64,128]{3,2,1,0:T(8,128)(2,1)S(1)}) custom-call(s32[8,4,128]{2,1,0:T(4,128)S(1)} %tile.22.lists_ref, s32[8,128]{1,0:T(8,128)S(1)} %tile.25.slots_ref, ...), custom_call_target="tpu_custom_call" | custom-call | flops 939524096 | bytes 2904064 | tf_op jit(solution)/shard_map/pallas_call | solution.py:113
  31.4 0.6 %collective-permute-start.9 = (bf16[2,2,64,128]{3,2,1,0:T(8,128)(2,1)S(1)}, bf16[2,2,64,128]{3,2,1,0:T(8,128)(2,1)S(1)}, u32[]{:S(2)}, u32[]{:S(2)}) collective-permute-start(bf16[2,2,64,128]{3,2,1,0:T(8,128)(2,1)S(1)} %get-tuple-element.21), channel_id=1, source_target_pairs={{0,8},{4,12},{8,0},{12,4},{16,24},{20,28},{24,16},{28,20},{1,9},{5... | collective-permute-start | bytes 196616 | tf_op jit(solution)/shard_map/ppermute | solution.py:221
  32.5 2.4 %collective-permute-start.11 = (bf16[2,2,64,128]{3,2,1,0:T(8,128)(2,1)S(1)}, bf16[2,2,64,128]{3,2,1,0:T(8,128)(2,1)S(1)}, u32[]{:S(2)}, u32[]{:S(2)}) collective-permute-start(bf16[2,2,64,128]{3,2,1,0:T(8,128)(2,1)S(1)} %get-tuple-element.23), channel_id=1, source_target_pairs={{0,24},{4,28},{8,16},{12,20},{16,8},{20,12},{24,0},{28,4},{1,25},{... | collective-permute-start | bytes 196616 | tf_op jit(solution)/shard_map/ppermute | solution.py:221
  35.0 0.9 %collective-permute-done.9.refs_1_ = bf16[2,2,64,128]{3,2,1,0:T(8,128)(2,1)S(1)} collective-permute-done((bf16[2,2,64,128]{3,2,1,0:T(8,128)(2,1)S(1)}, bf16[2,2,64,128]{3,2,1,0:T(8,128)(2,1)S(1)}, u32[]{:S(2)}, u32[]{:S(2)}) %collective-permute-start.9) | collective-permute-done | bytes 65568 | tf_op jit(solution)/shard_map/ppermute | solution.py:221
  35.9 1.1 %collective-permute-done.10.refs_2_ = bf16[2,2,64,128]{3,2,1,0:T(8,128)(2,1)S(1)} collective-permute-done((bf16[2,2,64,128]{3,2,1,0:T(8,128)(2,1)S(1)}, bf16[2,2,64,128]{3,2,1,0:T(8,128)(2,1)S(1)}, u32[]{:S(2)}, u32[]{:S(2)}) %collective-permute-start.10) | collective-permute-done | bytes 65568 | tf_op jit(solution)/shard_map/ppermute | solution.py:221
  37.0 0.7 %collective-permute-done.11.refs_3_ = bf16[2,2,64,128]{3,2,1,0:T(8,128)(2,1)S(1)} collective-permute-done((bf16[2,2,64,128]{3,2,1,0:T(8,128)(2,1)S(1)}, bf16[2,2,64,128]{3,2,1,0:T(8,128)(2,1)S(1)}, u32[]{:S(2)}, u32[]{:S(2)}) %collective-permute-start.11) | collective-permute-done | bytes 65568 | tf_op jit(solution)/shard_map/ppermute | solution.py:221
  38.2 0.7 %collective-permute-done.15.refs_7_ = bf16[2,2,64,128]{3,2,1,0:T(8,128)(2,1)S(1)} collective-permute-done((bf16[2,2,64,128]{3,2,1,0:T(8,128)(2,1)S(1)}, bf16[2,2,64,128]{3,2,1,0:T(8,128)(2,1)S(1)}, u32[]{:S(2)}, u32[]{:S(2)}) %collective-permute-start.15) | collective-permute-done | bytes 65568 | tf_op jit(solution)/shard_map/ppermute | solution.py:221
  39.0 0.8 %shard_map.80 = (bf16[2,64,512]{2,1,0:T(8,128)(2,1)}, bf16[2,64,512]{2,1,0:T(8,128)(2,1)}) custom-call(bf16[2,2,64,128]{3,2,1,0:T(8,128)(2,1)S(1)} %get-tuple-element.20.refs_0_, bf16[2,2,64,128]{3,2,1,0:T(8,128)(2,1)S(1)} %collective-permute-done.9.refs_1_, bf16[2,2,64,128]{3,2,1,0:T(8,128)(2,1)S(1)} %collective-permute-done.10.refs_2_, ...), custom_call_target="tpu_custom_call" | custom-call | bytes 786432 | tf_op jit(solution)/shard_map/pallas_call | solution.py:113
  (34 shorter events, 3.1 us)
Async XLA Ops:
  0.6 0.9 %copy-start = (bf16[2,64,512]{2,1,0:T(8,128)(2,1)S(1)}, bf16[2,64,512]{2,1,0:T(8,128)(2,1)}, u32[]{:S(2)}) copy-start(bf16[2,64,512]{2,1,0:T(8,128)(2,1)} %lesser_ref.1) | copy-start | bytes 393220
  1.5 0.9 %copy-start.1 = (bf16[2,64,512]{2,1,0:T(8,128)(2,1)S(1)}, bf16[2,64,512]{2,1,0:T(8,128)(2,1)}, u32[]{:S(2)}) copy-start(bf16[2,64,512]{2,1,0:T(8,128)(2,1)} %greater_ref.1) | copy-start | bytes 393220
  2.4 25.7 %copy-start.2 = (bf16[2,512,512]{2,1,0:T(8,128)(2,1)S(1)}, bf16[2,512,512]{2,1,0:T(8,128)(2,1)}, u32[]{:S(2)}) copy-start(bf16[2,512,512]{2,1,0:T(8,128)(2,1)} %constant.57.clone.refs_7_) | copy-start | bytes 3145732
  2.6 6.3 %collective-permute-start = (bf16[2,2,64,128]{3,2,1,0:T(8,128)(2,1)S(1)}, bf16[2,2,64,128]{3,2,1,0:T(8,128)(2,1)S(1)}, u32[]{:S(2)}, u32[]{:S(2)}) collective-permute-start(bf16[2,2,64,128]{3,2,1,0:T(8,128)(2,1)S(1)} %get-tuple-element.14), channel_id=1, source_target_pairs={{0,8},{4,12},{8,0},{12,4},{16,24},{20,28},{24,16},{28,20},{1,9},{5... | collective-permute-start | bytes 196616 | tf_op jit(solution)/shard_map/ppermute | solution.py:221
  5.6 4.3 %collective-permute-start.1 = (bf16[2,2,64,128]{3,2,1,0:T(8,128)(2,1)S(1)}, bf16[2,2,64,128]{3,2,1,0:T(8,128)(2,1)S(1)}, u32[]{:S(2)}, u32[]{:S(2)}) collective-permute-start(bf16[2,2,64,128]{3,2,1,0:T(8,128)(2,1)S(1)} %get-tuple-element.15), channel_id=1, source_target_pairs={{0,16},{4,20},{8,24},{12,28},{16,0},{20,4},{24,8},{28,12},{1,17},{... | collective-permute-start | bytes 196616 | tf_op jit(solution)/shard_map/ppermute | solution.py:221
  7.1 5.2 %collective-permute-start.2 = (bf16[2,2,64,128]{3,2,1,0:T(8,128)(2,1)S(1)}, bf16[2,2,64,128]{3,2,1,0:T(8,128)(2,1)S(1)}, u32[]{:S(2)}, u32[]{:S(2)}) collective-permute-start(bf16[2,2,64,128]{3,2,1,0:T(8,128)(2,1)S(1)} %get-tuple-element.16), channel_id=1, source_target_pairs={{0,24},{4,28},{8,16},{12,20},{16,8},{20,12},{24,0},{28,4},{1,25},{... | collective-permute-start | bytes 196616 | tf_op jit(solution)/shard_map/ppermute | solution.py:221
  12.5 6.3 %collective-permute-start.6 = (bf16[4,64,128]{2,1,0:T(8,128)(2,1)S(1)}, bf16[4,64,128]{2,1,0:T(8,128)(2,1)S(1)}, u32[]{:S(2)}, u32[]{:S(2)}) collective-permute-start(bf16[4,64,128]{2,1,0:T(8,128)(2,1)S(1)} %get-tuple-element.19), channel_id=1, source_target_pairs={{0,2},{1,3},{2,0},{3,1},{4,6},{5,7},{6,4},{7,5},{8,10},{9,11},{10,... | collective-permute-start | bytes 196616 | tf_op jit(solution)/shard_map/ppermute | solution.py:221
  17.2 4.3 %collective-permute-start.4 = (bf16[4,64,128]{2,1,0:T(8,128)(2,1)S(1)}, bf16[4,64,128]{2,1,0:T(8,128)(2,1)S(1)}, u32[]{:S(2)}, u32[]{:S(2)}) collective-permute-start(bf16[4,64,128]{2,1,0:T(8,128)(2,1)S(1)} %get-tuple-element.18), channel_id=1, source_target_pairs={{0,1},{1,0},{2,3},{3,2},{4,5},{5,4},{6,7},{7,6},{8,9},{9,8},{10,11... | collective-permute-start | bytes 196616 | tf_op jit(solution)/shard_map/ppermute | solution.py:221
  18.8 5.2 %collective-permute-start.7 = (bf16[4,64,128]{2,1,0:T(8,128)(2,1)S(1)}, bf16[4,64,128]{2,1,0:T(8,128)(2,1)S(1)}, u32[]{:S(2)}, u32[]{:S(2)}) collective-permute-start(bf16[4,64,128]{2,1,0:T(8,128)(2,1)S(1)} %broadcast_select_fusion), channel_id=1, source_target_pairs={{0,1},{1,0},{2,3},{3,2},{4,5},{5,4},{6,7},{7,6},{8,9},{9,8},{10,11... | collective-permute-start | bytes 196616 | tf_op jit(solution)/shard_map/ppermute | solution.py:221
  21.5 5.2 %collective-permute-start.5 = (bf16[4,64,128]{2,1,0:T(8,128)(2,1)S(1)}, bf16[4,64,128]{2,1,0:T(8,128)(2,1)S(1)}, u32[]{:S(2)}, u32[]{:S(2)}) collective-permute-start(bf16[4,64,128]{2,1,0:T(8,128)(2,1)S(1)} %broadcast_select_fusion.2), channel_id=1, source_target_pairs={{0,2},{1,3},{2,0},{3,1},{4,6},{5,7},{6,4},{7,5},{8,10},{9,11},{10,... | collective-permute-start | bytes 196616 | tf_op jit(solution)/shard_map/ppermute | solution.py:221
  24.0 3.6 %collective-permute-start.3 = (bf16[4,2,64,128]{3,2,1,0:T(8,128)(2,1)S(1)}, bf16[4,2,64,128]{3,2,1,0:T(8,128)(2,1)S(1)}, u32[]{:S(2)}, u32[]{:S(2)}) collective-permute-start(bf16[4,2,64,128]{3,2,1,0:T(8,128)(2,1)S(1)} %get-tuple-element.17), channel_id=1, source_target_pairs={{0,4},{4,0},{8,12},{12,8},{16,20},{20,16},{24,28},{28,24},{1,5},{5... | collective-permute-start | bytes 393224 | tf_op jit(solution)/shard_map/ppermute | solution.py:221
  26.8 0.7 %copy-start.4 = (s32[512]{0:T(512)S(1)}, s32[512]{0:T(512)}, u32[]{:S(2)}) copy-start(s32[512]{0:T(512)} %param.9) | copy-start | bytes 6148
  26.8 1.3 %collective-permute-start.8 = (bf16[4,64,128]{2,1,0:T(8,128)(2,1)S(1)}, bf16[4,64,128]{2,1,0:T(8,128)(2,1)S(1)}, u32[]{:S(2)}, u32[]{:S(2)}) collective-permute-start(bf16[4,64,128]{2,1,0:T(8,128)(2,1)S(1)} %get-tuple-element.24), channel_id=1, source_target_pairs={{0,4},{4,0},{8,12},{12,8},{16,20},{20,16},{24,28},{28,24},{1,5},{5... | collective-permute-start | bytes 196616 | tf_op jit(solution)/shard_map/ppermute | solution.py:221
  28.1 1.2 %copy-start.3 = (bf16[2,512,512]{2,1,0:T(8,128)(2,1)S(1)}, bf16[2,512,512]{2,1,0:T(8,128)(2,1)}, u32[]{:S(2)}) copy-start(bf16[2,512,512]{2,1,0:T(8,128)(2,1)} %constant.58.clone.refs_8_) | copy-start | bytes 3145732
  31.4 4.5 %collective-permute-start.9 = (bf16[2,2,64,128]{3,2,1,0:T(8,128)(2,1)S(1)}, bf16[2,2,64,128]{3,2,1,0:T(8,128)(2,1)S(1)}, u32[]{:S(2)}, u32[]{:S(2)}) collective-permute-start(bf16[2,2,64,128]{3,2,1,0:T(8,128)(2,1)S(1)} %get-tuple-element.21), channel_id=1, source_target_pairs={{0,8},{4,12},{8,0},{12,4},{16,24},{20,28},{24,16},{28,20},{1,9},{5... | collective-permute-start | bytes 196616 | tf_op jit(solution)/shard_map/ppermute | solution.py:221
  32.0 5.0 %collective-permute-start.10 = (bf16[2,2,64,128]{3,2,1,0:T(8,128)(2,1)S(1)}, bf16[2,2,64,128]{3,2,1,0:T(8,128)(2,1)S(1)}, u32[]{:S(2)}, u32[]{:S(2)}) collective-permute-start(bf16[2,2,64,128]{3,2,1,0:T(8,128)(2,1)S(1)} %get-tuple-element.22), channel_id=1, source_target_pairs={{0,16},{4,20},{8,24},{12,28},{16,0},{20,4},{24,8},{28,12},{1,17},{... | collective-permute-start | bytes 196616 | tf_op jit(solution)/shard_map/ppermute | solution.py:221
  32.5 5.2 %collective-permute-start.11 = (bf16[2,2,64,128]{3,2,1,0:T(8,128)(2,1)S(1)}, bf16[2,2,64,128]{3,2,1,0:T(8,128)(2,1)S(1)}, u32[]{:S(2)}, u32[]{:S(2)}) collective-permute-start(bf16[2,2,64,128]{3,2,1,0:T(8,128)(2,1)S(1)} %get-tuple-element.23), channel_id=1, source_target_pairs={{0,24},{4,28},{8,16},{12,20},{16,8},{20,12},{24,0},{28,4},{1,25},{... | collective-permute-start | bytes 196616 | tf_op jit(solution)/shard_map/ppermute | solution.py:221
  35.0 2.7 %collective-permute-start.12 = (bf16[2,2,64,128]{3,2,1,0:T(8,128)(2,1)S(1)}, bf16[2,2,64,128]{3,2,1,0:T(8,128)(2,1)S(1)}, u32[]{:S(2)}, u32[]{:S(2)}) collective-permute-start(bf16[2,2,64,128]{3,2,1,0:T(8,128)(2,1)S(1)} %get-tuple-element.20.refs_0_), channel_id=1, source_target_pairs={{0,4},{4,0},{8,12},{12,8},{16,20},{20,16},{24,28},{28,24},{1,5},{5... | collective-permute-start | bytes 196616 | tf_op jit(solution)/shard_map/ppermute | solution.py:221
  35.9 1.8 %collective-permute-start.13 = (bf16[2,2,64,128]{3,2,1,0:T(8,128)(2,1)S(1)}, bf16[2,2,64,128]{3,2,1,0:T(8,128)(2,1)S(1)}, u32[]{:S(2)}, u32[]{:S(2)}) collective-permute-start(bf16[2,2,64,128]{3,2,1,0:T(8,128)(2,1)S(1)} %collective-permute-done.9.refs_1_), channel_id=1, source_target_pairs={{0,4},{4,0},{8,12},{12,8},{16,20},{20,16},{24,28},{28,24},{1,5},{5... | collective-permute-start | bytes 196616 | tf_op jit(solution)/shard_map/ppermute | solution.py:221
  37.0 1.3 %collective-permute-start.14 = (bf16[2,2,64,128]{3,2,1,0:T(8,128)(2,1)S(1)}, bf16[2,2,64,128]{3,2,1,0:T(8,128)(2,1)S(1)}, u32[]{:S(2)}, u32[]{:S(2)}) collective-permute-start(bf16[2,2,64,128]{3,2,1,0:T(8,128)(2,1)S(1)} %collective-permute-done.10.refs_2_), channel_id=1, source_target_pairs={{0,4},{4,0},{8,12},{12,8},{16,20},{20,16},{24,28},{28,24},{1,5},{5... | collective-permute-start | bytes 196616 | tf_op jit(solution)/shard_map/ppermute | solution.py:221
  37.7 1.3 %collective-permute-start.15 = (bf16[2,2,64,128]{3,2,1,0:T(8,128)(2,1)S(1)}, bf16[2,2,64,128]{3,2,1,0:T(8,128)(2,1)S(1)}, u32[]{:S(2)}, u32[]{:S(2)}) collective-permute-start(bf16[2,2,64,128]{3,2,1,0:T(8,128)(2,1)S(1)} %collective-permute-done.11.refs_3_), channel_id=1, source_target_pairs={{0,4},{4,0},{8,12},{12,8},{16,20},{20,16},{24,28},{28,24},{1,5},{5... | collective-permute-start | bytes 196616 | tf_op jit(solution)/shard_map/ppermute | solution.py:221

commit v3 on v2

v3 whole, which is shorter than its diff:
```python
import functools
import math

import jax
import jax.numpy as jnp
import numpy as np
from jax import lax
from jax.experimental import pallas as pl
from jax.experimental.pallas import tpu as pltpu
from jax.sharding import PartitionSpec as P

BF16 = jnp.bfloat16
F32 = jnp.float32
VMEM_BYTES = 24 * 1024 * 1024


def fourier_tables(length):
    half = length // 2
    steps = np.arange(half)[:, None] * np.arange(length)[None, :] % length
    angle = steps * (2.0 * math.pi / length)
    sines = np.sin(angle)
    sines[0] = 1.0 - 2.0 * (np.arange(length) % 2)
    table = np.concatenate([np.cos(angle), sines], 0)

    def split(values):
        high = values.astype(np.float32).astype(jnp.bfloat16)
        low = (values - high.astype(np.float64)).astype(np.float32).astype(jnp.bfloat16)
        return np.stack([high, low])

    return np.concatenate([split(table), split(table.T)])


def pack_kernel(lesser_ref, greater_ref, out_ref):
    pieces, _, _, lanes = out_ref.shape
    width = lanes // 2
    for n in range(pieces):
        cols = slice(n * width, (n + 1) * width)
        out_ref[n] = jnp.concatenate([lesser_ref[:, :, cols], greater_ref[:, :, cols]], axis=-1)


def unpack_kernel(in_ref, lesser_ref, greater_ref):
    pieces, _, _, lanes = in_ref.shape
    width = lanes // 2
    per_tile = max(1, 128 // width)
    for first in range(0, pieces, per_tile):
        group = range(first, min(first + per_tile, pieces))
        cols = slice(first * width, (group[-1] + 1) * width)
        lesser_ref[:, :, cols] = jnp.concatenate([in_ref[n][:, :, :width] for n in group], axis=-1)
        greater_ref[:, :, cols] = jnp.concatenate([in_ref[n][:, :, width:] for n in group], axis=-1)


def one_hot(index_row, depth):
    rows = lax.broadcasted_iota(jnp.int32, (depth, index_row.shape[-1]), 0)
    return jnp.where(rows == index_row, 1.0, 0.0).astype(BF16)


def dot(a, b):
    return lax.dot_general(a, b, (((1,), (0,)), ((), ())), preferred_element_type=F32)


def rows_of(ref, part):
    blocks, _, energies, lanes = ref.shape
    return ref[:, part].reshape(blocks * energies, lanes)


def forward_sums(table_ref, signals):
    return dot(table_ref[0], signals) + dot(table_ref[1], signals)


def correlate(near, far, table_ref):
    half = near.shape[0] // 2
    length = near.shape[0]
    lanes = near.shape[1] // 2

    def parts(sums):
        return [sums[i * half : (i + 1) * half, j * lanes : (j + 1) * lanes] for i in range(2) for j in range(2)]

    a_re, a_im, b_re, b_im = parts(near)
    c_re, c_im, d_re, d_im = parts(far)
    first = lax.broadcasted_iota(jnp.int32, (half, lanes), 0) == 0
    ac_re, ac_im = a_re * c_re - a_im * c_im, a_re * c_im + a_im * c_re
    bd_re, bd_im = b_re * d_re - b_im * d_im, b_re * d_im + b_im * d_re
    u_re = jnp.where(first, 0.5 * ac_re, ac_re + bd_re)
    u_im = jnp.where(first, 0.5 * ac_im, ac_im + bd_im)
    v_re = jnp.where(first, 0.5 * bd_re, b_re * c_re - b_im * c_im - (a_re * d_re - a_im * d_im))
    v_im = jnp.where(first, 0.5 * bd_im, b_re * c_im + b_im * c_re - (a_re * d_im + a_im * d_re))
    top = jnp.concatenate([u_im, -u_re], axis=-1)
    bottom = jnp.concatenate([v_im, -v_re], axis=-1)
    products = jnp.concatenate([top, bottom], axis=0)
    high = products.astype(BF16)
    low = (products - high.astype(F32)).astype(BF16)
    back = dot(table_ref[2], high) + (dot(table_ref[2], low) + dot(table_ref[3], high))
    return (back * (2.0 / (length * math.sqrt(length)))).astype(BF16)


def correlate_kernel(index_ref, own_ref, far_ref, table_ref, out_ref):
    blocks, _, energies, lanes = own_ref.shape
    far = far_ref[...]
    own, partner = [], []
    for part in range(2):
        pick_far = one_hot(index_ref[part : part + 1, :], far.shape[-1])
        own.append(rows_of(own_ref, part))
        partner.append(dot(far, pick_far).astype(BF16))
    near = forward_sums(table_ref, jnp.concatenate(own, axis=-1))
    result = correlate(near, forward_sums(table_ref, jnp.concatenate(partner, axis=-1)), table_ref)
    for part in range(2):
        out_ref[:, part] = result[:, part * lanes : (part + 1) * lanes].reshape(blocks, energies, lanes)


def call(kernel, out_shape, flops, *args, scratch=(), in_hbm=False):
    outs = out_shape if isinstance(out_shape, (list, tuple)) else [out_shape]
    moved = sum(math.prod(v.shape) * v.dtype.itemsize for v in [*args, *outs])
    more = {"in_specs": [pl.BlockSpec(memory_space=pltpu.HBM)] * len(args)} if in_hbm else {}
    return pl.pallas_call(
        kernel,
        out_shape=out_shape,
        scratch_shapes=list(scratch),
        compiler_params=pltpu.CompilerParams(vmem_limit_bytes=VMEM_BYTES),
        cost_estimate=pl.CostEstimate(flops=flops, bytes_accessed=moved, transcendentals=0),
        **more,
    )(*args)


def place():
    me = lax.axis_index("energy")
    return me // 2, me % 2


def columns_of(chip, width):
    return pl.ds(pl.multiple_of(chip * 2 * width, 2 * width), 2 * width)


def split_kernel(lesser_ref, greater_ref, *refs):
    (diagonal_ref, beside_ref, keep_ref, give_ref, own_ref), (held, sems) = refs[:5], refs[5:]
    chip, core = place()
    width = own_ref.shape[-1] // 2
    copies = [
        [
            pltpu.make_async_copy(ref.at[:, :, columns_of(chip ^ j, width)], held.at[j, i], sems.at[j, i])
            for i, ref in enumerate((lesser_ref, greater_ref))
        ]
        for j in range(4)
    ]
    for j in (3, 2, 1, 0):
        for copy in copies[j]:
            copy.start()
    for j in (3, 2, 1, 0):
        for copy in copies[j]:
            copy.wait()
        lesser, greater = held[j, 0], held[j, 1]
        zero = jnp.concatenate([lesser[..., :width], greater[..., :width]], axis=-1)
        one = jnp.concatenate([lesser[..., width:], greater[..., width:]], axis=-1)
        if j >= 2:
            out_ref = diagonal_ref if j == 3 else beside_ref
            out_ref[0], out_ref[1] = zero, one
        else:
            keep = keep_ref if j == 1 else own_ref
            keep[...] = jnp.where(core == 0, zero, one)
            give_ref[1 - j] = jnp.where(core == 0, one, zero)


def swap(values, axis, bit):
    return lax.ppermute(values, axis, [(i, i ^ bit) for i in range(lax.axis_size(axis))])


def over_energy(diagonal, beside, keep, give, own):
    diagonal = swap(diagonal, "energy", 6)
    beside = swap(beside, "energy", 4)
    got = swap(give, "energy", 1)
    across = swap(jnp.stack([keep, got[0]]), "energy", 2)
    return own, got, across, beside, swap(beside, "energy", 1), diagonal, swap(diagonal, "energy", 1)


def blocks_of(refs, core):
    own_ref, got_ref, across_ref, beside_ref, beside_other_ref, diagonal_ref, diagonal_other_ref = refs
    return [
        (lambda: own_ref[...], lambda: got_ref[1]),
        (lambda: across_ref[0], lambda: across_ref[1]),
        (lambda: beside_ref[core], lambda: beside_other_ref[core]),
        (lambda: diagonal_ref[core], lambda: diagonal_other_ref[core]),
    ]


def lane_row(lanes):
    return lax.broadcasted_iota(jnp.int32, (1, lanes), 1)


def energies_of(device, energies):
    return pl.ds(pl.multiple_of(device * energies, energies), energies)


def gather_kernel(lists_ref, slots_ref, *refs):
    in_refs, (signals_ref, first_ref, second_ref, picks_ref, flip_ref) = refs[:7], refs[7:]
    chip, core = place()
    group = lax.axis_index("elem")
    energies, lanes = in_refs[0].shape[1:]
    width, cap = lanes // 2, lanes // 4
    for j, pair in enumerate(blocks_of(in_refs, core)):
        for which, block in enumerate(pair):
            values = block()
            rows = energies_of(2 * (chip ^ j) + (core if which == 0 else 1 - core), energies)
            for part in range(2):
                signals_ref[rows, part * lanes : (part + 1) * lanes] = values[part]
    piece = 2 * chip + core
    lane = lane_row(lanes)
    lists = lists_ref[piece]
    ids = lax.broadcasted_iota(jnp.int32, lists.shape, 0)
    greater = jnp.where(lane // cap % 2 == 1, width, 0)
    near_rows = jnp.sum(jnp.where(ids == group, lists, 0), axis=0, keepdims=True) + greater
    far_rows = jnp.sum(jnp.where(ids == group, 0, lists), axis=0, keepdims=True) + greater
    filled = jnp.max(lists, axis=1, keepdims=True) > 0
    flip = jnp.sum(jnp.where(filled, ids ^ group, 0), axis=0, keepdims=True)
    flip_ref[...] = jnp.broadcast_to(flip, flip_ref.shape)
    total = None
    for part in range(2):
        pick = one_hot(jnp.where(lane // (2 * cap) == part, far_rows, -1), lanes)
        picked = dot(signals_ref[:, part * lanes : (part + 1) * lanes], pick)
        total = picked if total is None else total + picked
    half = first_ref.shape[0]
    first_ref[...] = total[:half].astype(BF16)
    second_ref[...] = total[half:].astype(BF16)
    slots = slots_ref[pl.ds(piece, 1), :]
    source = slots // cap
    spot = slots - source * cap + jnp.where(lane < width, cap, 0)
    near = one_hot(jnp.where(lane < 2 * cap, near_rows, -1), lanes)
    picks_ref[0] = dot(near, one_hot(jnp.where(source == group, spot, -1), lanes)).astype(BF16)
    for part in range(2):
        picks_ref[1 + part] = one_hot(jnp.where(source == group, -1, spot + 2 * cap * part), lanes)


def own_kernel(signals_ref, picks_ref, table_ref, near_ref, partner_ref):
    lanes = picks_ref.shape[-1]
    for part in range(2):
        cols = slice(part * lanes, (part + 1) * lanes)
        partner_ref[:, cols] = dot(signals_ref[:, cols], picks_ref[0]).astype(BF16)
    near_ref[...] = forward_sums(table_ref, signals_ref[...])


def exchange_kernel(flip_ref, near_ref, partner_ref, picks_ref, first_ref, first_far_ref, second_ref, second_far_ref, table_ref, *refs):
    (diagonal_ref, beside_ref, keep_ref, give_ref, own_ref), (held,) = refs[:5], refs[5:]
    chip, core = place()
    energies, lanes = own_ref.shape[1:]
    flip = flip_ref[0:1, :]
    far = jnp.concatenate(
        [
            jnp.where(flip == 1, first_ref[...], first_far_ref[...]),
            jnp.where(flip == 2, second_ref[...], second_far_ref[...]),
        ],
        axis=0,
    )
    partner = [
        (partner_ref[:, part * lanes : (part + 1) * lanes].astype(F32) + dot(far, picks_ref[1 + part])).astype(BF16)
        for part in range(2)
    ]
    held[...] = correlate(near_ref[...], forward_sums(table_ref, jnp.concatenate(partner, axis=-1)), table_ref)

    def block(device):
        rows = energies_of(device, energies)
        return [held[rows, part * lanes : (part + 1) * lanes] for part in range(2)]

    for j, ref in ((3, diagonal_ref), (2, beside_ref)):
        for which in range(2):
            for part, values in enumerate(block(2 * (chip ^ j) + which)):
                ref[which, part] = values
    for j, ref in ((1, keep_ref), (0, own_ref)):
        for part, values in enumerate(block(2 * (chip ^ j) + core)):
            ref[part] = values
        for part, values in enumerate(block(2 * (chip ^ j) + 1 - core)):
            give_ref[1 - j, part] = values


def join_kernel(*refs):
    in_refs, (lesser_ref, greater_ref) = refs[:7], refs[7:]
    chip, core = place()
    width = in_refs[0].shape[-1] // 2
    for j, (mine, other) in enumerate(blocks_of(in_refs, core)):
        mine, other = mine(), other()
        even = jnp.where(core == 0, mine, other)
        odd = jnp.where(core == 0, other, mine)
        cols = columns_of(chip ^ j, width)
        lesser_ref[:, :, cols] = jnp.concatenate([even[..., :width], odd[..., :width]], axis=-1)
        greater_ref[:, :, cols] = jnp.concatenate([even[..., width:], odd[..., width:]], axis=-1)


def four_chips(g_lesser, g_greater, send_rows, partner_slot):
    _, energies, group_rows = g_lesser.shape
    cap = send_rows.shape[-1]
    lanes = 4 * cap
    length = 8 * energies
    block = jax.ShapeDtypeStruct((2, energies, lanes), BF16)
    pair = jax.ShapeDtypeStruct((2, 2, energies, lanes), BF16)
    leaving = [pair, pair, block, pair, block]
    half = jax.ShapeDtypeStruct((length // 2, lanes), BF16)
    whole = jax.ShapeDtypeStruct((length, 2 * lanes), BF16)
    lists = jnp.tile(send_rows[0], (1, 1, 4))
    slots = jnp.tile(partner_slot.reshape(8, lanes // 2), (1, 2))
    table = jnp.asarray(fourier_tables(length))

    scratch = [pltpu.VMEM((4, 2, 2, energies, lanes), BF16), pltpu.SemaphoreType.DMA((4, 2))]
    packed = call(split_kernel, leaving, 0, g_lesser, g_greater, scratch=scratch, in_hbm=True)
    arrived = over_energy(*packed)
    gathered = [whole, half, half, jax.ShapeDtypeStruct((3, lanes, lanes), BF16), jax.ShapeDtypeStruct((8, lanes), jnp.int32)]
    signals, first, second, picks, flip = call(gather_kernel, gathered, 2**26, lists, slots, *arrived)
    relay = flip[:1] == 3
    first_one, second_one = swap(first, "elem", 1), swap(second, "elem", 2)
    sums = jax.ShapeDtypeStruct((length, 2 * lanes), F32)
    near, partner = call(own_kernel, [sums, whole], 2**29, signals, picks, table)
    first_two = swap(jnp.where(relay, first_one, first), "elem", 2)
    second_two = swap(jnp.where(relay, second_one, second), "elem", 1)
    results = call(
        exchange_kernel,
        leaving,
        2**30,
        flip,
        near,
        partner,
        picks,
        first_one,
        first_two,
        second_one,
        second_two,
        table,
        scratch=[pltpu.VMEM((length, 2 * lanes), BF16)],
    )
    out = jax.ShapeDtypeStruct((2, energies, group_rows), BF16)
    return tuple(call(join_kernel, [out, out], 0, *over_energy(*results)))


def any_mesh(g_lesser, g_greater, send_rows, partner_slot):
    piece = lax.axis_index("energy")
    pieces = lax.axis_size("energy")
    _, energies, group_rows = g_lesser.shape
    groups, cap = send_rows.shape[2:]
    width = group_rows // pieces
    lanes = 2 * width
    length = pieces * energies
    packed_shape = jax.ShapeDtypeStruct((pieces, 2, energies, lanes), BF16)
    packed = call(pack_kernel, packed_shape, 0, g_lesser, g_greater)
    own = lax.all_to_all(packed, "energy", split_axis=0, concat_axis=0, tiled=True)
    rows = lax.dynamic_index_in_dim(send_rows[0], piece, 0, keepdims=False).reshape(-1)
    slots = lax.dynamic_slice_in_dim(partner_slot, piece * width, width, 0)
    pick = (jnp.arange(width, dtype=jnp.int32)[:, None] == rows[None, :]).astype(BF16)
    split = own.reshape(pieces, 2, energies, 2, width)
    outgoing = jnp.einsum("pceds,sm->mpced", split, pick, preferred_element_type=F32).astype(BF16)
    incoming = lax.all_to_all(outgoing, "elem", split_axis=0, concat_axis=0, tiled=True)
    table_width = groups * cap
    far = jnp.transpose(incoming, (1, 3, 2, 4, 0)).reshape(length, 4 * table_width)
    index = jnp.concatenate([slots + table_width, slots])
    index = jnp.stack([index, index + 2 * table_width])
    result = call(
        correlate_kernel,
        packed_shape,
        2 * length * length * lanes * 14,
        index,
        own,
        far,
        jnp.asarray(fourier_tables(length)),
    )
    back = lax.all_to_all(result, "energy", split_axis=0, concat_axis=0, tiled=True)
    out = jax.ShapeDtypeStruct((2, energies, group_rows), BF16)
    return tuple(call(unpack_kernel, [out, out], 0, back))


def shards(g_lesser, g_greater, send_rows, partner_slot):
    _, pieces, groups, cap = send_rows.shape
    fits = pieces == 8 and groups == 4 and cap == 32 and partner_slot.shape[0] == 512
    path = four_chips if fits else any_mesh
    return path(g_lesser, g_greater, send_rows, partner_slot)


def solution(mesh):
    in_specs = (
        P(None, "energy", "elem"),
        P(None, "energy", "elem"),
        P("elem", None, None, None),
        P("elem"),
    )
    out_specs = (P(None, "energy", "elem"), P(None, "energy", "elem"))
    return jax.shard_map(shards, mesh=mesh, in_specs=in_specs, out_specs=out_specs, check_vma=False)
```

time: 40.2 us -> 38.7 us (0.963)
  between operations: 3.36 us -> 0.74 us
  starting transfers between devices: 14.4 us -> 15.7 us
  other arithmetic: 1.07 us -> 0.04 us
  Pallas kernels: 3.29 us -> 3.84 us
  local copies, waits for them, and re-layouts: 5.2 us -> 5.65 us
    ppermute x16, starting transfers between devices: 14.4 us -> 15.7 us  [swap(): lax.ppermute(values, axis, [(i, i ^ bit) for i in range(lax.axis_size(axi...]
    reduce_sum x2 -> x0, other arithmetic: 1.03 us -> none  [the longest x1 0.92 us: four_chips(): filled = jnp.sum(send_rows[0], axis=2) > 0]
    another operation x3, local copies, waits for them, and re-layouts: 0.16 us -> 0.84 us  [four_chips(): slots = jnp.tile(partner_slot.reshape(8, lanes // 2), (1, 2))]
    dynamic_slice x1 -> x0, local copies, waits for them, and re-layouts: 0.59 us -> none  [four_chips(): lax.dynamic_index_in_dim(flips, 2 * chip + 1, 0, keepdims=False)]
    pallas_call x4 -> x5, Pallas kernels: 3.29 us -> 3.84 us  [call(): pl.pallas_call(kernel, out_shape=out_shape, scratch_shapes=list(scratch),...]
    unnamed x10 -> x8, local copies, waits for them, and re-layouts: 3.61 us -> 3.97 us
  transfers between devices with their start and end apart: 16 -> 16, of which waited for: 10 -> 9; matrix products, arithmetic and copies ran while one was open for 7% -> 4% of each run, Pallas kernels for 0% -> 1%
where the time goes in v3:
time: 38.7 us; the launch traced here: 38.4 us
  starting transfers between devices  15.7 us (41%)
  waiting for transfers between devices  12.4 us (32%)
  local copies, waits for them, and re-layouts  5.65 us (15%)
  Pallas kernels  3.84 us (10%)
  between operations  0.74 us (2%)
    ppermute x16, starting transfers between devices, swap(): lax.ppermute(values, axis, [(i, i ^ bit) for i in range(lax.axis_size(axi...  15.7 us
    ppermute x16, waiting for transfers between devices, swap(): lax.ppermute(values, axis, [(i, i ^ bit) for i in range(lax.axis_size(axi...  12.4 us
    unnamed x8, local copies, waits for them, and re-layouts  3.97 us
    pallas_call x5, Pallas kernels, call(): pl.pallas_call(kernel, out_shape=out_shape, scratch_shapes=list(scratch),...  3.84 us
    another operation x3, local copies, waits for them, and re-layouts, four_chips(): slots = jnp.tile(partner_slot.reshape(8, lanes // 2), (1, 2))  0.84 us
    another operation x2, local copies, waits for them, and re-layouts, four_chips(): lists = jnp.tile(send_rows[0], (1, 1, 4))  0.83 us
  transfers between devices with their start and end apart: 16, of which 9 were waited for; matrix products, arithmetic and copies ran while one was open for 4% of the time, Pallas kernels for 1%

profile of v3, /device:TPU:0, one launch (start us, length us, event | category | flops | bytes accessed | tf_op | source)
XLA Modules:
  0.0 38.4 jit_solution(10913032139333265628)
XLA Ops:
  0.6 0.9 %copy-done.2 = bf16[2,64,512]{2,1,0:T(8,128)(2,1)S(1)} copy-done((bf16[2,64,512]{2,1,0:T(8,128)(2,1)S(1)}, bf16[2,64,512]{2,1,0:T(8,128)(2,1)}, u32[]{:S(2)}) %copy-start.2) | copy-done | bytes 131096
  1.5 0.9 %copy-done.3 = bf16[2,64,512]{2,1,0:T(8,128)(2,1)S(1)} copy-done((bf16[2,64,512]{2,1,0:T(8,128)(2,1)S(1)}, bf16[2,64,512]{2,1,0:T(8,128)(2,1)}, u32[]{:S(2)}) %copy-start.3) | copy-done | bytes 131096
  2.9 0.5 %collective-permute-start = (bf16[2,2,64,128]{3,2,1,0:T(8,128)(2,1)S(1)}, bf16[2,2,64,128]{3,2,1,0:T(8,128)(2,1)S(1)}, u32[]{:S(2)}, u32[]{:S(2)}) collective-permute-start(bf16[2,2,64,128]{3,2,1,0:T(8,128)(2,1)S(1)} %get-tuple-element.20), channel_id=1, source_target_pairs={{0,4},{4,0},{8,12},{12,8},{16,20},{20,16},{24,28},{28,24},{1,5},{5... | collective-permute-start | bytes 196616 | tf_op jit(solution)/shard_map/ppermute | solution.py:163
  3.4 2.6 %collective-permute-start.2 = (bf16[2,2,64,128]{3,2,1,0:T(8,128)(2,1)S(1)}, bf16[2,2,64,128]{3,2,1,0:T(8,128)(2,1)S(1)}, u32[]{:S(2)}, u32[]{:S(2)}) collective-permute-start(bf16[2,2,64,128]{3,2,1,0:T(8,128)(2,1)S(1)} %get-tuple-element.22), channel_id=1, source_target_pairs={{0,16},{4,20},{8,24},{12,28},{16,0},{20,4},{24,8},{28,12},{1,17},{... | collective-permute-start | bytes 196616 | tf_op jit(solution)/shard_map/ppermute | solution.py:163
  6.0 1.4 %collective-permute-start.4 = (bf16[2,2,64,128]{3,2,1,0:T(8,128)(2,1)S(1)}, bf16[2,2,64,128]{3,2,1,0:T(8,128)(2,1)S(1)}, u32[]{:S(2)}, u32[]{:S(2)}) collective-permute-start(bf16[2,2,64,128]{3,2,1,0:T(8,128)(2,1)S(1)} %get-tuple-element.23), channel_id=1, source_target_pairs={{0,24},{4,28},{8,16},{12,20},{16,8},{20,12},{24,0},{28,4},{1,25},{... | collective-permute-start | bytes 196616 | tf_op jit(solution)/shard_map/ppermute | solution.py:163
  7.7 1.8 %collective-permute-done.2.refs_3_ = bf16[2,2,64,128]{3,2,1,0:T(8,128)(2,1)S(1)} collective-permute-done((bf16[2,2,64,128]{3,2,1,0:T(8,128)(2,1)S(1)}, bf16[2,2,64,128]{3,2,1,0:T(8,128)(2,1)S(1)}, u32[]{:S(2)}, u32[]{:S(2)}) %collective-permute-start.2) | collective-permute-done | bytes 65568 | tf_op jit(solution)/shard_map/ppermute | solution.py:163
  9.4 2.0 %collective-permute-done.4.refs_5_ = bf16[2,2,64,128]{3,2,1,0:T(8,128)(2,1)S(1)} collective-permute-done((bf16[2,2,64,128]{3,2,1,0:T(8,128)(2,1)S(1)}, bf16[2,2,64,128]{3,2,1,0:T(8,128)(2,1)S(1)}, u32[]{:S(2)}, u32[]{:S(2)}) %collective-permute-start.4) | collective-permute-done | bytes 65568 | tf_op jit(solution)/shard_map/ppermute | solution.py:163
  11.5 0.8 %tile.23 = s32[8,64]{1,0:T(8,128)S(1)} reshape(s32[512]{0:T(512)} %param.8) | data formatting | bytes 4096 | tf_op jit(solution)/shard_map/tile | solution.py:296
  12.3 0.7 %tile.21 = s32[8,4,4,32]{3,2,1,0:T(4,128)S(1)} broadcast(s32[8,4,32]{2,1,0:T(4,128)} %bitcast.7), dimensions={0,1,3} | broadcast | bytes 20480 | tf_op jit(solution)/shard_map/tile | solution.py:295
  13.5 1.6 %collective-permute-start.6 = (bf16[256,128]{1,0:T(8,128)(2,1)S(1)}, bf16[256,128]{1,0:T(8,128)(2,1)S(1)}, u32[]{:S(2)}, u32[]{:S(2)}) collective-permute-start(bf16[256,128]{1,0:T(8,128)(2,1)S(1)} %get-tuple-element.29), channel_id=1, source_target_pairs={{0,1},{1,0},{2,3},{3,2},{4,5},{5,4},{6,7},{7,6},{8,9},{9,8},{10,11... | collective-permute-start | bytes 196616 | tf_op jit(solution)/shard_map/ppermute | solution.py:163
  15.1 2.6 %collective-permute-start.8 = (bf16[256,128]{1,0:T(8,128)(2,1)S(1)}, bf16[256,128]{1,0:T(8,128)(2,1)S(1)}, u32[]{:S(2)}, u32[]{:S(2)}) collective-permute-start(bf16[256,128]{1,0:T(8,128)(2,1)S(1)} %get-tuple-element.30), channel_id=1, source_target_pairs={{0,2},{1,3},{2,0},{3,1},{4,6},{5,7},{6,4},{7,5},{8,10},{9,11},{10,... | collective-permute-start | bytes 196616 | tf_op jit(solution)/shard_map/ppermute | solution.py:163
  18.1 3.6 %collective-permute-done.8.second_ref = bf16[256,128]{1,0:T(8,128)(2,1)S(1)} collective-permute-done((bf16[256,128]{1,0:T(8,128)(2,1)S(1)}, bf16[256,128]{1,0:T(8,128)(2,1)S(1)}, u32[]{:S(2)}, u32[]{:S(2)}) %collective-permute-start.8) | collective-permute-done | bytes 65568 | tf_op jit(solution)/shard_map/ppermute | solution.py:163
  21.7 0.5 %collective-permute-start.9 = (bf16[256,128]{1,0:T(8,128)(2,1)S(1)}, bf16[256,128]{1,0:T(8,128)(2,1)S(1)}, u32[]{:S(2)}, u32[]{:S(2)}) collective-permute-start(bf16[256,128]{1,0:T(8,128)(2,1)S(1)} %get-tuple-element.36), channel_id=1, source_target_pairs={{0,1},{1,0},{2,3},{3,2},{4,5},{5,4},{6,7},{7,6},{8,9},{9,8},{10,11... | collective-permute-start | bytes 196616 | tf_op jit(solution)/shard_map/ppermute | solution.py:163
  22.3 2.6 %collective-permute-start.7 = (bf16[256,128]{1,0:T(8,128)(2,1)S(1)}, bf16[256,128]{1,0:T(8,128)(2,1)S(1)}, u32[]{:S(2)}, u32[]{:S(2)}) collective-permute-start(bf16[256,128]{1,0:T(8,128)(2,1)S(1)} %get-tuple-element.37), channel_id=1, source_target_pairs={{0,2},{1,3},{2,0},{3,1},{4,6},{5,7},{6,4},{7,5},{8,10},{9,11},{10,... | collective-permute-start | bytes 196616 | tf_op jit(solution)/shard_map/ppermute | solution.py:163
  24.8 1.6 %copy-done = bf16[4,512,512]{2,1,0:T(8,128)(2,1)S(1)} copy-done((bf16[4,512,512]{2,1,0:T(8,128)(2,1)S(1)}, bf16[4,512,512]{2,1,0:T(8,128)(2,1)}, u32[]{:S(2)}) %copy-start) | copy-done | bytes 2097176
  26.4 0.5 %shard_map.70 = (f32[512,256]{1,0:T(8,128)S(1)}, bf16[512,256]{1,0:T(8,128)(2,1)S(1)}) custom-call(bf16[512,256]{1,0:T(8,128)(2,1)S(1)} %get-tuple-element.25.signals_ref, bf16[3,128,128]{2,1,0:T(8,128)(2,1)S(1)} %get-tuple-element.26.picks_ref, bf16[4,512,512]{2,1,0:T(8,128)(2,1)S(1)} %copy-done), custom_call_target="tpu_custom_call" | custom-call | flops 536870912 | bytes 3244032 | tf_op jit(solution)/shard_map/pallas_call | solution.py:114
  27.4 0.6 %copy-done.1 = bf16[4,512,512]{2,1,0:T(8,128)(2,1)S(1)} copy-done((bf16[4,512,512]{2,1,0:T(8,128)(2,1)S(1)}, bf16[4,512,512]{2,1,0:T(8,128)(2,1)}, u32[]{:S(2)}) %copy-start.1) | copy-done | bytes 2097176
  28.0 1.7 %shard_map.71 = (bf16[2,2,64,128]{3,2,1,0:T(8,128)(2,1)S(1)}, bf16[2,2,64,128]{3,2,1,0:T(8,128)(2,1)S(1)}, bf16[2,64,128]{2,1,0:T(8,128)(2,1)S(1)}, bf16[2,2,64,...) custom-call(s32[8,128]{1,0:T(8,128)S(1)} %get-tuple-element.24.flip_ref, f32[512,256]{1,0:T(8,128)S(1)} %get-tuple-element.27.near_ref, ...), custom_call_target="tpu_custom_call" | custom-call | flops 1073741824 | bytes 3510272 | tf_op jit(solution)/shard_map/pallas_call | solution.py:114
  29.8 0.8 %collective-permute-start.12 = (bf16[2,2,64,128]{3,2,1,0:T(8,128)(2,1)S(1)}, bf16[2,2,64,128]{3,2,1,0:T(8,128)(2,1)S(1)}, u32[]{:S(2)}, u32[]{:S(2)}) collective-permute-start(bf16[2,2,64,128]{3,2,1,0:T(8,128)(2,1)S(1)} %get-tuple-element.34), channel_id=1, source_target_pairs={{0,16},{4,20},{8,24},{12,28},{16,0},{20,4},{24,8},{28,12},{1,17},{... | collective-permute-start | bytes 196616 | tf_op jit(solution)/shard_map/ppermute | solution.py:163
  30.7 2.5 %collective-permute-start.14 = (bf16[2,2,64,128]{3,2,1,0:T(8,128)(2,1)S(1)}, bf16[2,2,64,128]{3,2,1,0:T(8,128)(2,1)S(1)}, u32[]{:S(2)}, u32[]{:S(2)}) collective-permute-start(bf16[2,2,64,128]{3,2,1,0:T(8,128)(2,1)S(1)} %get-tuple-element.35), channel_id=1, source_target_pairs={{0,24},{4,28},{8,16},{12,20},{16,8},{20,12},{24,0},{28,4},{1,25},{... | collective-permute-start | bytes 196616 | tf_op jit(solution)/shard_map/ppermute | solution.py:163
  33.5 0.9 %collective-permute-done.12.refs_3_ = bf16[2,2,64,128]{3,2,1,0:T(8,128)(2,1)S(1)} collective-permute-done((bf16[2,2,64,128]{3,2,1,0:T(8,128)(2,1)S(1)}, bf16[2,2,64,128]{3,2,1,0:T(8,128)(2,1)S(1)}, u32[]{:S(2)}, u32[]{:S(2)}) %collective-permute-start.12) | collective-permute-done | bytes 65568 | tf_op jit(solution)/shard_map/ppermute | solution.py:163
  34.4 1.7 %collective-permute-done.14.refs_5_ = bf16[2,2,64,128]{3,2,1,0:T(8,128)(2,1)S(1)} collective-permute-done((bf16[2,2,64,128]{3,2,1,0:T(8,128)(2,1)S(1)}, bf16[2,2,64,128]{3,2,1,0:T(8,128)(2,1)S(1)}, u32[]{:S(2)}, u32[]{:S(2)}) %collective-permute-start.14) | collective-permute-done | bytes 65568 | tf_op jit(solution)/shard_map/ppermute | solution.py:163
  36.1 1.5 %collective-permute-done.11.refs_2_ = bf16[2,2,64,128]{3,2,1,0:T(8,128)(2,1)S(1)} collective-permute-done((bf16[2,2,64,128]{3,2,1,0:T(8,128)(2,1)S(1)}, bf16[2,2,64,128]{3,2,1,0:T(8,128)(2,1)S(1)}, u32[]{:S(2)}, u32[]{:S(2)}) %collective-permute-start.11) | collective-permute-done | bytes 65568 | tf_op jit(solution)/shard_map/ppermute | solution.py:163
  37.5 0.8 %shard_map.72 = (bf16[2,64,512]{2,1,0:T(8,128)(2,1)}, bf16[2,64,512]{2,1,0:T(8,128)(2,1)}) custom-call(bf16[2,64,128]{2,1,0:T(8,128)(2,1)S(1)} %get-tuple-element.31.refs_0_, bf16[2,2,64,128]{3,2,1,0:T(8,128)(2,1)S(1)} %collective-permute-done.10.refs_1_, bf16[2,2,64,128]{3,2,1,0:T(8,128)(2,1)S(1)} %collective-permute-done.11.refs_2_, ...), custom_call_target="tpu_custom_call" | custom-call | bytes 688128 | tf_op jit(solution)/shard_map/pallas_call | solution.py:114
  (32 shorter events, 2.4 us)
Async XLA Ops:
  0.6 0.9 %copy-start.2 = (bf16[2,64,512]{2,1,0:T(8,128)(2,1)S(1)}, bf16[2,64,512]{2,1,0:T(8,128)(2,1)}, u32[]{:S(2)}) copy-start(bf16[2,64,512]{2,1,0:T(8,128)(2,1)} %lesser_ref.1) | copy-start | bytes 393220
  1.5 0.9 %copy-start.3 = (bf16[2,64,512]{2,1,0:T(8,128)(2,1)S(1)}, bf16[2,64,512]{2,1,0:T(8,128)(2,1)}, u32[]{:S(2)}) copy-start(bf16[2,64,512]{2,1,0:T(8,128)(2,1)} %greater_ref.1) | copy-start | bytes 393220
  2.9 4.5 %collective-permute-start = (bf16[2,2,64,128]{3,2,1,0:T(8,128)(2,1)S(1)}, bf16[2,2,64,128]{3,2,1,0:T(8,128)(2,1)S(1)}, u32[]{:S(2)}, u32[]{:S(2)}) collective-permute-start(bf16[2,2,64,128]{3,2,1,0:T(8,128)(2,1)S(1)} %get-tuple-element.20), channel_id=1, source_target_pairs={{0,4},{4,0},{8,12},{12,8},{16,20},{20,16},{24,28},{28,24},{1,5},{5... | collective-permute-start | bytes 196616 | tf_op jit(solution)/shard_map/ppermute | solution.py:163
  3.4 6.0 %collective-permute-start.2 = (bf16[2,2,64,128]{3,2,1,0:T(8,128)(2,1)S(1)}, bf16[2,2,64,128]{3,2,1,0:T(8,128)(2,1)S(1)}, u32[]{:S(2)}, u32[]{:S(2)}) collective-permute-start(bf16[2,2,64,128]{3,2,1,0:T(8,128)(2,1)S(1)} %get-tuple-element.22), channel_id=1, source_target_pairs={{0,16},{4,20},{8,24},{12,28},{16,0},{20,4},{24,8},{28,12},{1,17},{... | collective-permute-start | bytes 196616 | tf_op jit(solution)/shard_map/ppermute | solution.py:163
  6.0 5.4 %collective-permute-start.4 = (bf16[2,2,64,128]{3,2,1,0:T(8,128)(2,1)S(1)}, bf16[2,2,64,128]{3,2,1,0:T(8,128)(2,1)S(1)}, u32[]{:S(2)}, u32[]{:S(2)}) collective-permute-start(bf16[2,2,64,128]{3,2,1,0:T(8,128)(2,1)S(1)} %get-tuple-element.23), channel_id=1, source_target_pairs={{0,24},{4,28},{8,16},{12,20},{16,8},{20,12},{24,0},{28,4},{1,25},{... | collective-permute-start | bytes 196616 | tf_op jit(solution)/shard_map/ppermute | solution.py:163
  7.5 5.7 %collective-permute-start.1 = (bf16[2,2,64,128]{3,2,1,0:T(8,128)(2,1)S(1)}, bf16[2,2,64,128]{3,2,1,0:T(8,128)(2,1)S(1)}, u32[]{:S(2)}, u32[]{:S(2)}) collective-permute-start(bf16[2,2,64,128]{3,2,1,0:T(8,128)(2,1)S(1)} %pad_maximum_fusion), channel_id=1, source_target_pairs={{0,8},{4,12},{8,0},{12,4},{16,24},{20,28},{24,16},{28,20},{1,9},{5... | collective-permute-start | bytes 196616 | tf_op jit(solution)/shard_map/ppermute | solution.py:163
  9.4 3.7 %collective-permute-start.3 = (bf16[2,2,64,128]{3,2,1,0:T(8,128)(2,1)S(1)}, bf16[2,2,64,128]{3,2,1,0:T(8,128)(2,1)S(1)}, u32[]{:S(2)}, u32[]{:S(2)}) collective-permute-start(bf16[2,2,64,128]{3,2,1,0:T(8,128)(2,1)S(1)} %collective-permute-done.2.refs_3_), channel_id=1, source_target_pairs={{0,4},{4,0},{8,12},{12,8},{16,20},{20,16},{24,28},{28,24},{1,5},{5... | collective-permute-start | bytes 196616 | tf_op jit(solution)/shard_map/ppermute | solution.py:163
  11.5 1.7 %collective-permute-start.5 = (bf16[2,2,64,128]{3,2,1,0:T(8,128)(2,1)S(1)}, bf16[2,2,64,128]{3,2,1,0:T(8,128)(2,1)S(1)}, u32[]{:S(2)}, u32[]{:S(2)}) collective-permute-start(bf16[2,2,64,128]{3,2,1,0:T(8,128)(2,1)S(1)} %collective-permute-done.4.refs_5_), channel_id=1, source_target_pairs={{0,4},{4,0},{8,12},{12,8},{16,20},{20,16},{24,28},{28,24},{1,5},{5... | collective-permute-start | bytes 196616 | tf_op jit(solution)/shard_map/ppermute | solution.py:163
  13.5 4.6 %collective-permute-start.6 = (bf16[256,128]{1,0:T(8,128)(2,1)S(1)}, bf16[256,128]{1,0:T(8,128)(2,1)S(1)}, u32[]{:S(2)}, u32[]{:S(2)}) collective-permute-start(bf16[256,128]{1,0:T(8,128)(2,1)S(1)} %get-tuple-element.29), channel_id=1, source_target_pairs={{0,1},{1,0},{2,3},{3,2},{4,5},{5,4},{6,7},{7,6},{8,9},{9,8},{10,11... | collective-permute-start | bytes 196616 | tf_op jit(solution)/shard_map/ppermute | solution.py:163
  15.1 6.6 %collective-permute-start.8 = (bf16[256,128]{1,0:T(8,128)(2,1)S(1)}, bf16[256,128]{1,0:T(8,128)(2,1)S(1)}, u32[]{:S(2)}, u32[]{:S(2)}) collective-permute-start(bf16[256,128]{1,0:T(8,128)(2,1)S(1)} %get-tuple-element.30), channel_id=1, source_target_pairs={{0,2},{1,3},{2,0},{3,1},{4,6},{5,7},{6,4},{7,5},{8,10},{9,11},{10,... | collective-permute-start | bytes 196616 | tf_op jit(solution)/shard_map/ppermute | solution.py:163
  21.7 5.3 %collective-permute-start.9 = (bf16[256,128]{1,0:T(8,128)(2,1)S(1)}, bf16[256,128]{1,0:T(8,128)(2,1)S(1)}, u32[]{:S(2)}, u32[]{:S(2)}) collective-permute-start(bf16[256,128]{1,0:T(8,128)(2,1)S(1)} %get-tuple-element.36), channel_id=1, source_target_pairs={{0,1},{1,0},{2,3},{3,2},{4,5},{5,4},{6,7},{7,6},{8,9},{9,8},{10,11... | collective-permute-start | bytes 196616 | tf_op jit(solution)/shard_map/ppermute | solution.py:163
  22.3 5.2 %collective-permute-start.7 = (bf16[256,128]{1,0:T(8,128)(2,1)S(1)}, bf16[256,128]{1,0:T(8,128)(2,1)S(1)}, u32[]{:S(2)}, u32[]{:S(2)}) collective-permute-start(bf16[256,128]{1,0:T(8,128)(2,1)S(1)} %get-tuple-element.37), channel_id=1, source_target_pairs={{0,2},{1,3},{2,0},{3,1},{4,6},{5,7},{6,4},{7,5},{8,10},{9,11},{10,... | collective-permute-start | bytes 196616 | tf_op jit(solution)/shard_map/ppermute | solution.py:163
  24.8 1.6 %copy-start = (bf16[4,512,512]{2,1,0:T(8,128)(2,1)S(1)}, bf16[4,512,512]{2,1,0:T(8,128)(2,1)}, u32[]{:S(2)}) copy-start(bf16[4,512,512]{2,1,0:T(8,128)(2,1)} %constant.4.clone.table_ref) | copy-start | bytes 6291460
  26.4 1.6 %copy-start.1 = (bf16[4,512,512]{2,1,0:T(8,128)(2,1)S(1)}, bf16[4,512,512]{2,1,0:T(8,128)(2,1)}, u32[]{:S(2)}) copy-start(bf16[4,512,512]{2,1,0:T(8,128)(2,1)} %constant.4.clone.table_ref) | copy-start | bytes 6291460
  29.8 3.4 %collective-permute-start.10 = (bf16[2,2,64,128]{3,2,1,0:T(8,128)(2,1)S(1)}, bf16[2,2,64,128]{3,2,1,0:T(8,128)(2,1)S(1)}, u32[]{:S(2)}, u32[]{:S(2)}) collective-permute-start(bf16[2,2,64,128]{3,2,1,0:T(8,128)(2,1)S(1)} %get-tuple-element.32), channel_id=1, source_target_pairs={{0,4},{4,0},{8,12},{12,8},{16,20},{20,16},{24,28},{28,24},{1,5},{5... | collective-permute-start | bytes 196616 | tf_op jit(solution)/shard_map/ppermute | solution.py:163
  29.8 4.5 %collective-permute-start.12 = (bf16[2,2,64,128]{3,2,1,0:T(8,128)(2,1)S(1)}, bf16[2,2,64,128]{3,2,1,0:T(8,128)(2,1)S(1)}, u32[]{:S(2)}, u32[]{:S(2)}) collective-permute-start(bf16[2,2,64,128]{3,2,1,0:T(8,128)(2,1)S(1)} %get-tuple-element.34), channel_id=1, source_target_pairs={{0,16},{4,20},{8,24},{12,28},{16,0},{20,4},{24,8},{28,12},{1,17},{... | collective-permute-start | bytes 196616 | tf_op jit(solution)/shard_map/ppermute | solution.py:163
  30.7 5.4 %collective-permute-start.14 = (bf16[2,2,64,128]{3,2,1,0:T(8,128)(2,1)S(1)}, bf16[2,2,64,128]{3,2,1,0:T(8,128)(2,1)S(1)}, u32[]{:S(2)}, u32[]{:S(2)}) collective-permute-start(bf16[2,2,64,128]{3,2,1,0:T(8,128)(2,1)S(1)} %get-tuple-element.35), channel_id=1, source_target_pairs={{0,24},{4,28},{8,16},{12,20},{16,8},{20,12},{24,0},{28,4},{1,25},{... | collective-permute-start | bytes 196616 | tf_op jit(solution)/shard_map/ppermute | solution.py:163
  33.2 4.3 %collective-permute-start.11 = (bf16[2,2,64,128]{3,2,1,0:T(8,128)(2,1)S(1)}, bf16[2,2,64,128]{3,2,1,0:T(8,128)(2,1)S(1)}, u32[]{:S(2)}, u32[]{:S(2)}) collective-permute-start(bf16[2,2,64,128]{3,2,1,0:T(8,128)(2,1)S(1)} %pad_maximum_fusion.1), channel_id=1, source_target_pairs={{0,8},{4,12},{8,0},{12,4},{16,24},{20,28},{24,16},{28,20},{1,9},{5... | collective-permute-start | bytes 196616 | tf_op jit(solution)/shard_map/ppermute | solution.py:163
  34.4 3.2 %collective-permute-start.13 = (bf16[2,2,64,128]{3,2,1,0:T(8,128)(2,1)S(1)}, bf16[2,2,64,128]{3,2,1,0:T(8,128)(2,1)S(1)}, u32[]{:S(2)}, u32[]{:S(2)}) collective-permute-start(bf16[2,2,64,128]{3,2,1,0:T(8,128)(2,1)S(1)} %collective-permute-done.12.refs_3_), channel_id=1, source_target_pairs={{0,4},{4,0},{8,12},{12,8},{16,20},{20,16},{24,28},{28,24},{1,5},{5... | collective-permute-start | bytes 196616 | tf_op jit(solution)/shard_map/ppermute | solution.py:163
  36.1 1.5 %collective-permute-start.15 = (bf16[2,2,64,128]{3,2,1,0:T(8,128)(2,1)S(1)}, bf16[2,2,64,128]{3,2,1,0:T(8,128)(2,1)S(1)}, u32[]{:S(2)}, u32[]{:S(2)}) collective-permute-start(bf16[2,2,64,128]{3,2,1,0:T(8,128)(2,1)S(1)} %collective-permute-done.14.refs_5_), channel_id=1, source_target_pairs={{0,4},{4,0},{8,12},{12,8},{16,20},{20,16},{24,28},{28,24},{1,5},{5... | collective-permute-start | bytes 196616 | tf_op jit(solution)/shard_map/ppermute | solution.py:163

commit v4 on v3

--- a/solution.py
+++ b/solution.py
@@ -111,6 +111,8 @@
     outs = out_shape if isinstance(out_shape, (list, tuple)) else [out_shape]
     moved = sum(math.prod(v.shape) * v.dtype.itemsize for v in [*args, *outs])
     more = {"in_specs": [pl.BlockSpec(memory_space=pltpu.HBM)] * len(args)} if in_hbm else {}
+    if in_hbm:
+        args = [pltpu.with_memory_space_constraint(v, pltpu.HBM) for v in args]
     return pl.pallas_call(
         kernel,
         out_shape=out_shape,
@@ -130,9 +132,16 @@
     return pl.ds(pl.multiple_of(chip * 2 * width, 2 * width), 2 * width)
 
 
-def split_kernel(lesser_ref, greater_ref, *refs):
-    (diagonal_ref, beside_ref, keep_ref, give_ref, own_ref), (held, sems) = refs[:5], refs[5:]
+def split_kernel(lists_ref, slots_ref, lesser_ref, greater_ref, *refs):
+    (diagonal_ref, beside_ref, keep_ref, give_ref, own_ref, picks_ref, flip_ref) = refs[:7]
+    held, lists, slots, sems, index_sems = refs[7:]
     chip, core = place()
+    index_copies = [
+        pltpu.make_async_copy(lists_ref.at[0, 2 * chip + core], lists, index_sems.at[0]),
+        pltpu.make_async_copy(slots_ref, slots, index_sems.at[1]),
+    ]
+    for copy in index_copies:
+        copy.start()
     width = own_ref.shape[-1] // 2
     copies = [
         [
@@ -144,6 +153,9 @@
     for j in (3, 2, 1, 0):
         for copy in copies[j]:
             copy.start()
+    for copy in index_copies:
+        copy.wait()
+    index_tables(lists[...], slots[pl.ds(chip, 1), :], picks_ref, flip_ref)
     for j in (3, 2, 1, 0):
         for copy in copies[j]:
             copy.wait()
@@ -168,11 +180,11 @@
     beside = swap(beside, "energy", 4)
     got = swap(give, "energy", 1)
     across = swap(jnp.stack([keep, got[0]]), "energy", 2)
-    return own, got, across, beside, swap(beside, "energy", 1), diagonal, swap(diagonal, "energy", 1)
+    return own, got, diagonal, swap(diagonal, "energy", 1), beside, swap(beside, "energy", 1), across
 
 
 def blocks_of(refs, core):
-    own_ref, got_ref, across_ref, beside_ref, beside_other_ref, diagonal_ref, diagonal_other_ref = refs
+    own_ref, got_ref, diagonal_ref, diagonal_other_ref, beside_ref, beside_other_ref, across_ref = refs
     return [
         (lambda: own_ref[...], lambda: got_ref[1]),
         (lambda: across_ref[0], lambda: across_ref[1]),
@@ -189,43 +201,52 @@
     return pl.ds(pl.multiple_of(device * energies, energies), energies)
 
 
-def gather_kernel(lists_ref, slots_ref, *refs):
-    in_refs, (signals_ref, first_ref, second_ref, picks_ref, flip_ref) = refs[:7], refs[7:]
+def repeat(values, index_row):
+    return dot(values.astype(F32).astype(BF16), one_hot(index_row, values.shape[-1])).astype(jnp.int32)
+
+
+def relay_kernel(flip_ref, passed_ref, own_ref, out_ref):
+    out_ref[...] = jnp.where(flip_ref[0:1, :] == 3, passed_ref[...], own_ref[...])
+
+
+def index_tables(lists, slots, picks_ref, flip_ref):
+    _, core = place()
+    group = lax.axis_index("elem")
+    lanes = picks_ref.shape[-1]
+    width, cap = lanes // 2, lanes // 4
+    lane = lane_row(lanes)
+    lists = repeat(lists, lane % cap)
+    ids = lax.broadcasted_iota(jnp.int32, lists.shape, 0)
+    greater = jnp.where(lane // cap % 2 == 1, width, 0)
+    near_rows = jnp.sum(jnp.where(ids == group, lists, 0), axis=0, keepdims=True) + greater
+    far_rows = jnp.sum(jnp.where(ids == group, 0, lists), axis=0, keepdims=True) + greater
+    filled = jnp.max(lists, axis=1, keepdims=True) > 0
+    flip = jnp.sum(jnp.where(filled, ids ^ group, 0), axis=0, keepdims=True)
+    flip_ref[...] = jnp.broadcast_to(flip[:, :1], flip_ref.shape)
+    slots = repeat(slots, core * width + lane % width)
+    source = slots // cap
+    spot = slots - source * cap + jnp.where(lane < width, cap, 0)
+    near = one_hot(jnp.where(lane < 2 * cap, near_rows, -1), lanes)
+    picks_ref[0] = dot(near, one_hot(jnp.where(source == group, spot, -1), lanes)).astype(BF16)
+    for part in range(2):
+        picks_ref[1 + part] = one_hot(jnp.where(source == group, -1, spot + 2 * cap * part), lanes)
+        picks_ref[3 + part] = one_hot(jnp.where(lane // (2 * cap) == part, far_rows, -1), lanes)
+
+
+def gather_kernel(picks_ref, *refs):
+    in_refs, (signals_ref, first_ref, second_ref) = refs[:7], refs[7:]
     chip, core = place()
-    group = lax.axis_index("elem")
     energies, lanes = in_refs[0].shape[1:]
-    width, cap = lanes // 2, lanes // 4
     for j, pair in enumerate(blocks_of(in_refs, core)):
         for which, block in enumerate(pair):
             values = block()
             rows = energies_of(2 * (chip ^ j) + (core if which == 0 else 1 - core), energies)
             for part in range(2):
                 signals_ref[rows, part * lanes : (part + 1) * lanes] = values[part]
-    piece = 2 * chip + core
-    lane = lane_row(lanes)
-    lists = lists_ref[piece]
-    ids = lax.broadcasted_iota(jnp.int32, lists.shape, 0)
-    greater = jnp.where(lane // cap % 2 == 1, width, 0)
-    near_rows = jnp.sum(jnp.where(ids == group, lists, 0), axis=0, keepdims=True) + greater
-    far_rows = jnp.sum(jnp.where(ids == group, 0, lists), axis=0, keepdims=True) + greater
-    filled = jnp.max(lists, axis=1, keepdims=True) > 0
-    flip = jnp.sum(jnp.where(filled, ids ^ group, 0), axis=0, keepdims=True)
-    flip_ref[...] = jnp.broadcast_to(flip, flip_ref.shape)
-    total = None
-    for part in range(2):
-        pick = one_hot(jnp.where(lane // (2 * cap) == part, far_rows, -1), lanes)
-        picked = dot(signals_ref[:, part * lanes : (part + 1) * lanes], pick)
-        total = picked if total is None else total + picked
     half = first_ref.shape[0]
-    first_ref[...] = total[:half].astype(BF16)
-    second_ref[...] = total[half:].astype(BF16)
-    slots = slots_ref[pl.ds(piece, 1), :]
-    source = slots // cap
-    spot = slots - source * cap + jnp.where(lane < width, cap, 0)
-    near = one_hot(jnp.where(lane < 2 * cap, near_rows, -1), lanes)
-    picks_ref[0] = dot(near, one_hot(jnp.where(source == group, spot, -1), lanes)).astype(BF16)
-    for part in range(2):
-        picks_ref[1 + part] = one_hot(jnp.where(source == group, -1, spot + 2 * cap * part), lanes)
+    for i, ref in enumerate((first_ref, second_ref)):
+        rows = slice(i * half, (i + 1) * half)
+        ref[...] = (dot(signals_ref[rows, :lanes], picks_ref[3]) + dot(signals_ref[rows, lanes:], picks_ref[4])).astype(BF16)
 
 
 def own_kernel(signals_ref, picks_ref, table_ref, near_ref, partner_ref):
@@ -292,21 +313,27 @@
     leaving = [pair, pair, block, pair, block]
     half = jax.ShapeDtypeStruct((length // 2, lanes), BF16)
     whole = jax.ShapeDtypeStruct((length, 2 * lanes), BF16)
-    lists = jnp.tile(send_rows[0], (1, 1, 4))
-    slots = jnp.tile(partner_slot.reshape(8, lanes // 2), (1, 2))
+    slots = partner_slot.reshape(4, lanes)
     table = jnp.asarray(fourier_tables(length))
 
-    scratch = [pltpu.VMEM((4, 2, 2, energies, lanes), BF16), pltpu.SemaphoreType.DMA((4, 2))]
-    packed = call(split_kernel, leaving, 0, g_lesser, g_greater, scratch=scratch, in_hbm=True)
+    scratch = [
+        pltpu.VMEM((4, 2, 2, energies, lanes), BF16),
+        pltpu.VMEM(send_rows.shape[2:], jnp.int32),
+        pltpu.VMEM(slots.shape, jnp.int32),
+        pltpu.SemaphoreType.DMA((4, 2)),
+        pltpu.SemaphoreType.DMA((2,)),
+    ]
+    tables = [jax.ShapeDtypeStruct((5, lanes, lanes), BF16), jax.ShapeDtypeStruct((8, lanes), jnp.int32)]
+    *packed, picks, flip = call(
+        split_kernel, leaving + tables, 2**24, send_rows, slots, g_lesser, g_greater, scratch=scratch, in_hbm=True
+    )
     arrived = over_energy(*packed)
-    gathered = [whole, half, half, jax.ShapeDtypeStruct((3, lanes, lanes), BF16), jax.ShapeDtypeStruct((8, lanes), jnp.int32)]
-    signals, first, second, picks, flip = call(gather_kernel, gathered, 2**26, lists, slots, *arrived)
-    relay = flip[:1] == 3
-    first_one, second_one = swap(first, "elem", 1), swap(second, "elem", 2)
+    signals, first, second = call(gather_kernel, [whole, half, half], 2**26, picks, *arrived)
+    second_one, first_one = swap(second, "elem", 2), swap(first, "elem", 1)
     sums = jax.ShapeDtypeStruct((length, 2 * lanes), F32)
     near, partner = call(own_kernel, [sums, whole], 2**29, signals, picks, table)
-    first_two = swap(jnp.where(relay, first_one, first), "elem", 2)
-    second_two = swap(jnp.where(relay, second_one, second), "elem", 1)
+    first_two = swap(call(relay_kernel, half, 0, flip, first_one, first), "elem", 2)
+    second_two = swap(call(relay_kernel, half, 0, flip, second_one, second), "elem", 1)
     results = call(
         exchange_kernel,
         leaving,

time: 38.7 us -> 36.3 us (0.938)
  local copies, waits for them, and re-layouts: 5.65 us -> 1.6 us
  Pallas kernels: 3.84 us -> 4.93 us
  starting transfers between devices: 15.7 us -> 16.5 us
    unnamed x8 -> x4, local copies, waits for them, and re-layouts: 3.97 us -> 1.59 us
    another operation x5 -> x0, local copies, waits for them, and re-layouts: 1.67 us -> none  [the longest x3 0.84 us: four_chips(): slots = jnp.tile(partner_slot.reshape(8, lanes // 2), (1, 2))]
    pallas_call x5 -> x7, Pallas kernels: 3.84 us -> 4.93 us  [call(): pl.pallas_call(kernel, out_shape=out_shape, scratch_shapes=list(scratch),...]
    ppermute x16, starting transfers between devices: 15.7 us -> 16.5 us  [swap(): lax.ppermute(values, axis, [(i, i ^ bit) for i in range(lax.axis_size(axi...]
  transfers between devices with their start and end apart: 16 -> 16, of which waited for: 9 -> 11; matrix products, arithmetic and copies ran while one was open for 4% -> 0% of each run, Pallas kernels for 1% -> 1%
where the time goes in v4:
time: 36.3 us; the launch traced here: 36 us
  starting transfers between devices  16.5 us (45%)
  waiting for transfers between devices  12.3 us (34%)
  Pallas kernels  4.93 us (14%)
  local copies, waits for them, and re-layouts  1.6 us (4%)
  between operations  0.71 us (2%)
    ppermute x16, starting transfers between devices, swap(): lax.ppermute(values, axis, [(i, i ^ bit) for i in range(lax.axis_size(axi...  16.5 us
    ppermute x16, waiting for transfers between devices, swap(): lax.ppermute(values, axis, [(i, i ^ bit) for i in range(lax.axis_size(axi...  12.3 us
    pallas_call x7, Pallas kernels, call(): pl.pallas_call(kernel, out_shape=out_shape, scratch_shapes=list(scratch),...  4.93 us
    unnamed x4, local copies, waits for them, and re-layouts  1.59 us
  transfers between devices with their start and end apart: 16, of which 11 were waited for; matrix products, arithmetic and copies ran while one was open for 0% of the time, Pallas kernels for 1%

profile of v4, /device:TPU:0, one launch (start us, length us, event | category | flops | bytes accessed | tf_op | source)
XLA Modules:
  0.0 36.0 jit_solution(17724798450777265806)
XLA Ops:
  0.6 1.6 %shard_map.68 = (bf16[2,2,64,128]{3,2,1,0:T(8,128)(2,1)S(1)}, bf16[2,2,64,128]{3,2,1,0:T(8,128)(2,1)S(1)}, bf16[2,64,128]{2,1,0:T(8,128)(2,1)S(1)}, bf16[2,2,64,...) custom-call(s32[1,8,4,32]{3,2,1,0:T(4,128)} %lists_ref.1, ...), custom_call_target="tpu_custom_call" | custom-call | flops 16777216 | bytes 698368 | tf_op jit(solution)/shard_map/pallas_call | solution.py:116
  2.2 0.5 %collective-permute-start = (bf16[2,2,64,128]{3,2,1,0:T(8,128)(2,1)S(1)}, bf16[2,2,64,128]{3,2,1,0:T(8,128)(2,1)S(1)}, u32[]{:S(2)}, u32[]{:S(2)}) collective-permute-start(bf16[2,2,64,128]{3,2,1,0:T(8,128)(2,1)S(1)} %get-tuple-element.22), channel_id=1, source_target_pairs={{0,4},{4,0},{8,12},{12,8},{16,20},{20,16},{24,28},{28,24},{1,5},{5... | collective-permute-start | bytes 196616 | tf_op jit(solution)/shard_map/ppermute | solution.py:175
  2.7 3.5 %collective-permute-start.1 = (bf16[2,2,64,128]{3,2,1,0:T(8,128)(2,1)S(1)}, bf16[2,2,64,128]{3,2,1,0:T(8,128)(2,1)S(1)}, u32[]{:S(2)}, u32[]{:S(2)}) collective-permute-start(bf16[2,2,64,128]{3,2,1,0:T(8,128)(2,1)S(1)} %get-tuple-element.23), channel_id=1, source_target_pairs={{0,24},{4,28},{8,16},{12,20},{16,8},{20,12},{24,0},{28,4},{1,25},{... | collective-permute-start | bytes 196616 | tf_op jit(solution)/shard_map/ppermute | solution.py:175
  6.3 0.5 %collective-permute-start.3 = (bf16[2,2,64,128]{3,2,1,0:T(8,128)(2,1)S(1)}, bf16[2,2,64,128]{3,2,1,0:T(8,128)(2,1)S(1)}, u32[]{:S(2)}, u32[]{:S(2)}) collective-permute-start(bf16[2,2,64,128]{3,2,1,0:T(8,128)(2,1)S(1)} %get-tuple-element.24), channel_id=1, source_target_pairs={{0,16},{4,20},{8,24},{12,28},{16,0},{20,4},{24,8},{28,12},{1,17},{... | collective-permute-start | bytes 196616 | tf_op jit(solution)/shard_map/ppermute | solution.py:175
  7.0 2.0 %collective-permute-done.1.refs_2_ = bf16[2,2,64,128]{3,2,1,0:T(8,128)(2,1)S(1)} collective-permute-done((bf16[2,2,64,128]{3,2,1,0:T(8,128)(2,1)S(1)}, bf16[2,2,64,128]{3,2,1,0:T(8,128)(2,1)S(1)}, u32[]{:S(2)}, u32[]{:S(2)}) %collective-permute-start.1) | collective-permute-done | bytes 65568 | tf_op jit(solution)/shard_map/ppermute | solution.py:175
  9.0 1.6 %collective-permute-done.3.refs_4_ = bf16[2,2,64,128]{3,2,1,0:T(8,128)(2,1)S(1)} collective-permute-done((bf16[2,2,64,128]{3,2,1,0:T(8,128)(2,1)S(1)}, bf16[2,2,64,128]{3,2,1,0:T(8,128)(2,1)S(1)}, u32[]{:S(2)}, u32[]{:S(2)}) %collective-permute-start.3) | collective-permute-done | bytes 65568 | tf_op jit(solution)/shard_map/ppermute | solution.py:175
  10.5 0.6 %collective-permute-done.5.refs_6_ = bf16[2,2,64,128]{3,2,1,0:T(8,128)(2,1)S(1)} collective-permute-done((bf16[2,2,64,128]{3,2,1,0:T(8,128)(2,1)S(1)}, bf16[2,2,64,128]{3,2,1,0:T(8,128)(2,1)S(1)}, u32[]{:S(2)}, u32[]{:S(2)}) %collective-permute-start.5) | collective-permute-done | bytes 65568 | tf_op jit(solution)/shard_map/ppermute | solution.py:175
  11.1 0.7 %collective-permute-done.4.refs_5_ = bf16[2,2,64,128]{3,2,1,0:T(8,128)(2,1)S(1)} collective-permute-done((bf16[2,2,64,128]{3,2,1,0:T(8,128)(2,1)S(1)}, bf16[2,2,64,128]{3,2,1,0:T(8,128)(2,1)S(1)}, u32[]{:S(2)}, u32[]{:S(2)}) %collective-permute-start.4) | collective-permute-done | bytes 65568 | tf_op jit(solution)/shard_map/ppermute | solution.py:175
  12.0 1.7 %collective-permute-start.6 = (bf16[256,128]{1,0:T(8,128)(2,1)S(1)}, bf16[256,128]{1,0:T(8,128)(2,1)S(1)}, u32[]{:S(2)}, u32[]{:S(2)}) collective-permute-start(bf16[256,128]{1,0:T(8,128)(2,1)S(1)} %get-tuple-element.29.own_ref), channel_id=1, source_target_pairs={{0,1},{1,0},{2,3},{3,2},{4,5},{5,4},{6,7},{7,6},{8,9},{9,8},{10,11... | collective-permute-start | bytes 196616 | tf_op jit(solution)/shard_map/ppermute | solution.py:175
  13.7 2.6 %collective-permute-start.8 = (bf16[256,128]{1,0:T(8,128)(2,1)S(1)}, bf16[256,128]{1,0:T(8,128)(2,1)S(1)}, u32[]{:S(2)}, u32[]{:S(2)}) collective-permute-start(bf16[256,128]{1,0:T(8,128)(2,1)S(1)} %get-tuple-element.30.own_ref), channel_id=1, source_target_pairs={{0,2},{1,3},{2,0},{3,1},{4,6},{5,7},{6,4},{7,5},{8,10},{9,11},{10,... | collective-permute-start | bytes 196616 | tf_op jit(solution)/shard_map/ppermute | solution.py:175
  16.4 3.3 %collective-permute-start.7 = (bf16[256,128]{1,0:T(8,128)(2,1)S(1)}, bf16[256,128]{1,0:T(8,128)(2,1)S(1)}, u32[]{:S(2)}, u32[]{:S(2)}) collective-permute-start(bf16[256,128]{1,0:T(8,128)(2,1)S(1)} %shard_map.71), channel_id=1, source_target_pairs={{0,2},{1,3},{2,0},{3,1},{4,6},{5,7},{6,4},{7,5},{8,10},{9,11},{10,... | collective-permute-start | bytes 196616 | tf_op jit(solution)/shard_map/ppermute | solution.py:175
  19.7 1.3 %collective-permute-done.8.passed_ref.second_ref = bf16[256,128]{1,0:T(8,128)(2,1)S(1)} collective-permute-done((bf16[256,128]{1,0:T(8,128)(2,1)S(1)}, bf16[256,128]{1,0:T(8,128)(2,1)S(1)}, u32[]{:S(2)}, u32[]{:S(2)}) %collective-permute-start.8) | collective-permute-done | bytes 65568 | tf_op jit(solution)/shard_map/ppermute | solution.py:175
  21.5 1.6 %copy-done = bf16[4,512,512]{2,1,0:T(8,128)(2,1)S(1)} copy-done((bf16[4,512,512]{2,1,0:T(8,128)(2,1)S(1)}, bf16[4,512,512]{2,1,0:T(8,128)(2,1)}, u32[]{:S(2)}) %copy-start) | copy-done | bytes 2097176
  23.1 0.5 %shard_map.70 = (f32[512,256]{1,0:T(8,128)S(1)}, bf16[512,256]{1,0:T(8,128)(2,1)S(1)}) custom-call(bf16[512,256]{1,0:T(8,128)(2,1)S(1)} %get-tuple-element.26.signals_ref, bf16[5,128,128]{2,1,0:T(8,128)(2,1)S(1)} %get-tuple-element.20.picks_ref, bf16[4,512,512]{2,1,0:T(8,128)(2,1)S(1)} %copy-done), custom_call_target="tpu_custom_call" | custom-call | flops 536870912 | bytes 3309568 | tf_op jit(solution)/shard_map/pallas_call | solution.py:116
  23.6 1.8 %collective-permute-done.9.second_far_ref = bf16[256,128]{1,0:T(8,128)(2,1)S(1)} collective-permute-done((bf16[256,128]{1,0:T(8,128)(2,1)S(1)}, bf16[256,128]{1,0:T(8,128)(2,1)S(1)}, u32[]{:S(2)}, u32[]{:S(2)}) %collective-permute-start.9) | collective-permute-done | bytes 65568 | tf_op jit(solution)/shard_map/ppermute | solution.py:175
  25.3 1.7 %shard_map.73 = (bf16[2,2,64,128]{3,2,1,0:T(8,128)(2,1)S(1)}, bf16[2,2,64,128]{3,2,1,0:T(8,128)(2,1)S(1)}, bf16[2,64,128]{2,1,0:T(8,128)(2,1)S(1)}, bf16[2,2,64,...) custom-call(s32[8,128]{1,0:T(8,128)S(1)} %get-tuple-element.19.flip_ref, f32[512,256]{1,0:T(8,128)S(1)} %get-tuple-element.27.near_ref, ...), custom_call_target="tpu_custom_call" | custom-call | flops 1073741824 | bytes 3575808 | tf_op jit(solution)/shard_map/pallas_call | solution.py:116
  27.1 1.8 %collective-permute-start.11 = (bf16[2,2,64,128]{3,2,1,0:T(8,128)(2,1)S(1)}, bf16[2,2,64,128]{3,2,1,0:T(8,128)(2,1)S(1)}, u32[]{:S(2)}, u32[]{:S(2)}) collective-permute-start(bf16[2,2,64,128]{3,2,1,0:T(8,128)(2,1)S(1)} %get-tuple-element.33), channel_id=1, source_target_pairs={{0,24},{4,28},{8,16},{12,20},{16,8},{20,12},{24,0},{28,4},{1,25},{... | collective-permute-start | bytes 196616 | tf_op jit(solution)/shard_map/ppermute | solution.py:175
  29.0 1.2 %collective-permute-start.13 = (bf16[2,2,64,128]{3,2,1,0:T(8,128)(2,1)S(1)}, bf16[2,2,64,128]{3,2,1,0:T(8,128)(2,1)S(1)}, u32[]{:S(2)}, u32[]{:S(2)}) collective-permute-start(bf16[2,2,64,128]{3,2,1,0:T(8,128)(2,1)S(1)} %get-tuple-element.34), channel_id=1, source_target_pairs={{0,16},{4,20},{8,24},{12,28},{16,0},{20,4},{24,8},{28,12},{1,17},{... | collective-permute-start | bytes 196616 | tf_op jit(solution)/shard_map/ppermute | solution.py:175
  30.2 0.6 %collective-permute-start.15 = (bf16[2,2,64,128]{3,2,1,0:T(8,128)(2,1)S(1)}, bf16[2,2,64,128]{3,2,1,0:T(8,128)(2,1)S(1)}, u32[]{:S(2)}, u32[]{:S(2)}) collective-permute-start(bf16[2,2,64,128]{3,2,1,0:T(8,128)(2,1)S(1)} %pad_maximum_fusion.1), channel_id=1, source_target_pairs={{0,8},{4,12},{8,0},{12,4},{16,24},{20,28},{24,16},{28,20},{1,9},{5... | collective-permute-start | bytes 196616 | tf_op jit(solution)/shard_map/ppermute | solution.py:175
  30.8 1.9 %collective-permute-done.11.refs_2_ = bf16[2,2,64,128]{3,2,1,0:T(8,128)(2,1)S(1)} collective-permute-done((bf16[2,2,64,128]{3,2,1,0:T(8,128)(2,1)S(1)}, bf16[2,2,64,128]{3,2,1,0:T(8,128)(2,1)S(1)}, u32[]{:S(2)}, u32[]{:S(2)}) %collective-permute-start.11) | collective-permute-done | bytes 65568 | tf_op jit(solution)/shard_map/ppermute | solution.py:175
  32.6 1.3 %collective-permute-done.13.refs_4_ = bf16[2,2,64,128]{3,2,1,0:T(8,128)(2,1)S(1)} collective-permute-done((bf16[2,2,64,128]{3,2,1,0:T(8,128)(2,1)S(1)}, bf16[2,2,64,128]{3,2,1,0:T(8,128)(2,1)S(1)}, u32[]{:S(2)}, u32[]{:S(2)}) %collective-permute-start.13) | collective-permute-done | bytes 65568 | tf_op jit(solution)/shard_map/ppermute | solution.py:175
  34.0 0.5 %collective-permute-done.15.refs_6_ = bf16[2,2,64,128]{3,2,1,0:T(8,128)(2,1)S(1)} collective-permute-done((bf16[2,2,64,128]{3,2,1,0:T(8,128)(2,1)S(1)}, bf16[2,2,64,128]{3,2,1,0:T(8,128)(2,1)S(1)}, u32[]{:S(2)}, u32[]{:S(2)}) %collective-permute-start.15) | collective-permute-done | bytes 65568 | tf_op jit(solution)/shard_map/ppermute | solution.py:175
  34.5 0.7 %collective-permute-done.14.refs_5_ = bf16[2,2,64,128]{3,2,1,0:T(8,128)(2,1)S(1)} collective-permute-done((bf16[2,2,64,128]{3,2,1,0:T(8,128)(2,1)S(1)}, bf16[2,2,64,128]{3,2,1,0:T(8,128)(2,1)S(1)}, u32[]{:S(2)}, u32[]{:S(2)}) %collective-permute-start.14) | collective-permute-done | bytes 65568 | tf_op jit(solution)/shard_map/ppermute | solution.py:175
  35.2 0.8 %shard_map.74 = (bf16[2,64,512]{2,1,0:T(8,128)(2,1)}, bf16[2,64,512]{2,1,0:T(8,128)(2,1)}) custom-call(bf16[2,64,128]{2,1,0:T(8,128)(2,1)S(1)} %get-tuple-element.31.refs_0_, bf16[2,2,64,128]{3,2,1,0:T(8,128)(2,1)S(1)} %collective-permute-done.10.refs_1_, bf16[2,2,64,128]{3,2,1,0:T(8,128)(2,1)S(1)} %collective-permute-done.11.refs_2_, ...), custom_call_target="tpu_custom_call" | custom-call | bytes 688128 | tf_op jit(solution)/shard_map/pallas_call | solution.py:116
  (23 shorter events, 1.2 us)
Async XLA Ops:
  2.2 4.5 %collective-permute-start = (bf16[2,2,64,128]{3,2,1,0:T(8,128)(2,1)S(1)}, bf16[2,2,64,128]{3,2,1,0:T(8,128)(2,1)S(1)}, u32[]{:S(2)}, u32[]{:S(2)}) collective-permute-start(bf16[2,2,64,128]{3,2,1,0:T(8,128)(2,1)S(1)} %get-tuple-element.22), channel_id=1, source_target_pairs={{0,4},{4,0},{8,12},{12,8},{16,20},{20,16},{24,28},{28,24},{1,5},{5... | collective-permute-start | bytes 196616 | tf_op jit(solution)/shard_map/ppermute | solution.py:175
  2.7 6.2 %collective-permute-start.1 = (bf16[2,2,64,128]{3,2,1,0:T(8,128)(2,1)S(1)}, bf16[2,2,64,128]{3,2,1,0:T(8,128)(2,1)S(1)}, u32[]{:S(2)}, u32[]{:S(2)}) collective-permute-start(bf16[2,2,64,128]{3,2,1,0:T(8,128)(2,1)S(1)} %get-tuple-element.23), channel_id=1, source_target_pairs={{0,24},{4,28},{8,16},{12,20},{16,8},{20,12},{24,0},{28,4},{1,25},{... | collective-permute-start | bytes 196616 | tf_op jit(solution)/shard_map/ppermute | solution.py:175
  6.3 4.3 %collective-permute-start.3 = (bf16[2,2,64,128]{3,2,1,0:T(8,128)(2,1)S(1)}, bf16[2,2,64,128]{3,2,1,0:T(8,128)(2,1)S(1)}, u32[]{:S(2)}, u32[]{:S(2)}) collective-permute-start(bf16[2,2,64,128]{3,2,1,0:T(8,128)(2,1)S(1)} %get-tuple-element.24), channel_id=1, source_target_pairs={{0,16},{4,20},{8,24},{12,28},{16,0},{20,4},{24,8},{28,12},{1,17},{... | collective-permute-start | bytes 196616 | tf_op jit(solution)/shard_map/ppermute | solution.py:175
  6.8 4.3 %collective-permute-start.5 = (bf16[2,2,64,128]{3,2,1,0:T(8,128)(2,1)S(1)}, bf16[2,2,64,128]{3,2,1,0:T(8,128)(2,1)S(1)}, u32[]{:S(2)}, u32[]{:S(2)}) collective-permute-start(bf16[2,2,64,128]{3,2,1,0:T(8,128)(2,1)S(1)} %pad_maximum_fusion), channel_id=1, source_target_pairs={{0,8},{4,12},{8,0},{12,4},{16,24},{20,28},{24,16},{28,20},{1,9},{5... | collective-permute-start | bytes 196616 | tf_op jit(solution)/shard_map/ppermute | solution.py:175
  9.0 2.2 %collective-permute-start.2 = (bf16[2,2,64,128]{3,2,1,0:T(8,128)(2,1)S(1)}, bf16[2,2,64,128]{3,2,1,0:T(8,128)(2,1)S(1)}, u32[]{:S(2)}, u32[]{:S(2)}) collective-permute-start(bf16[2,2,64,128]{3,2,1,0:T(8,128)(2,1)S(1)} %collective-permute-done.1.refs_2_), channel_id=1, source_target_pairs={{0,4},{4,0},{8,12},{12,8},{16,20},{20,16},{24,28},{28,24},{1,5},{5... | collective-permute-start | bytes 196616 | tf_op jit(solution)/shard_map/ppermute | solution.py:175
  10.5 1.3 %collective-permute-start.4 = (bf16[2,2,64,128]{3,2,1,0:T(8,128)(2,1)S(1)}, bf16[2,2,64,128]{3,2,1,0:T(8,128)(2,1)S(1)}, u32[]{:S(2)}, u32[]{:S(2)}) collective-permute-start(bf16[2,2,64,128]{3,2,1,0:T(8,128)(2,1)S(1)} %collective-permute-done.3.refs_4_), channel_id=1, source_target_pairs={{0,4},{4,0},{8,12},{12,8},{16,20},{20,16},{24,28},{28,24},{1,5},{5... | collective-permute-start | bytes 196616 | tf_op jit(solution)/shard_map/ppermute | solution.py:175
  12.0 4.3 %collective-permute-start.6 = (bf16[256,128]{1,0:T(8,128)(2,1)S(1)}, bf16[256,128]{1,0:T(8,128)(2,1)S(1)}, u32[]{:S(2)}, u32[]{:S(2)}) collective-permute-start(bf16[256,128]{1,0:T(8,128)(2,1)S(1)} %get-tuple-element.29.own_ref), channel_id=1, source_target_pairs={{0,1},{1,0},{2,3},{3,2},{4,5},{5,4},{6,7},{7,6},{8,9},{9,8},{10,11... | collective-permute-start | bytes 196616 | tf_op jit(solution)/shard_map/ppermute | solution.py:175
  13.7 7.2 %collective-permute-start.8 = (bf16[256,128]{1,0:T(8,128)(2,1)S(1)}, bf16[256,128]{1,0:T(8,128)(2,1)S(1)}, u32[]{:S(2)}, u32[]{:S(2)}) collective-permute-start(bf16[256,128]{1,0:T(8,128)(2,1)S(1)} %get-tuple-element.30.own_ref), channel_id=1, source_target_pairs={{0,2},{1,3},{2,0},{3,1},{4,6},{5,7},{6,4},{7,5},{8,10},{9,11},{10,... | collective-permute-start | bytes 196616 | tf_op jit(solution)/shard_map/ppermute | solution.py:175
  16.4 7.1 %collective-permute-start.7 = (bf16[256,128]{1,0:T(8,128)(2,1)S(1)}, bf16[256,128]{1,0:T(8,128)(2,1)S(1)}, u32[]{:S(2)}, u32[]{:S(2)}) collective-permute-start(bf16[256,128]{1,0:T(8,128)(2,1)S(1)} %shard_map.71), channel_id=1, source_target_pairs={{0,2},{1,3},{2,0},{3,1},{4,6},{5,7},{6,4},{7,5},{8,10},{9,11},{10,... | collective-permute-start | bytes 196616 | tf_op jit(solution)/shard_map/ppermute | solution.py:175
  21.0 4.3 %collective-permute-start.9 = (bf16[256,128]{1,0:T(8,128)(2,1)S(1)}, bf16[256,128]{1,0:T(8,128)(2,1)S(1)}, u32[]{:S(2)}, u32[]{:S(2)}) collective-permute-start(bf16[256,128]{1,0:T(8,128)(2,1)S(1)} %shard_map.72), channel_id=1, source_target_pairs={{0,1},{1,0},{2,3},{3,2},{4,5},{5,4},{6,7},{7,6},{8,9},{9,8},{10,11... | collective-permute-start | bytes 196616 | tf_op jit(solution)/shard_map/ppermute | solution.py:175
  21.5 1.6 %copy-start = (bf16[4,512,512]{2,1,0:T(8,128)(2,1)S(1)}, bf16[4,512,512]{2,1,0:T(8,128)(2,1)}, u32[]{:S(2)}) copy-start(bf16[4,512,512]{2,1,0:T(8,128)(2,1)} %constant.2.clone.table_ref) | copy-start | bytes 6291460
  23.1 2.3 %copy-start.1 = (bf16[4,512,512]{2,1,0:T(8,128)(2,1)S(1)}, bf16[4,512,512]{2,1,0:T(8,128)(2,1)}, u32[]{:S(2)}) copy-start(bf16[4,512,512]{2,1,0:T(8,128)(2,1)} %constant.2.clone.table_ref) | copy-start | bytes 6291460
  27.1 3.1 %collective-permute-start.10 = (bf16[2,2,64,128]{3,2,1,0:T(8,128)(2,1)S(1)}, bf16[2,2,64,128]{3,2,1,0:T(8,128)(2,1)S(1)}, u32[]{:S(2)}, u32[]{:S(2)}) collective-permute-start(bf16[2,2,64,128]{3,2,1,0:T(8,128)(2,1)S(1)} %get-tuple-element.32), channel_id=1, source_target_pairs={{0,4},{4,0},{8,12},{12,8},{16,20},{20,16},{24,28},{28,24},{1,5},{5... | collective-permute-start | bytes 196616 | tf_op jit(solution)/shard_map/ppermute | solution.py:175
  27.1 5.5 %collective-permute-start.11 = (bf16[2,2,64,128]{3,2,1,0:T(8,128)(2,1)S(1)}, bf16[2,2,64,128]{3,2,1,0:T(8,128)(2,1)S(1)}, u32[]{:S(2)}, u32[]{:S(2)}) collective-permute-start(bf16[2,2,64,128]{3,2,1,0:T(8,128)(2,1)S(1)} %get-tuple-element.33), channel_id=1, source_target_pairs={{0,24},{4,28},{8,16},{12,20},{16,8},{20,12},{24,0},{28,4},{1,25},{... | collective-permute-start | bytes 196616 | tf_op jit(solution)/shard_map/ppermute | solution.py:175
  29.0 5.0 %collective-permute-start.13 = (bf16[2,2,64,128]{3,2,1,0:T(8,128)(2,1)S(1)}, bf16[2,2,64,128]{3,2,1,0:T(8,128)(2,1)S(1)}, u32[]{:S(2)}, u32[]{:S(2)}) collective-permute-start(bf16[2,2,64,128]{3,2,1,0:T(8,128)(2,1)S(1)} %get-tuple-element.34), channel_id=1, source_target_pairs={{0,16},{4,20},{8,24},{12,28},{16,0},{20,4},{24,8},{28,12},{1,17},{... | collective-permute-start | bytes 196616 | tf_op jit(solution)/shard_map/ppermute | solution.py:175
  30.2 4.3 %collective-permute-start.15 = (bf16[2,2,64,128]{3,2,1,0:T(8,128)(2,1)S(1)}, bf16[2,2,64,128]{3,2,1,0:T(8,128)(2,1)S(1)}, u32[]{:S(2)}, u32[]{:S(2)}) collective-permute-start(bf16[2,2,64,128]{3,2,1,0:T(8,128)(2,1)S(1)} %pad_maximum_fusion.1), channel_id=1, source_target_pairs={{0,8},{4,12},{8,0},{12,4},{16,24},{20,28},{24,16},{28,20},{1,9},{5... | collective-permute-start | bytes 196616 | tf_op jit(solution)/shard_map/ppermute | solution.py:175
  32.6 1.9 %collective-permute-start.12 = (bf16[2,2,64,128]{3,2,1,0:T(8,128)(2,1)S(1)}, bf16[2,2,64,128]{3,2,1,0:T(8,128)(2,1)S(1)}, u32[]{:S(2)}, u32[]{:S(2)}) collective-permute-start(bf16[2,2,64,128]{3,2,1,0:T(8,128)(2,1)S(1)} %collective-permute-done.11.refs_2_), channel_id=1, source_target_pairs={{0,4},{4,0},{8,12},{12,8},{16,20},{20,16},{24,28},{28,24},{1,5},{5... | collective-permute-start | bytes 196616 | tf_op jit(solution)/shard_map/ppermute | solution.py:175
  34.0 1.3 %collective-permute-start.14 = (bf16[2,2,64,128]{3,2,1,0:T(8,128)(2,1)S(1)}, bf16[2,2,64,128]{3,2,1,0:T(8,128)(2,1)S(1)}, u32[]{:S(2)}, u32[]{:S(2)}) collective-permute-start(bf16[2,2,64,128]{3,2,1,0:T(8,128)(2,1)S(1)} %collective-permute-done.13.refs_4_), channel_id=1, source_target_pairs={{0,4},{4,0},{8,12},{12,8},{16,20},{20,16},{24,28},{28,24},{1,5},{5... | collective-permute-start | bytes 196616 | tf_op jit(solution)/shard_map/ppermute | solution.py:175

commit v5 on v4

--- a/solution.py
+++ b/solution.py
@@ -107,19 +107,18 @@
         out_ref[:, part] = result[:, part * lanes : (part + 1) * lanes].reshape(blocks, energies, lanes)
 
 
-def call(kernel, out_shape, flops, *args, scratch=(), in_hbm=False):
+def call(kernel, out_shape, flops, *args, scratch=(), in_hbm=()):
     outs = out_shape if isinstance(out_shape, (list, tuple)) else [out_shape]
     moved = sum(math.prod(v.shape) * v.dtype.itemsize for v in [*args, *outs])
-    more = {"in_specs": [pl.BlockSpec(memory_space=pltpu.HBM)] * len(args)} if in_hbm else {}
-    if in_hbm:
-        args = [pltpu.with_memory_space_constraint(v, pltpu.HBM) for v in args]
+    spaces = [pltpu.HBM if i in in_hbm else pltpu.VMEM for i in range(len(args))]
+    args = [pltpu.with_memory_space_constraint(v, pltpu.HBM) if i in in_hbm else v for i, v in enumerate(args)]
     return pl.pallas_call(
         kernel,
         out_shape=out_shape,
+        in_specs=[pl.BlockSpec(memory_space=space) for space in spaces],
         scratch_shapes=list(scratch),
         compiler_params=pltpu.CompilerParams(vmem_limit_bytes=VMEM_BYTES),
         cost_estimate=pl.CostEstimate(flops=flops, bytes_accessed=moved, transcendentals=0),
-        **more,
     )(*args)
 
 
@@ -133,8 +132,8 @@
 
 
 def split_kernel(lists_ref, slots_ref, lesser_ref, greater_ref, *refs):
-    (diagonal_ref, beside_ref, keep_ref, give_ref, own_ref, picks_ref, flip_ref) = refs[:7]
-    held, lists, slots, sems, index_sems = refs[7:]
+    (diagonal_ref, keep_ref, give_ref, picks_ref, flip_ref) = refs[:5]
+    held, lists, slots, sems, index_sems = refs[5:]
     chip, core = place()
     index_copies = [
         pltpu.make_async_copy(lists_ref.at[0, 2 * chip + core], lists, index_sems.at[0]),
@@ -142,7 +141,7 @@
     ]
     for copy in index_copies:
         copy.start()
-    width = own_ref.shape[-1] // 2
+    width = keep_ref.shape[-1] // 2
     copies = [
         [
             pltpu.make_async_copy(ref.at[:, :, columns_of(chip ^ j, width)], held.at[j, i], sems.at[j, i])
@@ -162,33 +161,38 @@
         lesser, greater = held[j, 0], held[j, 1]
         zero = jnp.concatenate([lesser[..., :width], greater[..., :width]], axis=-1)
         one = jnp.concatenate([lesser[..., width:], greater[..., width:]], axis=-1)
-        if j >= 2:
-            out_ref = diagonal_ref if j == 3 else beside_ref
-            out_ref[0], out_ref[1] = zero, one
+        if j == 3:
+            diagonal_ref[0], diagonal_ref[1] = zero, one
         else:
-            keep = keep_ref if j == 1 else own_ref
-            keep[...] = jnp.where(core == 0, zero, one)
-            give_ref[1 - j] = jnp.where(core == 0, one, zero)
+            keep_ref[j] = jnp.where(core == 0, zero, one)
+            give_ref[j] = jnp.where(core == 0, one, zero)
 
 
 def swap(values, axis, bit):
     return lax.ppermute(values, axis, [(i, i ^ bit) for i in range(lax.axis_size(axis))])
 
 
-def over_energy(diagonal, beside, keep, give, own):
+def over_elem(values, bits):
+    groups = lax.axis_size("elem")
+    pairs = [(n * groups + i, n * groups + (i ^ bits[n % 2])) for n in range(lax.axis_size("energy")) for i in range(groups)]
+    return lax.ppermute(values, ("energy", "elem"), pairs)
+
+
+def over_energy(diagonal, keep, give):
     diagonal = swap(diagonal, "energy", 6)
-    beside = swap(beside, "energy", 4)
     got = swap(give, "energy", 1)
-    across = swap(jnp.stack([keep, got[0]]), "energy", 2)
-    return own, got, diagonal, swap(diagonal, "energy", 1), beside, swap(beside, "energy", 1), across
+    beside = swap(jnp.stack([keep[2], got[2]]), "energy", 4)
+    across = swap(jnp.stack([keep[1], got[1]]), "energy", 2)
+    diagonal, beside = lax.optimization_barrier((diagonal, beside))
+    return keep, got, diagonal, swap(diagonal, "energy", 1), beside, across
 
 
 def blocks_of(refs, core):
-    own_ref, got_ref, diagonal_ref, diagonal_other_ref, beside_ref, beside_other_ref, across_ref = refs
+    keep_ref, got_ref, diagonal_ref, diagonal_other_ref, beside_ref, across_ref = refs
     return [
-        (lambda: own_ref[...], lambda: got_ref[1]),
+        (lambda: keep_ref[0], lambda: got_ref[0]),
         (lambda: across_ref[0], lambda: across_ref[1]),
-        (lambda: beside_ref[core], lambda: beside_other_ref[core]),
+        (lambda: beside_ref[0], lambda: beside_ref[1]),
         (lambda: diagonal_ref[core], lambda: diagonal_other_ref[core]),
     ]
 
@@ -205,8 +209,8 @@
     return dot(values.astype(F32).astype(BF16), one_hot(index_row, values.shape[-1])).astype(jnp.int32)
 
 
-def relay_kernel(flip_ref, passed_ref, own_ref, out_ref):
-    out_ref[...] = jnp.where(flip_ref[0:1, :] == 3, passed_ref[...], own_ref[...])
+def relay_kernel(flip_ref, first_ref, own_ref, _, out_ref):
+    out_ref[...] = jnp.where(flip_ref[0:1, :] == 3, first_ref[...], own_ref[...])
 
 
 def index_tables(lists, slots, picks_ref, flip_ref):
@@ -234,64 +238,60 @@
 
 
 def gather_kernel(picks_ref, *refs):
-    in_refs, (signals_ref, first_ref, second_ref) = refs[:7], refs[7:]
+    in_refs, (signals_ref, sent_ref) = refs[:6], refs[6:]
     chip, core = place()
-    energies, lanes = in_refs[0].shape[1:]
+    energies, lanes = in_refs[0].shape[2:]
     for j, pair in enumerate(blocks_of(in_refs, core)):
         for which, block in enumerate(pair):
             values = block()
             rows = energies_of(2 * (chip ^ j) + (core if which == 0 else 1 - core), energies)
             for part in range(2):
                 signals_ref[rows, part * lanes : (part + 1) * lanes] = values[part]
-    half = first_ref.shape[0]
-    for i, ref in enumerate((first_ref, second_ref)):
-        rows = slice(i * half, (i + 1) * half)
-        ref[...] = (dot(signals_ref[rows, :lanes], picks_ref[3]) + dot(signals_ref[rows, lanes:], picks_ref[4])).astype(BF16)
-
-
-def own_kernel(signals_ref, picks_ref, table_ref, near_ref, partner_ref):
+    sent_ref[...] = (dot(signals_ref[:, :lanes], picks_ref[3]) + dot(signals_ref[:, lanes:], picks_ref[4])).astype(BF16)
+
+
+def own_kernel(signals_ref, picks_ref, table_ref, near_ref, partner_ref, held_ref, sems):
     lanes = picks_ref.shape[-1]
+    steps = sems.shape[0] // 4
+    height = table_ref.shape[1] // steps
+    copies = []
+    for i in range(4 * steps):
+        rows = pl.ds(i % steps * height, height)
+        copies.append(pltpu.make_async_copy(table_ref.at[i // steps, rows], held_ref.at[i // steps, rows], sems.at[i]))
+    for copy in copies:
+        copy.start()
     for part in range(2):
         cols = slice(part * lanes, (part + 1) * lanes)
         partner_ref[:, cols] = dot(signals_ref[:, cols], picks_ref[0]).astype(BF16)
-    near_ref[...] = forward_sums(table_ref, signals_ref[...])
-
-
-def exchange_kernel(flip_ref, near_ref, partner_ref, picks_ref, first_ref, first_far_ref, second_ref, second_far_ref, table_ref, *refs):
-    (diagonal_ref, beside_ref, keep_ref, give_ref, own_ref), (held,) = refs[:5], refs[5:]
+    for copy in copies:
+        copy.wait()
+    near_ref[...] = forward_sums(held_ref, signals_ref[...])
+
+
+def exchange_kernel(flip_ref, near_ref, partner_ref, picks_ref, first_ref, second_ref, table_ref, *refs):
+    (diagonal_ref, keep_ref, give_ref), (held,) = refs[:3], refs[3:]
     chip, core = place()
-    energies, lanes = own_ref.shape[1:]
-    flip = flip_ref[0:1, :]
-    far = jnp.concatenate(
-        [
-            jnp.where(flip == 1, first_ref[...], first_far_ref[...]),
-            jnp.where(flip == 2, second_ref[...], second_far_ref[...]),
-        ],
-        axis=0,
-    )
+    energies, lanes = keep_ref.shape[2:]
+    far = jnp.where(flip_ref[0:1, :] == 1 + core, first_ref[...], second_ref[...])
     partner = [
         (partner_ref[:, part * lanes : (part + 1) * lanes].astype(F32) + dot(far, picks_ref[1 + part])).astype(BF16)
         for part in range(2)
     ]
     held[...] = correlate(near_ref[...], forward_sums(table_ref, jnp.concatenate(partner, axis=-1)), table_ref)
 
-    def block(device):
-        rows = energies_of(device, energies)
+    def block(j, core):
+        rows = energies_of(2 * (chip ^ j) + core, energies)
         return [held[rows, part * lanes : (part + 1) * lanes] for part in range(2)]
 
-    for j, ref in ((3, diagonal_ref), (2, beside_ref)):
-        for which in range(2):
-            for part, values in enumerate(block(2 * (chip ^ j) + which)):
-                ref[which, part] = values
-    for j, ref in ((1, keep_ref), (0, own_ref)):
-        for part, values in enumerate(block(2 * (chip ^ j) + core)):
-            ref[part] = values
-        for part, values in enumerate(block(2 * (chip ^ j) + 1 - core)):
-            give_ref[1 - j, part] = values
+    for which in range(2):
+        diagonal_ref[which, 0], diagonal_ref[which, 1] = block(3, which)
+    for j in range(3):
+        keep_ref[j, 0], keep_ref[j, 1] = block(j, core)
+        give_ref[j, 0], give_ref[j, 1] = block(j, 1 - core)
 
 
 def join_kernel(*refs):
-    in_refs, (lesser_ref, greater_ref) = refs[:7], refs[7:]
+    in_refs, (lesser_ref, greater_ref) = refs[:6], refs[6:]
     chip, core = place()
     width = in_refs[0].shape[-1] // 2
     for j, (mine, other) in enumerate(blocks_of(in_refs, core)):
@@ -308,10 +308,10 @@
     cap = send_rows.shape[-1]
     lanes = 4 * cap
     length = 8 * energies
-    block = jax.ShapeDtypeStruct((2, energies, lanes), BF16)
     pair = jax.ShapeDtypeStruct((2, 2, energies, lanes), BF16)
-    leaving = [pair, pair, block, pair, block]
-    half = jax.ShapeDtypeStruct((length // 2, lanes), BF16)
+    three = jax.ShapeDtypeStruct((3, 2, energies, lanes), BF16)
+    leaving = [pair, three, three]
+    column = jax.ShapeDtypeStruct((length, lanes), BF16)
     whole = jax.ShapeDtypeStruct((length, 2 * lanes), BF16)
     slots = partner_slot.reshape(4, lanes)
     table = jnp.asarray(fourier_tables(length))
@@ -325,15 +325,21 @@
     ]
     tables = [jax.ShapeDtypeStruct((5, lanes, lanes), BF16), jax.ShapeDtypeStruct((8, lanes), jnp.int32)]
     *packed, picks, flip = call(
-        split_kernel, leaving + tables, 2**24, send_rows, slots, g_lesser, g_greater, scratch=scratch, in_hbm=True
+        split_kernel, leaving + tables, 2**24, send_rows, slots, g_lesser, g_greater, scratch=scratch, in_hbm=(0, 1, 2, 3)
     )
-    arrived = over_energy(*packed)
-    signals, first, second = call(gather_kernel, [whole, half, half], 2**26, picks, *arrived)
-    second_one, first_one = swap(second, "elem", 2), swap(first, "elem", 1)
-    sums = jax.ShapeDtypeStruct((length, 2 * lanes), F32)
-    near, partner = call(own_kernel, [sums, whole], 2**29, signals, picks, table)
-    first_two = swap(call(relay_kernel, half, 0, flip, first_one, first), "elem", 2)
-    second_two = swap(call(relay_kernel, half, 0, flip, second_one, second), "elem", 1)
+    signals, sent = call(gather_kernel, [whole, column], 2**26, picks, *over_energy(*packed))
+    first = over_elem(sent, (1, 2))
+    near, partner, held = call(
+        own_kernel,
+        [jax.ShapeDtypeStruct(whole.shape, F32), whole, jax.ShapeDtypeStruct(table.shape, BF16)],
+        2**29,
+        signals,
+        picks,
+        table,
+        scratch=[pltpu.SemaphoreType.DMA((16,))],
+        in_hbm=(2,),
+    )
+    second = over_elem(call(relay_kernel, column, 0, flip, first, sent, partner), (2, 1))
     results = call(
         exchange_kernel,
         leaving,
@@ -342,12 +348,10 @@
         near,
         partner,
         picks,
-        first_one,
-        first_two,
-        second_one,
-        second_two,
-        table,
-        scratch=[pltpu.VMEM((length, 2 * lanes), BF16)],
+        first,
+        second,
+        held,
+        scratch=[pltpu.VMEM(whole.shape, BF16)],
     )
     out = jax.ShapeDtypeStruct((2, energies, group_rows), BF16)
     return tuple(call(join_kernel, [out, out], 0, *over_energy(*results)))

time: 36.3 us -> 37.2 us (1.025)
  waiting for transfers between devices: 12.3 us -> 18 us
  starting transfers between devices: 16.5 us -> 11.5 us
  Pallas kernels: 4.93 us -> 6.63 us
  local copies, waits for them, and re-layouts: 1.6 us -> 0.02 us
    ppermute x16 -> x10, starting transfers between devices: 16.5 us -> 8.08 us  [swap(): lax.ppermute(values, axis, [(i, i ^ bit) for i in range(lax.axis_size(axi...]
    ppermute x0 -> x2, waiting for transfers between devices: none -> 7.19 us  [over_elem(): return lax.ppermute(values, ('energy', 'elem'), pairs)]
    ppermute x0 -> x2, starting transfers between devices: none -> 3.45 us  [over_elem(): return lax.ppermute(values, ('energy', 'elem'), pairs)]
    pallas_call x7 -> x6, Pallas kernels: 4.93 us -> 6.63 us  [call(): pl.pallas_call(kernel, out_shape=out_shape, in_specs=[pl.BlockSpec(memory...]
    unnamed x4 -> x0, local copies, waits for them, and re-layouts: 1.59 us -> none
    ppermute x16 -> x10, waiting for transfers between devices: 12.3 us -> 10.9 us  [swap(): lax.ppermute(values, axis, [(i, i ^ bit) for i in range(lax.axis_size(axi...]
  transfers between devices with their start and end apart: 16 -> 12, of which waited for: 11 -> 11; matrix products, arithmetic and copies ran while one was open for 0% -> 0% of each run, Pallas kernels for 1% -> 6%
where the time goes in v5:
time: 37.2 us; the launch traced here: 36.9 us
  waiting for transfers between devices  18 us (48%)
  starting transfers between devices  11.5 us (31%)
  Pallas kernels  6.63 us (18%)
  between operations  0.7 us (2%)
    ppermute x10, waiting for transfers between devices, swap(): lax.ppermute(values, axis, [(i, i ^ bit) for i in range(lax.axis_size(axi...  10.9 us
    ppermute x10, starting transfers between devices, swap(): lax.ppermute(values, axis, [(i, i ^ bit) for i in range(lax.axis_size(axi...  8.08 us
    ppermute x2, waiting for transfers between devices, over_elem(): return lax.ppermute(values, ('energy', 'elem'), pairs)  7.19 us
    pallas_call x6, Pallas kernels, call(): pl.pallas_call(kernel, out_shape=out_shape, in_specs=[pl.BlockSpec(memory...  6.63 us
    ppermute x2, starting transfers between devices, over_elem(): return lax.ppermute(values, ('energy', 'elem'), pairs)  3.45 us
  transfers between devices with their start and end apart: 12, of which 11 were waited for; matrix products, arithmetic and copies ran while one was open for 0% of the time, Pallas kernels for 6%

profile of v5, /device:TPU:0, one launch (start us, length us, event | category | flops | bytes accessed | tf_op | source)
XLA Modules:
  0.0 36.9 jit_solution(6723122152794326185)
XLA Ops:
  0.6 1.6 %shard_map.68 = (bf16[2,2,64,128]{3,2,1,0:T(8,128)(2,1)S(1)}, bf16[3,2,64,128]{3,2,1,0:T(8,128)(2,1)S(1)}, bf16[3,2,64,128]{3,2,1,0:T(8,128)(2,1)S(1)}, bf16[5,128,128]{2,1,0:T(8,128)(2,1)S(1)}, s32[8,128]{1,0:T(8,128)S(1)}) custom-call(s32[1,8,4,32]{3,2,1,0:T(4,128)} %lists_ref.1, s32[4,128]{1,0:T(4,128)} %bitcast.1, bf16[2,64,512]{2,1,0:T(8,128)(2,1)} %lesser_ref.1, ...), custom_call_target="tpu_custom_call" | custom-call | flops 16777216 | bytes 698368 | tf_op jit(solution)/shard_map/pallas_call | solution.py:115
  2.2 4.0 %collective-permute-start.1 = (bf16[2,2,64,128]{3,2,1,0:T(8,128)(2,1)S(1)}, bf16[2,2,64,128]{3,2,1,0:T(8,128)(2,1)S(1)}, u32[]{:S(2)}, u32[]{:S(2)}) collective-permute-start(bf16[2,2,64,128]{3,2,1,0:T(8,128)(2,1)S(1)} %get-tuple-element.23), channel_id=1, source_target_pairs={{0,24},{4,28},{8,16},{12,20},{16,8},{20,12},{24,0},{28,4},{1,25},{... | collective-permute-start | bytes 196616 | tf_op jit(solution)/shard_map/ppermute | solution.py:172
  6.2 1.3 %collective-permute-done.refs_1_ = bf16[3,2,64,128]{3,2,1,0:T(8,128)(2,1)S(1)} collective-permute-done((bf16[3,2,64,128]{3,2,1,0:T(8,128)(2,1)S(1)}, bf16[3,2,64,128]{3,2,1,0:T(8,128)(2,1)S(1)}, u32[]{:S(2)}, u32[]{:S(2)}) %collective-permute-start) | collective-permute-done | bytes 98336 | tf_op jit(solution)/shard_map/ppermute | solution.py:172
  7.5 0.6 %collective-permute-start.2 = (bf16[2,2,64,128]{3,2,1,0:T(8,128)(2,1)S(1)}, bf16[2,2,64,128]{3,2,1,0:T(8,128)(2,1)S(1)}, u32[]{:S(2)}, u32[]{:S(2)}) collective-permute-start(bf16[2,2,64,128]{3,2,1,0:T(8,128)(2,1)S(1)} %pad_maximum_fusion), channel_id=1, source_target_pairs={{0,16},{4,20},{8,24},{12,28},{16,0},{20,4},{24,8},{28,12},{1,17},{... | collective-permute-start | bytes 196616 | tf_op jit(solution)/shard_map/ppermute | solution.py:172
  8.1 0.2 collective-permute-start.4
  8.3 0.1 collective-permute-done.1.refs_2_
  8.4 3.4 %collective-permute-done.2.refs_4_ = bf16[2,2,64,128]{3,2,1,0:T(8,128)(2,1)S(1)} collective-permute-done((bf16[2,2,64,128]{3,2,1,0:T(8,128)(2,1)S(1)}, bf16[2,2,64,128]{3,2,1,0:T(8,128)(2,1)S(1)}, u32[]{:S(2)}, u32[]{:S(2)}) %collective-permute-start.2) | collective-permute-done | bytes 65568 | tf_op jit(solution)/shard_map/ppermute | solution.py:172
  11.8 0.6 %collective-permute-done.4.refs_5_ = bf16[2,2,64,128]{3,2,1,0:T(8,128)(2,1)S(1)} collective-permute-done((bf16[2,2,64,128]{3,2,1,0:T(8,128)(2,1)S(1)}, bf16[2,2,64,128]{3,2,1,0:T(8,128)(2,1)S(1)}, u32[]{:S(2)}, u32[]{:S(2)}) %collective-permute-start.4) | collective-permute-done | bytes 65568 | tf_op jit(solution)/shard_map/ppermute | solution.py:172
  12.4 0.7 %collective-permute-done.3.refs_3_ = bf16[2,2,64,128]{3,2,1,0:T(8,128)(2,1)S(1)} collective-permute-done((bf16[2,2,64,128]{3,2,1,0:T(8,128)(2,1)S(1)}, bf16[2,2,64,128]{3,2,1,0:T(8,128)(2,1)S(1)}, u32[]{:S(2)}, u32[]{:S(2)}) %collective-permute-start.3) | collective-permute-done | bytes 65568 | tf_op jit(solution)/shard_map/ppermute | solution.py:172
  13.1 0.3 shard_map.69
  13.4 1.6 %collective-permute-start.5 = (bf16[512,128]{1,0:T(8,128)(2,1)S(1)}, bf16[512,128]{1,0:T(8,128)(2,1)S(1)}, u32[]{:S(2)}, u32[]{:S(2)}) collective-permute-start(bf16[512,128]{1,0:T(8,128)(2,1)S(1)} %get-tuple-element.29.own_ref), channel_id=1, source_target_pairs={{0,1},{1,0},{2,3},{3,2},{4,6},{5,7},{6,4},{7,5},{8,9},{9,8},{10,11... | collective-permute-start | bytes 393224 | tf_op jit(solution)/shard_map/ppermute | solution.py:178
  15.0 2.2 %shard_map.70 = (f32[512,256]{1,0:T(8,128)S(1)}, bf16[512,256]{1,0:T(8,128)(2,1)S(1)}, bf16[4,512,512]{2,1,0:T(8,128)(2,1)S(1)}) custom-call(bf16[512,256]{1,0:T(8,128)(2,1)S(1)} %get-tuple-element.26.signals_ref, bf16[5,128,128]{2,1,0:T(8,128)(2,1)S(1)} %get-tuple-element.20.picks_ref, bf16[4,512,512]{2,1,0:T(8,128)(2,1)} %constant.2.clone.table_ref), custom_call_target="tpu_custom_call" | custom-call | flops 536870912 | bytes 5406720 | tf_op jit(solution)/shard_map/pallas_call | solution.py:115
  17.2 2.5 %collective-permute-done.5.first_ref = bf16[512,128]{1,0:T(8,128)(2,1)S(1)} collective-permute-done((bf16[512,128]{1,0:T(8,128)(2,1)S(1)}, bf16[512,128]{1,0:T(8,128)(2,1)S(1)}, u32[]{:S(2)}, u32[]{:S(2)}) %collective-permute-start.5) | collective-permute-done | bytes 131104 | tf_op jit(solution)/shard_map/ppermute | solution.py:178
  19.8 1.8 %collective-permute-start.6 = (bf16[512,128]{1,0:T(8,128)(2,1)S(1)}, bf16[512,128]{1,0:T(8,128)(2,1)S(1)}, u32[]{:S(2)}, u32[]{:S(2)}) collective-permute-start(bf16[512,128]{1,0:T(8,128)(2,1)S(1)} %shard_map.71), channel_id=1, source_target_pairs={{0,2},{1,3},{2,0},{3,1},{4,5},{5,4},{6,7},{7,6},{8,10},{9,11},{10,... | collective-permute-start | bytes 393224 | tf_op jit(solution)/shard_map/ppermute | solution.py:178
  21.6 4.7 %collective-permute-done.6.second_ref = bf16[512,128]{1,0:T(8,128)(2,1)S(1)} collective-permute-done((bf16[512,128]{1,0:T(8,128)(2,1)S(1)}, bf16[512,128]{1,0:T(8,128)(2,1)S(1)}, u32[]{:S(2)}, u32[]{:S(2)}) %collective-permute-start.6) | collective-permute-done | bytes 131104 | tf_op jit(solution)/shard_map/ppermute | solution.py:178
  26.2 1.7 %shard_map.72 = (bf16[2,2,64,128]{3,2,1,0:T(8,128)(2,1)S(1)}, bf16[3,2,64,128]{3,2,1,0:T(8,128)(2,1)S(1)}, bf16[3,2,64,128]{3,2,1,0:T(8,128)(2,1)S(1)}) custom-call(s32[8,128]{1,0:T(8,128)S(1)} %get-tuple-element.19.flip_ref, f32[512,256]{1,0:T(8,128)S(1)} %get-tuple-element.27.near_ref, bf16[512,256]{1,0:T(8,128)(2,1)S(1)} %get-tuple-element.28._.partner_ref, ...), custom_call_target="tpu_custom_call" | custom-call | flops 1073741824 | bytes 3575808 | tf_op jit(solution)/shard_map/pallas_call | solution.py:115
  28.0 0.8 %collective-permute-start.8 = (bf16[2,2,64,128]{3,2,1,0:T(8,128)(2,1)S(1)}, bf16[2,2,64,128]{3,2,1,0:T(8,128)(2,1)S(1)}, u32[]{:S(2)}, u32[]{:S(2)}) collective-permute-start(bf16[2,2,64,128]{3,2,1,0:T(8,128)(2,1)S(1)} %get-tuple-element.33), channel_id=1, source_target_pairs={{0,24},{4,28},{8,16},{12,20},{16,8},{20,12},{24,0},{28,4},{1,25},{... | collective-permute-start | bytes 196616 | tf_op jit(solution)/shard_map/ppermute | solution.py:172
  28.9 0.5 %collective-permute-done.7.refs_1_ = bf16[3,2,64,128]{3,2,1,0:T(8,128)(2,1)S(1)} collective-permute-done((bf16[3,2,64,128]{3,2,1,0:T(8,128)(2,1)S(1)}, bf16[3,2,64,128]{3,2,1,0:T(8,128)(2,1)S(1)}, u32[]{:S(2)}, u32[]{:S(2)}) %collective-permute-start.7) | collective-permute-done | bytes 98336 | tf_op jit(solution)/shard_map/ppermute | solution.py:172
  29.3 0.8 %collective-permute-start.9 = (bf16[2,2,64,128]{3,2,1,0:T(8,128)(2,1)S(1)}, bf16[2,2,64,128]{3,2,1,0:T(8,128)(2,1)S(1)}, u32[]{:S(2)}, u32[]{:S(2)}) collective-permute-start(bf16[2,2,64,128]{3,2,1,0:T(8,128)(2,1)S(1)} %pad_maximum_fusion.2), channel_id=1, source_target_pairs={{0,16},{4,20},{8,24},{12,28},{16,0},{20,4},{24,8},{28,12},{1,17},{... | collective-permute-start | bytes 196616 | tf_op jit(solution)/shard_map/ppermute | solution.py:172
  30.2 1.6 %collective-permute-start.11 = (bf16[2,2,64,128]{3,2,1,0:T(8,128)(2,1)S(1)}, bf16[2,2,64,128]{3,2,1,0:T(8,128)(2,1)S(1)}, u32[]{:S(2)}, u32[]{:S(2)}) collective-permute-start(bf16[2,2,64,128]{3,2,1,0:T(8,128)(2,1)S(1)} %pad_maximum_fusion.3), channel_id=1, source_target_pairs={{0,8},{4,12},{8,0},{12,4},{16,24},{20,28},{24,16},{28,20},{1,9},{5... | collective-permute-start | bytes 196616 | tf_op jit(solution)/shard_map/ppermute | solution.py:172
  31.8 1.8 %collective-permute-done.8.refs_2_ = bf16[2,2,64,128]{3,2,1,0:T(8,128)(2,1)S(1)} collective-permute-done((bf16[2,2,64,128]{3,2,1,0:T(8,128)(2,1)S(1)}, bf16[2,2,64,128]{3,2,1,0:T(8,128)(2,1)S(1)}, u32[]{:S(2)}, u32[]{:S(2)}) %collective-permute-start.8) | collective-permute-done | bytes 65568 | tf_op jit(solution)/shard_map/ppermute | solution.py:172
  33.6 1.3 %collective-permute-done.9.refs_4_ = bf16[2,2,64,128]{3,2,1,0:T(8,128)(2,1)S(1)} collective-permute-done((bf16[2,2,64,128]{3,2,1,0:T(8,128)(2,1)S(1)}, bf16[2,2,64,128]{3,2,1,0:T(8,128)(2,1)S(1)}, u32[]{:S(2)}, u32[]{:S(2)}) %collective-permute-start.9) | collective-permute-done | bytes 65568 | tf_op jit(solution)/shard_map/ppermute | solution.py:172
  34.9 1.2 %collective-permute-done.10.refs_3_ = bf16[2,2,64,128]{3,2,1,0:T(8,128)(2,1)S(1)} collective-permute-done((bf16[2,2,64,128]{3,2,1,0:T(8,128)(2,1)S(1)}, bf16[2,2,64,128]{3,2,1,0:T(8,128)(2,1)S(1)}, u32[]{:S(2)}, u32[]{:S(2)}) %collective-permute-start.10) | collective-permute-done | bytes 65568 | tf_op jit(solution)/shard_map/ppermute | solution.py:172
  36.1 0.8 %shard_map.73 = (bf16[2,64,512]{2,1,0:T(8,128)(2,1)}, bf16[2,64,512]{2,1,0:T(8,128)(2,1)}) custom-call(bf16[3,2,64,128]{3,2,1,0:T(8,128)(2,1)S(1)} %get-tuple-element.31.refs_0_, bf16[3,2,64,128]{3,2,1,0:T(8,128)(2,1)S(1)} %collective-permute-done.7.refs_1_, bf16[2,2,64,128]{3,2,1,0:T(8,128)(2,1)S(1)} %collective-permute-done.8.refs_2_, ...), custom_call_target="tpu_custom_call" | custom-call | bytes 720896 | tf_op jit(solution)/shard_map/pallas_call | solution.py:115
  (14 shorter events, 0.2 us)
Async XLA Ops:
  2.2 6.2 %collective-permute-start.1 = (bf16[2,2,64,128]{3,2,1,0:T(8,128)(2,1)S(1)}, bf16[2,2,64,128]{3,2,1,0:T(8,128)(2,1)S(1)}, u32[]{:S(2)}, u32[]{:S(2)}) collective-permute-start(bf16[2,2,64,128]{3,2,1,0:T(8,128)(2,1)S(1)} %get-tuple-element.23), channel_id=1, source_target_pairs={{0,24},{4,28},{8,16},{12,20},{16,8},{20,12},{24,0},{28,4},{1,25},{... | collective-permute-start | bytes 196616 | tf_op jit(solution)/shard_map/ppermute | solution.py:172
  6.2 1.3 %collective-permute-start = (bf16[3,2,64,128]{3,2,1,0:T(8,128)(2,1)S(1)}, bf16[3,2,64,128]{3,2,1,0:T(8,128)(2,1)S(1)}, u32[]{:S(2)}, u32[]{:S(2)}) collective-permute-start(bf16[3,2,64,128]{3,2,1,0:T(8,128)(2,1)S(1)} %get-tuple-element.22), channel_id=1, source_target_pairs={{0,4},{4,0},{8,12},{12,8},{16,20},{20,16},{24,28},{28,24},{1,5},{5... | collective-permute-start | bytes 294920 | tf_op jit(solution)/shard_map/ppermute | solution.py:172
  7.5 4.3 %collective-permute-start.2 = (bf16[2,2,64,128]{3,2,1,0:T(8,128)(2,1)S(1)}, bf16[2,2,64,128]{3,2,1,0:T(8,128)(2,1)S(1)}, u32[]{:S(2)}, u32[]{:S(2)}) collective-permute-start(bf16[2,2,64,128]{3,2,1,0:T(8,128)(2,1)S(1)} %pad_maximum_fusion), channel_id=1, source_target_pairs={{0,16},{4,20},{8,24},{12,28},{16,0},{20,4},{24,8},{28,12},{1,17},{... | collective-permute-start | bytes 196616 | tf_op jit(solution)/shard_map/ppermute | solution.py:172
  8.1 4.3 %collective-permute-start.4 = (bf16[2,2,64,128]{3,2,1,0:T(8,128)(2,1)S(1)}, bf16[2,2,64,128]{3,2,1,0:T(8,128)(2,1)S(1)}, u32[]{:S(2)}, u32[]{:S(2)}) collective-permute-start(bf16[2,2,64,128]{3,2,1,0:T(8,128)(2,1)S(1)} %pad_maximum_fusion.1), channel_id=1, source_target_pairs={{0,8},{4,12},{8,0},{12,4},{16,24},{20,28},{24,16},{28,20},{1,9},{5... | collective-permute-start | bytes 196616 | tf_op jit(solution)/shard_map/ppermute | solution.py:172
  11.8 1.3 %collective-permute-start.3 = (bf16[2,2,64,128]{3,2,1,0:T(8,128)(2,1)S(1)}, bf16[2,2,64,128]{3,2,1,0:T(8,128)(2,1)S(1)}, u32[]{:S(2)}, u32[]{:S(2)}) collective-permute-start(bf16[2,2,64,128]{3,2,1,0:T(8,128)(2,1)S(1)} %collective-permute-done.1.refs_2_), channel_id=1, source_target_pairs={{0,4},{4,0},{8,12},{12,8},{16,20},{20,16},{24,28},{28,24},{1,5},{5... | collective-permute-start | bytes 196616 | tf_op jit(solution)/shard_map/ppermute | solution.py:172
  13.4 6.4 %collective-permute-start.5 = (bf16[512,128]{1,0:T(8,128)(2,1)S(1)}, bf16[512,128]{1,0:T(8,128)(2,1)S(1)}, u32[]{:S(2)}, u32[]{:S(2)}) collective-permute-start(bf16[512,128]{1,0:T(8,128)(2,1)S(1)} %get-tuple-element.29.own_ref), channel_id=1, source_target_pairs={{0,1},{1,0},{2,3},{3,2},{4,6},{5,7},{6,4},{7,5},{8,9},{9,8},{10,11... | collective-permute-start | bytes 393224 | tf_op jit(solution)/shard_map/ppermute | solution.py:178
  19.8 6.5 %collective-permute-start.6 = (bf16[512,128]{1,0:T(8,128)(2,1)S(1)}, bf16[512,128]{1,0:T(8,128)(2,1)S(1)}, u32[]{:S(2)}, u32[]{:S(2)}) collective-permute-start(bf16[512,128]{1,0:T(8,128)(2,1)S(1)} %shard_map.71), channel_id=1, source_target_pairs={{0,2},{1,3},{2,0},{3,1},{4,5},{5,4},{6,7},{7,6},{8,10},{9,11},{10,... | collective-permute-start | bytes 393224 | tf_op jit(solution)/shard_map/ppermute | solution.py:178
  28.0 1.4 %collective-permute-start.7 = (bf16[3,2,64,128]{3,2,1,0:T(8,128)(2,1)S(1)}, bf16[3,2,64,128]{3,2,1,0:T(8,128)(2,1)S(1)}, u32[]{:S(2)}, u32[]{:S(2)}) collective-permute-start(bf16[3,2,64,128]{3,2,1,0:T(8,128)(2,1)S(1)} %get-tuple-element.32), channel_id=1, source_target_pairs={{0,4},{4,0},{8,12},{12,8},{16,20},{20,16},{24,28},{28,24},{1,5},{5... | collective-permute-start | bytes 294920 | tf_op jit(solution)/shard_map/ppermute | solution.py:172
  28.0 5.5 %collective-permute-start.8 = (bf16[2,2,64,128]{3,2,1,0:T(8,128)(2,1)S(1)}, bf16[2,2,64,128]{3,2,1,0:T(8,128)(2,1)S(1)}, u32[]{:S(2)}, u32[]{:S(2)}) collective-permute-start(bf16[2,2,64,128]{3,2,1,0:T(8,128)(2,1)S(1)} %get-tuple-element.33), channel_id=1, source_target_pairs={{0,24},{4,28},{8,16},{12,20},{16,8},{20,12},{24,0},{28,4},{1,25},{... | collective-permute-start | bytes 196616 | tf_op jit(solution)/shard_map/ppermute | solution.py:172
  29.3 5.5 %collective-permute-start.9 = (bf16[2,2,64,128]{3,2,1,0:T(8,128)(2,1)S(1)}, bf16[2,2,64,128]{3,2,1,0:T(8,128)(2,1)S(1)}, u32[]{:S(2)}, u32[]{:S(2)}) collective-permute-start(bf16[2,2,64,128]{3,2,1,0:T(8,128)(2,1)S(1)} %pad_maximum_fusion.2), channel_id=1, source_target_pairs={{0,16},{4,20},{8,24},{12,28},{16,0},{20,4},{24,8},{28,12},{1,17},{... | collective-permute-start | bytes 196616 | tf_op jit(solution)/shard_map/ppermute | solution.py:172
  30.2 4.7 %collective-permute-start.11 = (bf16[2,2,64,128]{3,2,1,0:T(8,128)(2,1)S(1)}, bf16[2,2,64,128]{3,2,1,0:T(8,128)(2,1)S(1)}, u32[]{:S(2)}, u32[]{:S(2)}) collective-permute-start(bf16[2,2,64,128]{3,2,1,0:T(8,128)(2,1)S(1)} %pad_maximum_fusion.3), channel_id=1, source_target_pairs={{0,8},{4,12},{8,0},{12,4},{16,24},{20,28},{24,16},{28,20},{1,9},{5... | collective-permute-start | bytes 196616 | tf_op jit(solution)/shard_map/ppermute | solution.py:172
  34.9 1.3 %collective-permute-start.10 = (bf16[2,2,64,128]{3,2,1,0:T(8,128)(2,1)S(1)}, bf16[2,2,64,128]{3,2,1,0:T(8,128)(2,1)S(1)}, u32[]{:S(2)}, u32[]{:S(2)}) collective-permute-start(bf16[2,2,64,128]{3,2,1,0:T(8,128)(2,1)S(1)} %collective-permute-done.8.refs_2_), channel_id=1, source_target_pairs={{0,4},{4,0},{8,12},{12,8},{16,20},{20,16},{24,28},{28,24},{1,5},{5... | collective-permute-start | bytes 196616 | tf_op jit(solution)/shard_map/ppermute | solution.py:172
